TPU v7x, 32 devices: a whole 2x2x4 slice. The times are simulated.
32 devices in a mesh: prow: 4 (over y, x), pcol: 8 (over z, core).
Axes of the slice: x: 2, y: 2, z: 4, core: 2. Of those that a mesh axis runs over, the one named last changes fastest.
Arguments:
- matrix: float32 [2048, 1024], P('prow', 'pcol'), may hold values from -6 to 6
- panel: float32 [2048, 1024], P(('prow', 'pcol')), as said below
- pivots: int32 [1024], replicated, may hold values from 0 to 2047, as said below
Outputs:
- trailing: float32 [2048, 1024], P('prow', 'pcol')
Inputs may be any that keep to these rules, and one draw needn't show every extreme that they name: pivots[i] is either i itself or a row at or beyond 1024; the rows at or beyond 1024 that are named are all different; at most 264 of them lie in the rows of one index of prow, and some index of prow holds exactly 264. `panel`: the top 1024 rows are unit lower triangular.
All inputs are finite; a program needn't handle non-finite values.
Results may differ from a plain program's by a relative error of at most 0.000061.
Values sent between devices are 32-bit elements; how exact they have to be, the bound alone decides.
No kernel may reach another device: no remote copies, remote signals or barrier semaphores. Data moves between devices by JAX's collectives and lax.ppermute only.
A program may use at most 64 MiB of HBM per device.

v0:
```python
import functools

import jax
import jax.numpy as jnp
from jax import lax
from jax.experimental import pallas as pl
from jax.experimental.pallas import tpu as pltpu
from jax.sharding import PartitionSpec as P


VMEM = pl.BlockSpec(memory_space=pltpu.VMEM)
SMEM = pl.BlockSpec(memory_space=pltpu.SMEM)


def swap(block, axis, mask):
    return lax.ppermute(block, axis, [(i, i ^ mask) for i in range(lax.axis_size(axis))])


def call(kernel, out_shape, scratch, where, *args):
    return pl.pallas_call(
        kernel,
        out_shape=out_shape,
        in_specs=[SMEM] + [VMEM] * len(args),
        out_specs=jax.tree.map(lambda _: VMEM, out_shape),
        scratch_shapes=scratch,
    )(where, *args)


def halves(value):
    high = value.astype(jnp.bfloat16)
    return high, (value - high.astype(jnp.float32)).astype(jnp.bfloat16)


def dot(a, b):
    return lax.dot_general(a, b, (((1,), (0,)), ((), ())), preferred_element_type=jnp.float32)


def product(high, low, pair):
    cols = pair.shape[1] // 2
    both = dot(high, pair)
    return both[:, :cols] + (both[:, cols:] + dot(low, pair[:, :cols]))


def prepare(n_rows, sources, where_ref, piv_row, piv_col, *refs):
    *blocks, top_ref, own_ref, whole = refs
    rows, cols = blocks[0].shape
    block = piv_row.shape[1]
    me = where_ref[0]
    for mask, ref in enumerate(blocks):
        whole[pl.ds(pl.multiple_of((me ^ mask) * rows, rows), rows), :] = ref[...]

    @pl.when(me < sources)
    def _():
        pivot = piv_col[...]
        high, low = halves(whole[pl.ds(0, block), :])
        picked = jnp.concatenate([high.astype(jnp.float32), low.astype(jnp.float32)], axis=1)
        picked = jnp.where(pivot < block, picked, 0.0)
        for source in range(sources, n_rows):
            ids = lax.broadcasted_iota(jnp.int32, (block, rows), 1) + source * rows
            chosen = (pivot == ids).astype(jnp.float32).astype(jnp.bfloat16)
            pair = jnp.concatenate(halves(whole[pl.ds(source * rows, rows), :]), axis=1)
            picked = picked + dot(chosen, pair)
        top_ref[...] = picked.astype(jnp.bfloat16)

    @pl.when(me >= sources)
    def _():
        ids = lax.broadcasted_iota(jnp.int32, (rows, block), 0) + me * rows
        match = piv_row[...] == ids
        chosen = match.astype(jnp.float32)
        named = jnp.max(chosen, axis=1, keepdims=True) > 0.0
        old = whole[pl.ds(0, block), :]
        high, middle = halves(old)
        low = (old - high.astype(jnp.float32) - middle.astype(jnp.float32)).astype(jnp.bfloat16)
        terms = dot(chosen.astype(jnp.bfloat16), jnp.concatenate([high, middle, low], axis=1))
        replaced = terms[:, :cols] + terms[:, cols : 2 * cols] + terms[:, 2 * cols :]
        own_ref[...] = jnp.where(named, replaced, blocks[0][...])


def collect(order, unit, chunk, me, pieces, high, low):
    for mask, ref in zip(order, pieces):
        at = pl.ds(pl.multiple_of((me ^ mask) * unit, unit), unit)
        start = 0 if ref.shape[0] == unit else chunk * unit
        high[at, :], low[at, :] = halves(ref[pl.ds(start, unit), :])


def early(order, unit, chunk, where_ref, *refs):
    *pieces, high, low = refs
    collect(order, unit, chunk, where_ref[1], pieces, high, low)


def solve(sources, order, unit, chunk, where_ref, top_ref, early_high, early_low, *refs):
    *pieces, out_ref, high, low = refs
    for mask in range(order[0]):
        at = pl.ds(pl.multiple_of((where_ref[1] ^ mask) * unit, unit), unit)
        high[at, :], low[at, :] = early_high[at, :], early_low[at, :]
    collect(order, unit, chunk, where_ref[1], pieces, high, low)

    @pl.when(where_ref[0] < sources)
    def _():
        out_ref[...] = product(high[...], low[...], top_ref[...])


def update(sources, masks, chunks, n_cols, where_ref, own_ref, *refs):
    solved, refs = refs[:chunks], refs[chunks:]
    split, refs = refs[: 2 * chunks], refs[2 * chunks :]
    *got, out_ref, upper = refs
    rows, _ = own_ref.shape
    depth = rows // n_cols
    unit = depth // chunks
    me = where_ref[0]

    @pl.when(me < sources)
    def _():
        for chunk in range(chunks):
            for i in range(n_cols):
                out_ref[pl.ds(i * depth + chunk * unit, unit), :] = solved[chunk][pl.ds(i * unit, unit), :]

    @pl.when(me >= sources)
    def _():
        for m, mask in enumerate(masks):
            source = me ^ mask

            @pl.when(source < sources)
            def _():
                for chunk in range(chunks):
                    ref = got[chunk * len(masks) + m]
                    for i in range(n_cols):
                        at = pl.multiple_of(source * rows, rows) + (i * depth + chunk * unit)
                        upper[pl.ds(pl.multiple_of(at, unit), unit), :] = ref[pl.ds(i * unit, unit), :]

        pair = jnp.concatenate(halves(upper[...]), axis=1)
        for chunk in range(chunks):
            part = product(split[2 * chunk][...], split[2 * chunk + 1][...], pair)
            for i in range(n_cols):
                at = pl.ds(i * depth + chunk * unit, unit)
                out_ref[at, :] = own_ref[at, :] - part[i * unit : (i + 1) * unit]


def per_device(matrix, panel, pivots):
    rows, cols = matrix.shape
    block = pivots.shape[0]
    depth = panel.shape[0]
    n_rows, n_cols = lax.axis_size("prow"), lax.axis_size("pcol")
    sources = block // rows
    chunks = 2 if depth % 32 == 0 else 1
    unit = depth // chunks
    where = jnp.stack([lax.axis_index("prow"), lax.axis_index("pcol")]).astype(jnp.int32)
    f32, bf16 = jnp.float32, jnp.bfloat16

    near = [panel, swap(panel, "pcol", 2)]
    near = [piece for block_ in near for piece in (block_, swap(block_, "pcol", 1))]
    far = []
    for chunk in range(chunks):
        part = panel[chunk * unit : (chunk + 1) * unit]
        got = [swap(part, "pcol", mask) for mask in range(4, n_cols, 2)]
        far.append([piece for block_ in got for piece in (block_, swap(block_, "pcol", 1))])
    blocks = [matrix] + [swap(matrix, "prow", mask) for mask in range(1, n_rows)]

    top, own = call(
        functools.partial(prepare, n_rows, sources),
        (jax.ShapeDtypeStruct((block, 2 * cols), bf16), jax.ShapeDtypeStruct((rows, cols), f32)),
        [pltpu.VMEM((n_rows * rows, cols), f32)],
        where, pivots.reshape(1, block), pivots.reshape(block, 1), *blocks,
    )

    masks = tuple(range(sources, n_rows))
    solved, split, got = [], [], []
    for chunk in range(chunks):
        terms = [jax.ShapeDtypeStruct((rows // chunks, block), bf16)] * 2
        high, low = call(
            functools.partial(early, range(len(near)), unit, chunk),
            terms,
            [],
            where, *near,
        )
        piece, high, low = call(
            functools.partial(solve, sources, tuple(range(len(near), n_cols)), unit, chunk),
            [jax.ShapeDtypeStruct((rows // chunks, cols), f32)] + terms,
            [],
            where, top, high, low, *far[chunk],
        )
        solved.append(piece)
        split += [high, low]
        got += [swap(piece, "prow", mask) for mask in masks]

    return call(
        functools.partial(update, sources, masks, chunks, n_cols),
        jax.ShapeDtypeStruct((rows, cols), f32),
        [pltpu.VMEM((block, cols), f32)],
        where, own, *solved, *split, *got,
    )


def solution(mesh):
    placed = (P("prow", "pcol"), P(("prow", "pcol"), None), P())
    return jax.shard_map(
        per_device, mesh=mesh, in_specs=placed, out_specs=P("prow", "pcol"), check_vma=False
    )
```

profile of v0, /device:TPU:0, one launch (start us, length us, event | category | flops | bytes accessed | tf_op | source)
XLA Modules:
  0.0 66.9 jit_solution(11690422355594787726)
XLA Ops:
  0.0 1.0 %fusion = (f32[32,1024]{1,0:T(8,128)S(1)}, f32[32,1024]{1,0:T(8,128)S(1)}) fusion(f32[64,1024]{1,0:T(8,128)} %refs_0_.5), kind=kLoop, calls=%fused_computation.1 | loop fusion | bytes 524288 | tf_op jit(solution)/shard_map/slice | solution.py:154
  1.1 4.1 %collective-permute-start.6 = (f32[32,1024]{1,0:T(8,128)S(1)}, f32[32,1024]{1,0:T(8,128)S(1)}, u32[]{:S(2)}, u32[]{:S(2)}) collective-permute-start(f32[32,1024]{1,0:T(8,128)S(1)} %get-tuple-element.30), channel_id=1, source_target_pairs={{0,4},{1,5},{2,6},{3,7},{4,0},{5,1},{6,2},{7,3},{8,12},{9,13},{10,... | collective-permute-start | bytes 393224 | tf_op jit(solution)/shard_map/ppermute | solution.py:16
  5.2 1.6 %collective-permute-start.4 = (f32[64,1024]{1,0:T(8,128)S(1)}, f32[64,1024]{1,0:T(8,128)S(1)}, u32[]{:S(2)}, u32[]{:S(2)}) collective-permute-start(f32[64,1024]{1,0:T(8,128)S(1)} %copy-done), channel_id=1, source_target_pairs={{0,2},{1,3},{2,0},{3,1},{4,6},{5,7},{6,4},{7,5},{8,10},{9,11},{10,... | collective-permute-start | bytes 786440 | tf_op jit(solution)/shard_map/ppermute | solution.py:16
  6.8 1.9 %collective-permute-start.10 = (f32[32,1024]{1,0:T(8,128)S(1)}, f32[32,1024]{1,0:T(8,128)S(1)}, u32[]{:S(2)}, u32[]{:S(2)}) collective-permute-start(f32[32,1024]{1,0:T(8,128)S(1)} %get-tuple-element.29), channel_id=1, source_target_pairs={{0,4},{1,5},{2,6},{3,7},{4,0},{5,1},{6,2},{7,3},{8,12},{9,13},{10,... | collective-permute-start | bytes 393224 | tf_op jit(solution)/shard_map/ppermute | solution.py:16
  8.7 1.9 %collective-permute-start.12 = (f32[32,1024]{1,0:T(8,128)S(1)}, f32[32,1024]{1,0:T(8,128)S(1)}, u32[]{:S(2)}, u32[]{:S(2)}) collective-permute-start(f32[32,1024]{1,0:T(8,128)S(1)} %get-tuple-element.29), channel_id=1, source_target_pairs={{0,6},{1,7},{2,4},{3,5},{4,2},{5,3},{6,0},{7,1},{8,14},{9,15},{10,... | collective-permute-start | bytes 393224 | tf_op jit(solution)/shard_map/ppermute | solution.py:16
  10.6 1.8 %collective-permute-done.6.refs_0_ = f32[32,1024]{1,0:T(8,128)S(1)} collective-permute-done((f32[32,1024]{1,0:T(8,128)S(1)}, f32[32,1024]{1,0:T(8,128)S(1)}, u32[]{:S(2)}, u32[]{:S(2)}) %collective-permute-start.6) | collective-permute-done | bytes 131104 | tf_op jit(solution)/shard_map/ppermute | solution.py:16
  12.3 1.8 %collective-permute-start = (f32[512,128]{1,0:T(8,128)S(1)}, f32[512,128]{1,0:T(8,128)S(1)}, u32[]{:S(2)}, u32[]{:S(2)}) collective-permute-start(f32[512,128]{1,0:T(8,128)S(1)} %copy-done.4), channel_id=1, source_target_pairs={{0,8},{8,0},{16,24},{24,16},{1,9},{9,1},{17,25},{25,17},{2,10},{10... | collective-permute-start | bytes 786440 | tf_op jit(solution)/shard_map/ppermute | solution.py:16
  14.1 5.3 %collective-permute-done.8.refs_2_ = f32[32,1024]{1,0:T(8,128)S(1)} collective-permute-done((f32[32,1024]{1,0:T(8,128)S(1)}, f32[32,1024]{1,0:T(8,128)S(1)}, u32[]{:S(2)}, u32[]{:S(2)}) %collective-permute-start.8) | collective-permute-done | bytes 131104 | tf_op jit(solution)/shard_map/ppermute | solution.py:16
  19.4 1.5 %collective-permute-start.1 = (f32[512,128]{1,0:T(8,128)S(1)}, f32[512,128]{1,0:T(8,128)S(1)}, u32[]{:S(2)}, u32[]{:S(2)}) collective-permute-start(f32[512,128]{1,0:T(8,128)S(1)} %copy-done.4), channel_id=1, source_target_pairs={{0,16},{8,24},{16,0},{24,8},{1,17},{9,25},{17,1},{25,9},{2,18},{10... | collective-permute-start | bytes 786440 | tf_op jit(solution)/shard_map/ppermute | solution.py:16
  20.9 5.5 %collective-permute-done.10.refs_0_ = f32[32,1024]{1,0:T(8,128)S(1)} collective-permute-done((f32[32,1024]{1,0:T(8,128)S(1)}, f32[32,1024]{1,0:T(8,128)S(1)}, u32[]{:S(2)}, u32[]{:S(2)}) %collective-permute-start.10) | collective-permute-done | bytes 131104 | tf_op jit(solution)/shard_map/ppermute | solution.py:16
  26.4 2.8 %collective-permute-start.2 = (f32[512,128]{1,0:T(8,128)S(1)}, f32[512,128]{1,0:T(8,128)S(1)}, u32[]{:S(2)}, u32[]{:S(2)}) collective-permute-start(f32[512,128]{1,0:T(8,128)S(1)} %copy-done.4), channel_id=1, source_target_pairs={{0,24},{8,16},{16,8},{24,0},{1,25},{9,17},{17,9},{25,1},{2,26},{10... | collective-permute-start | bytes 786440 | tf_op jit(solution)/shard_map/ppermute | solution.py:16
  29.1 0.0 collective-permute-start.3
  29.2 0.0 collective-permute-done.4.refs_2_
  29.2 0.5 collective-permute-start.5
  29.7 0.0 collective-permute-done.refs_1_
  29.7 0.1 collective-permute-start.7
  29.8 0.0 collective-permute-done.1.refs_2_
  29.8 0.4 collective-permute-start.9
  30.2 3.7 %collective-permute-done.2.refs_3_ = f32[512,128]{1,0:T(8,128)S(1)} collective-permute-done((f32[512,128]{1,0:T(8,128)S(1)}, f32[512,128]{1,0:T(8,128)S(1)}, u32[]{:S(2)}, u32[]{:S(2)}) %collective-permute-start.2) | collective-permute-done | bytes 262176 | tf_op jit(solution)/shard_map/ppermute | solution.py:16
  33.9 0.5 collective-permute-start.13
  34.4 0.7 %copy-done.20 = s32[1024]{0:T(1024)S(1)} copy-done((s32[1024]{0:T(1024)S(1)}, s32[1024]{0:T(1024)}, u32[]{:S(2)}) %copy-start.20) | copy-done | bytes 4120
  35.1 1.0 %copy.4.piv_col = s32[1024,1]{1,0:T(8,128)} copy(s32[1024,1]{0,1:T(1,128)S(1)} %bitcast.5) | data formatting | bytes 8192 | tf_op jit(solution)/shard_map/reshape | solution.py:163
  36.1 0.6 pad_add_fusion.where_ref
  36.7 3.1 %shard_map.37 = (bf16[1024,256]{1,0:T(8,128)(2,1)}, f32[512,128]{1,0:T(8,128)}) custom-call(s32[2]{0:T(128)} %pad_add_fusion.where_ref, s32[1,1024]{1,0:T(1,128)} %bitcast.4, s32[1024,1]{1,0:T(8,128)} %copy.4.piv_col, f32[512,128]{1,0:T(8,128)} %refs_0_.3, f32[512,128]{1,0:T(8,128)} %copy-done.5, f32[512,128]{1,0:T(8,128)} %copy-done.6, f32[512,128]{1,0:T(8,128)} %copy-done.7), custom_call_target="tpu_custom_call" | custom-call | tf_op jit(solution)/shard_map/pallas_call | solution.py:20
  39.9 0.0 collective-permute-done.5.refs_3_
  39.9 0.0 copy-start.3
  39.9 0.7 %copy-done.3 = f32[64,1024]{1,0:T(8,128)} copy-done((f32[64,1024]{1,0:T(8,128)}, f32[64,1024]{1,0:T(8,128)S(1)}, u32[]{:S(2)}) %copy-start.3) | copy-done | bytes 262168
  40.6 2.2 %shard_map.38 = (bf16[256,1024]{1,0:T(8,128)(2,1)}, bf16[256,1024]{1,0:T(8,128)(2,1)}) custom-call(s32[2]{0:T(128)} %pad_add_fusion.where_ref, f32[64,1024]{1,0:T(8,128)} %refs_0_.5, f32[64,1024]{1,0:T(8,128)} %copy-done.2, f32[64,1024]{1,0:T(8,128)} %copy-done.1, f32[64,1024]{1,0:T(8,128)} %copy-done.3), custom_call_target="tpu_custom_call" | custom-call | tf_op jit(solution)/shard_map/pallas_call | solution.py:20
  42.8 0.0 collective-permute-done.7.refs_1_
  42.9 0.0 collective-permute-done.9.refs_3_
  42.9 0.6 copy-done.14
  43.5 0.1 copy-done.15
  43.6 3.0 %shard_map.39 = (f32[256,128]{1,0:T(8,128)}, bf16[256,1024]{1,0:T(8,128)(2,1)}, bf16[256,1024]{1,0:T(8,128)(2,1)}) custom-call(s32[2]{0:T(128)} %pad_add_fusion.where_ref, bf16[1024,256]{1,0:T(8,128)(2,1)} %get-tuple-element.18.top_ref, bf16[256,1024]{1,0:T(8,128)(2,1)} %get-tuple-element.19.early_high, bf16[256,1024]{1,0:T(8,128)(2,1)} %get-tuple-element.20.early_low, ...), custom_call_target="tpu_custom_call" | custom-call | tf_op jit(solution)/shard_map/pallas_call | solution.py:20
  46.6 1.2 %collective-permute-start.14 = (f32[256,128]{1,0:T(8,128)}, f32[256,128]{1,0:T(8,128)S(1)}, u32[]{:S(2)}, u32[]{:S(2)}) collective-permute-start(f32[256,128]{1,0:T(8,128)} %get-tuple-element.21.refs_0_), channel_id=1, source_target_pairs={{0,16},{8,24},{16,0},{24,8},{1,17},{9,25},{17,1},{25,9},{2,18},{10... | collective-permute-start | bytes 393224 | tf_op jit(solution)/shard_map/ppermute | solution.py:16
  47.8 1.8 %collective-permute-start.15 = (f32[256,128]{1,0:T(8,128)}, f32[256,128]{1,0:T(8,128)S(1)}, u32[]{:S(2)}, u32[]{:S(2)}) collective-permute-start(f32[256,128]{1,0:T(8,128)} %get-tuple-element.21.refs_0_), channel_id=1, source_target_pairs={{0,24},{8,16},{16,8},{24,0},{1,25},{9,17},{17,9},{25,1},{2,26},{10... | collective-permute-start | bytes 393224 | tf_op jit(solution)/shard_map/ppermute | solution.py:16
  49.6 2.2 %shard_map.40 = (bf16[256,1024]{1,0:T(8,128)(2,1)}, bf16[256,1024]{1,0:T(8,128)(2,1)}) custom-call(s32[2]{0:T(128)} %pad_add_fusion.where_ref, f32[64,1024]{1,0:T(8,128)} %refs_0_.5, f32[64,1024]{1,0:T(8,128)} %copy-done.2, f32[64,1024]{1,0:T(8,128)} %copy-done.1, f32[64,1024]{1,0:T(8,128)} %copy-done.3), custom_call_target="tpu_custom_call" | custom-call | tf_op jit(solution)/shard_map/pallas_call | solution.py:20
  51.9 0.0 collective-permute-done.11.refs_1_
  51.9 0.6 copy-done.12
  52.5 0.0 copy-done.13
  52.6 3.0 %shard_map.41 = (f32[256,128]{1,0:T(8,128)}, bf16[256,1024]{1,0:T(8,128)(2,1)}, bf16[256,1024]{1,0:T(8,128)(2,1)}) custom-call(s32[2]{0:T(128)} %pad_add_fusion.where_ref, bf16[1024,256]{1,0:T(8,128)(2,1)} %get-tuple-element.18.top_ref, bf16[256,1024]{1,0:T(8,128)(2,1)} %get-tuple-element.22.early_high, bf16[256,1024]{1,0:T(8,128)(2,1)} %get-tuple-element.23.early_low, ...), custom_call_target="tpu_custom_call" | custom-call | tf_op jit(solution)/shard_map/pallas_call | solution.py:20
  55.6 0.7 %collective-permute-start.16 = (f32[256,128]{1,0:T(8,128)}, f32[256,128]{1,0:T(8,128)S(1)}, u32[]{:S(2)}, u32[]{:S(2)}) collective-permute-start(f32[256,128]{1,0:T(8,128)} %get-tuple-element.24.refs_1_), channel_id=1, source_target_pairs={{0,16},{8,24},{16,0},{24,8},{1,17},{9,25},{17,1},{25,9},{2,18},{10... | collective-permute-start | bytes 393224 | tf_op jit(solution)/shard_map/ppermute | solution.py:16
  56.3 1.3 %collective-permute-start.17 = (f32[256,128]{1,0:T(8,128)}, f32[256,128]{1,0:T(8,128)S(1)}, u32[]{:S(2)}, u32[]{:S(2)}) collective-permute-start(f32[256,128]{1,0:T(8,128)} %get-tuple-element.24.refs_1_), channel_id=1, source_target_pairs={{0,24},{8,16},{16,8},{24,0},{1,25},{9,17},{17,9},{25,1},{2,26},{10... | collective-permute-start | bytes 393224 | tf_op jit(solution)/shard_map/ppermute | solution.py:16
  57.5 0.0 collective-permute-done.14.refs_6_
  57.6 6.0 %collective-permute-done.16.refs_8_ = f32[256,128]{1,0:T(8,128)S(1)} collective-permute-done((f32[256,128]{1,0:T(8,128)}, f32[256,128]{1,0:T(8,128)S(1)}, u32[]{:S(2)}, u32[]{:S(2)}) %collective-permute-start.16) | collective-permute-done | bytes 131104 | tf_op jit(solution)/shard_map/ppermute | solution.py:16
  63.6 0.0 collective-permute-done.17.refs_9_
  63.6 0.6 copy-done.18
  64.2 0.1 copy-done.19
  64.3 2.6 %shard_map.42 = f32[512,128]{1,0:T(8,128)} custom-call(s32[2]{0:T(128)} %pad_add_fusion.where_ref, f32[512,128]{1,0:T(8,128)} %get-tuple-element.17.own_ref, f32[256,128]{1,0:T(8,128)} %get-tuple-element.21.refs_0_, f32[256,128]{1,0:T(8,128)} %get-tuple-element.24.refs_1_, bf16[256,1024]{1,0:T(8,128)(2,1)} %get-tuple-element.25.refs_2_, ...), custom_call_target="tpu_custom_call" | custom-call | tf_op jit(solution)/shard_map/pallas_call | solution.py:20
  (39 shorter events, 0.1 us)
Async XLA Ops:
  0.0 5.2 %copy-start = (f32[64,1024]{1,0:T(8,128)S(1)}, f32[64,1024]{1,0:T(8,128)}, u32[]{:S(2)}) copy-start(f32[64,1024]{1,0:T(8,128)} %refs_0_.5) | copy-start | bytes 786436
  0.0 12.3 %copy-start.4 = (f32[512,128]{1,0:T(8,128)S(1)}, f32[512,128]{1,0:T(8,128)}, u32[]{:S(2)}) copy-start(f32[512,128]{1,0:T(8,128)} %refs_0_.3) | copy-start | bytes 786436
  1.1 11.3 %collective-permute-start.6 = (f32[32,1024]{1,0:T(8,128)S(1)}, f32[32,1024]{1,0:T(8,128)S(1)}, u32[]{:S(2)}, u32[]{:S(2)}) collective-permute-start(f32[32,1024]{1,0:T(8,128)S(1)} %get-tuple-element.30), channel_id=1, source_target_pairs={{0,4},{1,5},{2,6},{3,7},{4,0},{5,1},{6,2},{7,3},{8,12},{9,13},{10,... | collective-permute-start | bytes 393224 | tf_op jit(solution)/shard_map/ppermute | solution.py:16
  5.2 24.0 %collective-permute-start.4 = (f32[64,1024]{1,0:T(8,128)S(1)}, f32[64,1024]{1,0:T(8,128)S(1)}, u32[]{:S(2)}, u32[]{:S(2)}) collective-permute-start(f32[64,1024]{1,0:T(8,128)S(1)} %copy-done), channel_id=1, source_target_pairs={{0,2},{1,3},{2,0},{3,1},{4,6},{5,7},{6,4},{7,5},{8,10},{9,11},{10,... | collective-permute-start | bytes 786440 | tf_op jit(solution)/shard_map/ppermute | solution.py:16
  6.8 12.6 %collective-permute-start.8 = (f32[32,1024]{1,0:T(8,128)S(1)}, f32[32,1024]{1,0:T(8,128)S(1)}, u32[]{:S(2)}, u32[]{:S(2)}) collective-permute-start(f32[32,1024]{1,0:T(8,128)S(1)} %get-tuple-element.30), channel_id=1, source_target_pairs={{0,6},{1,7},{2,4},{3,5},{4,2},{5,3},{6,0},{7,1},{8,14},{9,15},{10,... | collective-permute-start | bytes 393224 | tf_op jit(solution)/shard_map/ppermute | solution.py:16
  6.8 19.6 %collective-permute-start.10 = (f32[32,1024]{1,0:T(8,128)S(1)}, f32[32,1024]{1,0:T(8,128)S(1)}, u32[]{:S(2)}, u32[]{:S(2)}) collective-permute-start(f32[32,1024]{1,0:T(8,128)S(1)} %get-tuple-element.29), channel_id=1, source_target_pairs={{0,4},{1,5},{2,6},{3,7},{4,0},{5,1},{6,2},{7,3},{8,12},{9,13},{10,... | collective-permute-start | bytes 393224 | tf_op jit(solution)/shard_map/ppermute | solution.py:16
  8.7 20.5 %collective-permute-start.12 = (f32[32,1024]{1,0:T(8,128)S(1)}, f32[32,1024]{1,0:T(8,128)S(1)}, u32[]{:S(2)}, u32[]{:S(2)}) collective-permute-start(f32[32,1024]{1,0:T(8,128)S(1)} %get-tuple-element.29), channel_id=1, source_target_pairs={{0,6},{1,7},{2,4},{3,5},{4,2},{5,3},{6,0},{7,1},{8,14},{9,15},{10,... | collective-permute-start | bytes 393224 | tf_op jit(solution)/shard_map/ppermute | solution.py:16
  12.3 27.5 %copy-start.10 = (f32[32,1024]{1,0:T(8,128)}, f32[32,1024]{1,0:T(8,128)S(1)}, u32[]{:S(2)}) copy-start(f32[32,1024]{1,0:T(8,128)S(1)} %collective-permute-done.6.refs_0_) | copy-start | bytes 393220
  12.3 17.3 %collective-permute-start = (f32[512,128]{1,0:T(8,128)S(1)}, f32[512,128]{1,0:T(8,128)S(1)}, u32[]{:S(2)}, u32[]{:S(2)}) collective-permute-start(f32[512,128]{1,0:T(8,128)S(1)} %copy-done.4), channel_id=1, source_target_pairs={{0,8},{8,0},{16,24},{24,16},{1,9},{9,1},{17,25},{25,17},{2,10},{10... | collective-permute-start | bytes 786440 | tf_op jit(solution)/shard_map/ppermute | solution.py:16
  19.4 20.5 %copy-start.11 = (f32[32,1024]{1,0:T(8,128)}, f32[32,1024]{1,0:T(8,128)S(1)}, u32[]{:S(2)}) copy-start(f32[32,1024]{1,0:T(8,128)S(1)} %collective-permute-done.8.refs_2_) | copy-start | bytes 393220
  19.4 10.4 %collective-permute-start.1 = (f32[512,128]{1,0:T(8,128)S(1)}, f32[512,128]{1,0:T(8,128)S(1)}, u32[]{:S(2)}, u32[]{:S(2)}) collective-permute-start(f32[512,128]{1,0:T(8,128)S(1)} %copy-done.4), channel_id=1, source_target_pairs={{0,16},{8,24},{16,0},{24,8},{1,17},{9,25},{17,1},{25,9},{2,18},{10... | collective-permute-start | bytes 786440 | tf_op jit(solution)/shard_map/ppermute | solution.py:16
  26.4 13.5 %copy-start.8 = (f32[32,1024]{1,0:T(8,128)}, f32[32,1024]{1,0:T(8,128)S(1)}, u32[]{:S(2)}) copy-start(f32[32,1024]{1,0:T(8,128)S(1)} %collective-permute-done.10.refs_0_) | copy-start | bytes 393220
  26.4 7.5 %collective-permute-start.2 = (f32[512,128]{1,0:T(8,128)S(1)}, f32[512,128]{1,0:T(8,128)S(1)}, u32[]{:S(2)}, u32[]{:S(2)}) collective-permute-start(f32[512,128]{1,0:T(8,128)S(1)} %copy-done.4), channel_id=1, source_target_pairs={{0,24},{8,16},{16,8},{24,0},{1,25},{9,17},{17,9},{25,1},{2,26},{10... | collective-permute-start | bytes 786440 | tf_op jit(solution)/shard_map/ppermute | solution.py:16
  29.1 10.7 %copy-start.9 = (f32[32,1024]{1,0:T(8,128)}, f32[32,1024]{1,0:T(8,128)S(1)}, u32[]{:S(2)}) copy-start(f32[32,1024]{1,0:T(8,128)S(1)} %collective-permute-done.12.refs_2_) | copy-start | bytes 393220
  29.1 4.8 %collective-permute-start.3 = (f32[64,1024]{1,0:T(8,128)S(1)}, f32[64,1024]{1,0:T(8,128)S(1)}, u32[]{:S(2)}, u32[]{:S(2)}) collective-permute-start(f32[64,1024]{1,0:T(8,128)S(1)} %copy-done), channel_id=1, source_target_pairs={{0,1},{1,0},{2,3},{3,2},{4,5},{5,4},{6,7},{7,6},{8,9},{9,8},{10,11... | collective-permute-start | bytes 786440 | tf_op jit(solution)/shard_map/ppermute | solution.py:16
  29.2 7.0 %copy-start.1 = (f32[64,1024]{1,0:T(8,128)}, f32[64,1024]{1,0:T(8,128)S(1)}, u32[]{:S(2)}) copy-start(f32[64,1024]{1,0:T(8,128)S(1)} %collective-permute-done.4.refs_2_) | copy-start | bytes 786436
  29.2 10.7 %collective-permute-start.5 = (f32[64,1024]{1,0:T(8,128)S(1)}, f32[64,1024]{1,0:T(8,128)S(1)}, u32[]{:S(2)}, u32[]{:S(2)}) collective-permute-start(f32[64,1024]{1,0:T(8,128)S(1)} %collective-permute-done.4.refs_2_), channel_id=1, source_target_pairs={{0,1},{1,0},{2,3},{3,2},{4,5},{5,4},{6,7},{7,6},{8,9},{9,8},{10,11... | collective-permute-start | bytes 786440 | tf_op jit(solution)/shard_map/ppermute | solution.py:16
  29.7 7.1 %copy-start.5 = (f32[512,128]{1,0:T(8,128)}, f32[512,128]{1,0:T(8,128)S(1)}, u32[]{:S(2)}) copy-start(f32[512,128]{1,0:T(8,128)S(1)} %collective-permute-done.refs_1_) | copy-start | bytes 786436
  29.7 13.2 %collective-permute-start.7 = (f32[32,1024]{1,0:T(8,128)S(1)}, f32[32,1024]{1,0:T(8,128)S(1)}, u32[]{:S(2)}, u32[]{:S(2)}) collective-permute-start(f32[32,1024]{1,0:T(8,128)S(1)} %collective-permute-done.6.refs_0_), channel_id=1, source_target_pairs={{0,1},{1,0},{2,3},{3,2},{4,5},{5,4},{6,7},{7,6},{8,9},{9,8},{10,11... | collective-permute-start | bytes 393224 | tf_op jit(solution)/shard_map/ppermute | solution.py:16
  29.8 7.0 %copy-start.6 = (f32[512,128]{1,0:T(8,128)}, f32[512,128]{1,0:T(8,128)S(1)}, u32[]{:S(2)}) copy-start(f32[512,128]{1,0:T(8,128)S(1)} %collective-permute-done.1.refs_2_) | copy-start | bytes 786436
  29.8 13.1 %collective-permute-start.9 = (f32[32,1024]{1,0:T(8,128)S(1)}, f32[32,1024]{1,0:T(8,128)S(1)}, u32[]{:S(2)}, u32[]{:S(2)}) collective-permute-start(f32[32,1024]{1,0:T(8,128)S(1)} %collective-permute-done.8.refs_2_), channel_id=1, source_target_pairs={{0,1},{1,0},{2,3},{3,2},{4,5},{5,4},{6,7},{7,6},{8,9},{9,8},{10,11... | collective-permute-start | bytes 393224 | tf_op jit(solution)/shard_map/ppermute | solution.py:16
  33.9 2.8 %copy-start.7 = (f32[512,128]{1,0:T(8,128)}, f32[512,128]{1,0:T(8,128)S(1)}, u32[]{:S(2)}) copy-start(f32[512,128]{1,0:T(8,128)S(1)} %collective-permute-done.2.refs_3_) | copy-start | bytes 786436
  33.9 18.0 %collective-permute-start.11 = (f32[32,1024]{1,0:T(8,128)S(1)}, f32[32,1024]{1,0:T(8,128)S(1)}, u32[]{:S(2)}, u32[]{:S(2)}) collective-permute-start(f32[32,1024]{1,0:T(8,128)S(1)} %collective-permute-done.10.refs_0_), channel_id=1, source_target_pairs={{0,1},{1,0},{2,3},{3,2},{4,5},{5,4},{6,7},{7,6},{8,9},{9,8},{10,11... | collective-permute-start | bytes 393224 | tf_op jit(solution)/shard_map/ppermute | solution.py:16
  33.9 2.2 %copy-start.2 = (f32[64,1024]{1,0:T(8,128)}, f32[64,1024]{1,0:T(8,128)S(1)}, u32[]{:S(2)}) copy-start(f32[64,1024]{1,0:T(8,128)S(1)} %collective-permute-done.3.refs_1_) | copy-start | bytes 786436
  33.9 17.9 %collective-permute-start.13 = (f32[32,1024]{1,0:T(8,128)S(1)}, f32[32,1024]{1,0:T(8,128)S(1)}, u32[]{:S(2)}, u32[]{:S(2)}) collective-permute-start(f32[32,1024]{1,0:T(8,128)S(1)} %collective-permute-done.12.refs_2_), channel_id=1, source_target_pairs={{0,1},{1,0},{2,3},{3,2},{4,5},{5,4},{6,7},{7,6},{8,9},{9,8},{10,11... | collective-permute-start | bytes 393224 | tf_op jit(solution)/shard_map/ppermute | solution.py:16
  34.4 0.7 %copy-start.20 = (s32[1024]{0:T(1024)S(1)}, s32[1024]{0:T(1024)}, u32[]{:S(2)}) copy-start(s32[1024]{0:T(1024)} %param.5) | copy-start | bytes 12292
  39.9 0.7 %copy-start.3 = (f32[64,1024]{1,0:T(8,128)}, f32[64,1024]{1,0:T(8,128)S(1)}, u32[]{:S(2)}) copy-start(f32[64,1024]{1,0:T(8,128)S(1)} %collective-permute-done.5.refs_3_) | copy-start | bytes 786436
  42.8 0.6 copy-start.14
  42.9 0.7 %copy-start.15 = (f32[32,1024]{1,0:T(8,128)}, f32[32,1024]{1,0:T(8,128)S(1)}, u32[]{:S(2)}) copy-start(f32[32,1024]{1,0:T(8,128)S(1)} %collective-permute-done.9.refs_3_) | copy-start | bytes 393220
  46.6 10.9 %collective-permute-start.14 = (f32[256,128]{1,0:T(8,128)}, f32[256,128]{1,0:T(8,128)S(1)}, u32[]{:S(2)}, u32[]{:S(2)}) collective-permute-start(f32[256,128]{1,0:T(8,128)} %get-tuple-element.21.refs_0_), channel_id=1, source_target_pairs={{0,16},{8,24},{16,0},{24,8},{1,17},{9,25},{17,1},{25,9},{2,18},{10... | collective-permute-start | bytes 393224 | tf_op jit(solution)/shard_map/ppermute | solution.py:16
  47.8 9.7 %collective-permute-start.15 = (f32[256,128]{1,0:T(8,128)}, f32[256,128]{1,0:T(8,128)S(1)}, u32[]{:S(2)}, u32[]{:S(2)}) collective-permute-start(f32[256,128]{1,0:T(8,128)} %get-tuple-element.21.refs_0_), channel_id=1, source_target_pairs={{0,24},{8,16},{16,8},{24,0},{1,25},{9,17},{17,9},{25,1},{2,26},{10... | collective-permute-start | bytes 393224 | tf_op jit(solution)/shard_map/ppermute | solution.py:16
  51.9 0.7 copy-start.12
  51.9 0.7 %copy-start.13 = (f32[32,1024]{1,0:T(8,128)}, f32[32,1024]{1,0:T(8,128)S(1)}, u32[]{:S(2)}) copy-start(f32[32,1024]{1,0:T(8,128)S(1)} %collective-permute-done.13.refs_3_) | copy-start | bytes 393220
  55.6 8.0 %collective-permute-start.16 = (f32[256,128]{1,0:T(8,128)}, f32[256,128]{1,0:T(8,128)S(1)}, u32[]{:S(2)}, u32[]{:S(2)}) collective-permute-start(f32[256,128]{1,0:T(8,128)} %get-tuple-element.24.refs_1_), channel_id=1, source_target_pairs={{0,16},{8,24},{16,0},{24,8},{1,17},{9,25},{17,1},{25,9},{2,18},{10... | collective-permute-start | bytes 393224 | tf_op jit(solution)/shard_map/ppermute | solution.py:16
  56.3 7.3 %collective-permute-start.17 = (f32[256,128]{1,0:T(8,128)}, f32[256,128]{1,0:T(8,128)S(1)}, u32[]{:S(2)}, u32[]{:S(2)}) collective-permute-start(f32[256,128]{1,0:T(8,128)} %get-tuple-element.24.refs_1_), channel_id=1, source_target_pairs={{0,24},{8,16},{16,8},{24,0},{1,25},{9,17},{17,9},{25,1},{2,26},{10... | collective-permute-start | bytes 393224 | tf_op jit(solution)/shard_map/ppermute | solution.py:16
  57.5 6.0 %copy-start.16 = (f32[256,128]{1,0:T(8,128)}, f32[256,128]{1,0:T(8,128)S(1)}, u32[]{:S(2)}) copy-start(f32[256,128]{1,0:T(8,128)S(1)} %collective-permute-done.14.refs_6_) | copy-start | bytes 393220
  57.5 6.0 %copy-start.17 = (f32[256,128]{1,0:T(8,128)}, f32[256,128]{1,0:T(8,128)S(1)}, u32[]{:S(2)}) copy-start(f32[256,128]{1,0:T(8,128)S(1)} %collective-permute-done.15.refs_7_) | copy-start | bytes 393220
  63.6 0.7 copy-start.18
  63.6 0.7 %copy-start.19 = (f32[256,128]{1,0:T(8,128)}, f32[256,128]{1,0:T(8,128)S(1)}, u32[]{:S(2)}) copy-start(f32[256,128]{1,0:T(8,128)S(1)} %collective-permute-done.17.refs_9_) | copy-start | bytes 393220
where the time goes:
time: 67.2 us; the launch traced here: 66.9 us
  waiting for transfers between devices  22.2 us (33%)
  starting transfers between devices  22.1 us (33%)
  Pallas kernels  16.2 us (24%)
  local copies, waits for them, and re-layouts  5.58 us (8%)
    ppermute x18, waiting for transfers between devices, swap(): lax.ppermute(block, axis, [(i, i ^ mask) for i in range(lax.axis_size(axi...  22.2 us
    ppermute x18, starting transfers between devices, swap(): lax.ppermute(block, axis, [(i, i ^ mask) for i in range(lax.axis_size(axi...  22.1 us
    pallas_call x6, Pallas kernels, call(): pl.pallas_call(kernel, out_shape=out_shape, in_specs=[SMEM] + [VMEM] * le...  16.2 us
    unnamed x42, local copies, waits for them, and re-layouts  3.51 us
  transfers between devices with their start and end apart: 18, of which 5 were waited for; matrix products, arithmetic and copies ran while one was open for 2% of the time, Pallas kernels for 20%

commit v1 on v0

--- a/solution.py
+++ b/solution.py
@@ -9,21 +9,21 @@
 
 
 VMEM = pl.BlockSpec(memory_space=pltpu.VMEM)
-SMEM = pl.BlockSpec(memory_space=pltpu.SMEM)
 
 
 def swap(block, axis, mask):
     return lax.ppermute(block, axis, [(i, i ^ mask) for i in range(lax.axis_size(axis))])
 
 
-def call(kernel, out_shape, scratch, where, *args):
+def call(kernel, out_shape, scratch, *args):
     return pl.pallas_call(
         kernel,
         out_shape=out_shape,
-        in_specs=[SMEM] + [VMEM] * len(args),
+        in_specs=[VMEM] * len(args),
         out_specs=jax.tree.map(lambda _: VMEM, out_shape),
         scratch_shapes=scratch,
-    )(where, *args)
+        compiler_params=pltpu.CompilerParams(vmem_limit_bytes=16 * 2**20),
+    )(*(pltpu.with_memory_space_constraint(arg, pltpu.VMEM) for arg in args))
 
 
 def halves(value):
@@ -41,23 +41,25 @@
     return both[:, :cols] + (both[:, cols:] + dot(low, pair[:, :cols]))
 
 
-def prepare(n_rows, sources, where_ref, piv_row, piv_col, *refs):
+def prepare(n_rows, sources, piv_row, *refs):
     *blocks, top_ref, own_ref, whole = refs
     rows, cols = blocks[0].shape
     block = piv_row.shape[1]
-    me = where_ref[0]
+    me = lax.axis_index("prow")
     for mask, ref in enumerate(blocks):
         whole[pl.ds(pl.multiple_of((me ^ mask) * rows, rows), rows), :] = ref[...]
 
     @pl.when(me < sources)
     def _():
-        pivot = piv_col[...]
+        lanes = 128
+        pivot = jnp.broadcast_to(piv_row[...], (lanes, block)).T
         high, low = halves(whole[pl.ds(0, block), :])
         picked = jnp.concatenate([high.astype(jnp.float32), low.astype(jnp.float32)], axis=1)
-        picked = jnp.where(pivot < block, picked, 0.0)
+        picked = jnp.where(pivot[:, :1] < block, picked, 0.0)
         for source in range(sources, n_rows):
-            ids = lax.broadcasted_iota(jnp.int32, (block, rows), 1) + source * rows
-            chosen = (pivot == ids).astype(jnp.float32).astype(jnp.bfloat16)
+            ids = lax.broadcasted_iota(jnp.int32, (block, lanes), 1) + source * rows
+            chosen = [(pivot - i == ids).astype(jnp.float32).astype(jnp.bfloat16) for i in range(0, rows, lanes)]
+            chosen = jnp.concatenate(chosen, axis=1)
             pair = jnp.concatenate(halves(whole[pl.ds(source * rows, rows), :]), axis=1)
             picked = picked + dot(chosen, pair)
         top_ref[...] = picked.astype(jnp.bfloat16)
@@ -83,31 +85,31 @@
         high[at, :], low[at, :] = halves(ref[pl.ds(start, unit), :])
 
 
-def early(order, unit, chunk, where_ref, *refs):
+def early(order, unit, chunk, *refs):
     *pieces, high, low = refs
-    collect(order, unit, chunk, where_ref[1], pieces, high, low)
+    collect(order, unit, chunk, lax.axis_index("pcol"), pieces, high, low)
 
 
-def solve(sources, order, unit, chunk, where_ref, top_ref, early_high, early_low, *refs):
+def solve(sources, order, unit, chunk, top_ref, early_high, early_low, *refs):
     *pieces, out_ref, high, low = refs
     for mask in range(order[0]):
-        at = pl.ds(pl.multiple_of((where_ref[1] ^ mask) * unit, unit), unit)
+        at = pl.ds(pl.multiple_of((lax.axis_index("pcol") ^ mask) * unit, unit), unit)
         high[at, :], low[at, :] = early_high[at, :], early_low[at, :]
-    collect(order, unit, chunk, where_ref[1], pieces, high, low)
+    collect(order, unit, chunk, lax.axis_index("pcol"), pieces, high, low)
 
-    @pl.when(where_ref[0] < sources)
+    @pl.when(lax.axis_index("prow") < sources)
     def _():
         out_ref[...] = product(high[...], low[...], top_ref[...])
 
 
-def update(sources, masks, chunks, n_cols, where_ref, own_ref, *refs):
+def update(sources, masks, chunks, n_cols, own_ref, *refs):
     solved, refs = refs[:chunks], refs[chunks:]
     split, refs = refs[: 2 * chunks], refs[2 * chunks :]
     *got, out_ref, upper = refs
     rows, _ = own_ref.shape
     depth = rows // n_cols
     unit = depth // chunks
-    me = where_ref[0]
+    me = lax.axis_index("prow")
 
     @pl.when(me < sources)
     def _():
@@ -144,7 +146,6 @@
     sources = block // rows
     chunks = 2 if depth % 32 == 0 else 1
     unit = depth // chunks
-    where = jnp.stack([lax.axis_index("prow"), lax.axis_index("pcol")]).astype(jnp.int32)
     f32, bf16 = jnp.float32, jnp.bfloat16
 
     near = [panel, swap(panel, "pcol", 2)]
@@ -158,26 +159,21 @@
 
     top, own = call(
         functools.partial(prepare, n_rows, sources),
-        (jax.ShapeDtypeStruct((block, 2 * cols), bf16), jax.ShapeDtypeStruct((rows, cols), f32)),
+        (pltpu.VMEM((block, 2 * cols), bf16), pltpu.VMEM((rows, cols), f32)),
         [pltpu.VMEM((n_rows * rows, cols), f32)],
-        where, pivots.reshape(1, block), pivots.reshape(block, 1), *blocks,
+        pivots.reshape(1, block), *blocks,
     )
 
     masks = tuple(range(sources, n_rows))
     solved, split, got = [], [], []
     for chunk in range(chunks):
-        terms = [jax.ShapeDtypeStruct((rows // chunks, block), bf16)] * 2
-        high, low = call(
-            functools.partial(early, range(len(near)), unit, chunk),
-            terms,
-            [],
-            where, *near,
-        )
+        terms = [pltpu.VMEM((rows // chunks, block), bf16)] * 2
+        high, low = call(functools.partial(early, range(len(near)), unit, chunk), terms, [], *near)
         piece, high, low = call(
             functools.partial(solve, sources, tuple(range(len(near), n_cols)), unit, chunk),
-            [jax.ShapeDtypeStruct((rows // chunks, cols), f32)] + terms,
+            [pltpu.VMEM((rows // chunks, cols), f32)] + terms,
             [],
-            where, top, high, low, *far[chunk],
+            top, high, low, *far[chunk],
         )
         solved.append(piece)
         split += [high, low]
@@ -187,7 +183,7 @@
         functools.partial(update, sources, masks, chunks, n_cols),
         jax.ShapeDtypeStruct((rows, cols), f32),
         [pltpu.VMEM((block, cols), f32)],
-        where, own, *solved, *split, *got,
+        own, *solved, *split, *got,
     )
 
 

time: 67.2 us -> 50.8 us (0.76)
  Pallas kernels: 16.2 us -> 2.84 us
  local copies, waits for them, and re-layouts: 5.58 us -> 1.06 us
  waiting for transfers between devices: 22.2 us -> 24.4 us
    pallas_call x6, Pallas kernels: 16.2 us -> 2.84 us  [call(): pl.pallas_call(kernel, out_shape=out_shape, in_specs=[VMEM] * len(args),...]
    unnamed x42 -> x6, local copies, waits for them, and re-layouts: 3.51 us -> 0.01 us
    ppermute x18, waiting for transfers between devices: 22.2 us -> 24.4 us  [swap(): lax.ppermute(block, axis, [(i, i ^ mask) for i in range(lax.axis_size(axi...]
    reshape x1 -> x0, local copies, waits for them, and re-layouts: 1.03 us -> none  [per_device(): pivots.reshape(block, 1)]
  transfers between devices with their start and end apart: 18 -> 18, of which waited for: 5 -> 6; matrix products, arithmetic and copies ran while one was open for 2% -> 0% of each run, Pallas kernels for 20% -> 4%
where the time goes in v1:
time: 50.8 us; the launch traced here: 50.6 us
  waiting for transfers between devices  24.4 us (48%)
  starting transfers between devices  22.2 us (44%)
  Pallas kernels  2.84 us (6%)
  local copies, waits for them, and re-layouts  1.06 us (2%)
    ppermute x18, waiting for transfers between devices, swap(): lax.ppermute(block, axis, [(i, i ^ mask) for i in range(lax.axis_size(axi...  24.4 us
    ppermute x18, starting transfers between devices, swap(): lax.ppermute(block, axis, [(i, i ^ mask) for i in range(lax.axis_size(axi...  22.2 us
    pallas_call x6, Pallas kernels, call(): pl.pallas_call(kernel, out_shape=out_shape, in_specs=[VMEM] * len(args),...  2.84 us
    slice x1, local copies, waits for them, and re-layouts, per_device(): part = panel[chunk * unit:(chunk + 1) * unit]  1.04 us
  transfers between devices with their start and end apart: 18, of which 6 were waited for; matrix products, arithmetic and copies ran while one was open for 0% of the time, Pallas kernels for 4%

profile of v1, /device:TPU:0, one launch (start us, length us, event | category | flops | bytes accessed | tf_op | source)
XLA Modules:
  0.0 50.6 jit_solution(9652077358705500066)
XLA Ops:
  0.0 0.0 copy-start
  0.0 1.0 %fusion = (f32[32,1024]{1,0:T(8,128)S(1)}, f32[32,1024]{1,0:T(8,128)S(1)}) fusion(f32[64,1024]{1,0:T(8,128)} %refs_0_.5), kind=kLoop, calls=%fused_computation | loop fusion | bytes 524288 | tf_op jit(solution)/shard_map/slice | solution.py:155
  1.1 0.0 copy-start.2
  1.1 4.1 %collective-permute-start.6 = (f32[32,1024]{1,0:T(8,128)S(1)}, f32[32,1024]{1,0:T(8,128)S(1)}, u32[]{:S(2)}, u32[]{:S(2)}) collective-permute-start(f32[32,1024]{1,0:T(8,128)S(1)} %get-tuple-element.30), channel_id=1, source_target_pairs={{0,4},{1,5},{2,6},{3,7},{4,0},{5,1},{6,2},{7,3},{8,12},{9,13},{10,... | collective-permute-start | bytes 393224 | tf_op jit(solution)/shard_map/ppermute | solution.py:15
  5.2 0.0 copy-done
  5.2 1.6 %collective-permute-start.4 = (f32[64,1024]{1,0:T(8,128)S(1)}, f32[64,1024]{1,0:T(8,128)S(1)}, u32[]{:S(2)}, u32[]{:S(2)}) collective-permute-start(f32[64,1024]{1,0:T(8,128)S(1)} %copy-done), channel_id=1, source_target_pairs={{0,2},{1,3},{2,0},{3,1},{4,6},{5,7},{6,4},{7,5},{8,10},{9,11},{10,... | collective-permute-start | bytes 786440 | tf_op jit(solution)/shard_map/ppermute | solution.py:15
  6.8 0.0 collective-permute-start.8
  6.8 1.9 %collective-permute-start.10 = (f32[32,1024]{1,0:T(8,128)S(1)}, f32[32,1024]{1,0:T(8,128)S(1)}, u32[]{:S(2)}, u32[]{:S(2)}) collective-permute-start(f32[32,1024]{1,0:T(8,128)S(1)} %get-tuple-element.29), channel_id=1, source_target_pairs={{0,4},{1,5},{2,6},{3,7},{4,0},{5,1},{6,2},{7,3},{8,12},{9,13},{10,... | collective-permute-start | bytes 393224 | tf_op jit(solution)/shard_map/ppermute | solution.py:15
  8.7 1.9 %collective-permute-start.12 = (f32[32,1024]{1,0:T(8,128)S(1)}, f32[32,1024]{1,0:T(8,128)S(1)}, u32[]{:S(2)}, u32[]{:S(2)}) collective-permute-start(f32[32,1024]{1,0:T(8,128)S(1)} %get-tuple-element.29), channel_id=1, source_target_pairs={{0,6},{1,7},{2,4},{3,5},{4,2},{5,3},{6,0},{7,1},{8,14},{9,15},{10,... | collective-permute-start | bytes 393224 | tf_op jit(solution)/shard_map/ppermute | solution.py:15
  10.6 1.8 %collective-permute-done.6.refs_0_ = f32[32,1024]{1,0:T(8,128)S(1)} collective-permute-done((f32[32,1024]{1,0:T(8,128)S(1)}, f32[32,1024]{1,0:T(8,128)S(1)}, u32[]{:S(2)}, u32[]{:S(2)}) %collective-permute-start.6) | collective-permute-done | bytes 131104 | tf_op jit(solution)/shard_map/ppermute | solution.py:15
  12.4 0.0 copy-done.1
  12.4 1.8 %collective-permute-start = (f32[512,128]{1,0:T(8,128)S(1)}, f32[512,128]{1,0:T(8,128)S(1)}, u32[]{:S(2)}, u32[]{:S(2)}) collective-permute-start(f32[512,128]{1,0:T(8,128)S(1)} %copy-done.1), channel_id=1, source_target_pairs={{0,8},{8,0},{16,24},{24,16},{1,9},{9,1},{17,25},{25,17},{2,10},{10... | collective-permute-start | bytes 786440 | tf_op jit(solution)/shard_map/ppermute | solution.py:15
  14.2 5.3 %collective-permute-done.8.refs_2_ = f32[32,1024]{1,0:T(8,128)S(1)} collective-permute-done((f32[32,1024]{1,0:T(8,128)S(1)}, f32[32,1024]{1,0:T(8,128)S(1)}, u32[]{:S(2)}, u32[]{:S(2)}) %collective-permute-start.8) | collective-permute-done | bytes 131104 | tf_op jit(solution)/shard_map/ppermute | solution.py:15
  19.4 1.5 %collective-permute-start.1 = (f32[512,128]{1,0:T(8,128)S(1)}, f32[512,128]{1,0:T(8,128)S(1)}, u32[]{:S(2)}, u32[]{:S(2)}) collective-permute-start(f32[512,128]{1,0:T(8,128)S(1)} %copy-done.1), channel_id=1, source_target_pairs={{0,16},{8,24},{16,0},{24,8},{1,17},{9,25},{17,1},{25,9},{2,18},{10... | collective-permute-start | bytes 786440 | tf_op jit(solution)/shard_map/ppermute | solution.py:15
  20.9 5.5 %collective-permute-done.10.refs_0_ = f32[32,1024]{1,0:T(8,128)S(1)} collective-permute-done((f32[32,1024]{1,0:T(8,128)S(1)}, f32[32,1024]{1,0:T(8,128)S(1)}, u32[]{:S(2)}, u32[]{:S(2)}) %collective-permute-start.10) | collective-permute-done | bytes 131104 | tf_op jit(solution)/shard_map/ppermute | solution.py:15
  26.4 2.8 %collective-permute-start.2 = (f32[512,128]{1,0:T(8,128)S(1)}, f32[512,128]{1,0:T(8,128)S(1)}, u32[]{:S(2)}, u32[]{:S(2)}) collective-permute-start(f32[512,128]{1,0:T(8,128)S(1)} %copy-done.1), channel_id=1, source_target_pairs={{0,24},{8,16},{16,8},{24,0},{1,25},{9,17},{17,9},{25,1},{2,26},{10... | collective-permute-start | bytes 786440 | tf_op jit(solution)/shard_map/ppermute | solution.py:15
  29.1 0.0 collective-permute-done.12.refs_2_
  29.2 0.0 collective-permute-start.3
  29.2 0.0 collective-permute-done.4.refs_2_
  29.2 0.5 collective-permute-start.5
  29.7 0.0 collective-permute-done.refs_1_
  29.7 0.1 collective-permute-start.7
  29.7 0.0 collective-permute-done.1.refs_2_
  29.7 0.4 collective-permute-start.9
  30.2 3.7 %collective-permute-done.2.refs_3_ = f32[512,128]{1,0:T(8,128)S(1)} collective-permute-done((f32[512,128]{1,0:T(8,128)S(1)}, f32[512,128]{1,0:T(8,128)S(1)}, u32[]{:S(2)}, u32[]{:S(2)}) %collective-permute-start.2) | collective-permute-done | bytes 262176 | tf_op jit(solution)/shard_map/ppermute | solution.py:15
  33.9 0.0 collective-permute-start.11
  33.9 0.0 collective-permute-done.3.refs_1_
  33.9 0.5 %collective-permute-start.13 = (f32[32,1024]{1,0:T(8,128)S(1)}, f32[32,1024]{1,0:T(8,128)S(1)}, u32[]{:S(2)}, u32[]{:S(2)}) collective-permute-start(f32[32,1024]{1,0:T(8,128)S(1)} %collective-permute-done.12.refs_2_), channel_id=1, source_target_pairs={{0,1},{1,0},{2,3},{3,2},{4,5},{5,4},{6,7},{7,6},{8,9},{9,8},{10,11... | collective-permute-start | bytes 393224 | tf_op jit(solution)/shard_map/ppermute | solution.py:15
  34.4 0.0 copy-done.2
  34.4 0.9 %shard_map.37 = (bf16[1024,256]{1,0:T(8,128)(2,1)S(1)}, f32[512,128]{1,0:T(8,128)S(1)}) custom-call(s32[1,1024]{1,0:T(1,128)S(1)} %bitcast.1, f32[512,128]{1,0:T(8,128)S(1)} %copy-done.1, f32[512,128]{1,0:T(8,128)S(1)} %collective-permute-done.refs_1_, f32[512,128]{1,0:T(8,128)S(1)} %collective-permute-done.1.refs_2_, ...), custom_call_target="tpu_custom_call" | custom-call | tf_op jit(solution)/shard_map/pallas_call | solution.py:19
  35.3 0.0 collective-permute-done.5.refs_3_
  35.3 0.1 shard_map.38
  35.4 0.0 collective-permute-done.7.refs_1_
  35.4 0.0 collective-permute-done.9.refs_3_
  35.4 0.5 %shard_map.39 = (f32[256,128]{1,0:T(8,128)S(1)}, bf16[256,1024]{1,0:T(8,128)(2,1)S(1)}, bf16[256,1024]{1,0:T(8,128)(2,1)S(1)}) custom-call(bf16[1024,256]{1,0:T(8,128)(2,1)S(1)} %get-tuple-element.18.top_ref, bf16[256,1024]{1,0:T(8,128)(2,1)S(1)} %get-tuple-element.19.early_high, bf16[256,1024]{1,0:T(8,128)(2,1)S(1)} %get-tuple-element.20.early_low, ...), custom_call_target="tpu_custom_call" | custom-call | tf_op jit(solution)/shard_map/pallas_call | solution.py:19
  36.0 1.2 %collective-permute-start.14 = (f32[256,128]{1,0:T(8,128)S(1)}, f32[256,128]{1,0:T(8,128)S(1)}, u32[]{:S(2)}, u32[]{:S(2)}) collective-permute-start(f32[256,128]{1,0:T(8,128)S(1)} %get-tuple-element.21.refs_0_), channel_id=1, source_target_pairs={{0,16},{8,24},{16,0},{24,8},{1,17},{9,25},{17,1},{25,9},{2,18},{10... | collective-permute-start | bytes 393224 | tf_op jit(solution)/shard_map/ppermute | solution.py:15
  37.2 1.9 %collective-permute-start.15 = (f32[256,128]{1,0:T(8,128)S(1)}, f32[256,128]{1,0:T(8,128)S(1)}, u32[]{:S(2)}, u32[]{:S(2)}) collective-permute-start(f32[256,128]{1,0:T(8,128)S(1)} %get-tuple-element.21.refs_0_), channel_id=1, source_target_pairs={{0,24},{8,16},{16,8},{24,0},{1,25},{9,17},{17,9},{25,1},{2,26},{10... | collective-permute-start | bytes 393224 | tf_op jit(solution)/shard_map/ppermute | solution.py:15
  39.1 0.1 shard_map.40
  39.1 0.0 collective-permute-done.11.refs_1_
  39.1 0.0 collective-permute-done.13.refs_3_
  39.2 0.5 %shard_map.41 = (f32[256,128]{1,0:T(8,128)S(1)}, bf16[256,1024]{1,0:T(8,128)(2,1)S(1)}, bf16[256,1024]{1,0:T(8,128)(2,1)S(1)}) custom-call(bf16[1024,256]{1,0:T(8,128)(2,1)S(1)} %get-tuple-element.18.top_ref, bf16[256,1024]{1,0:T(8,128)(2,1)S(1)} %get-tuple-element.22.early_high, bf16[256,1024]{1,0:T(8,128)(2,1)S(1)} %get-tuple-element.23.early_low, ...), custom_call_target="tpu_custom_call" | custom-call | tf_op jit(solution)/shard_map/pallas_call | solution.py:19
  39.7 0.7 %collective-permute-start.16 = (f32[256,128]{1,0:T(8,128)S(1)}, f32[256,128]{1,0:T(8,128)S(1)}, u32[]{:S(2)}, u32[]{:S(2)}) collective-permute-start(f32[256,128]{1,0:T(8,128)S(1)} %get-tuple-element.24.refs_1_), channel_id=1, source_target_pairs={{0,16},{8,24},{16,0},{24,8},{1,17},{9,25},{17,1},{25,9},{2,18},{10... | collective-permute-start | bytes 393224 | tf_op jit(solution)/shard_map/ppermute | solution.py:15
  40.4 1.3 %collective-permute-start.17 = (f32[256,128]{1,0:T(8,128)S(1)}, f32[256,128]{1,0:T(8,128)S(1)}, u32[]{:S(2)}, u32[]{:S(2)}) collective-permute-start(f32[256,128]{1,0:T(8,128)S(1)} %get-tuple-element.24.refs_1_), channel_id=1, source_target_pairs={{0,24},{8,16},{16,8},{24,0},{1,25},{9,17},{17,9},{25,1},{2,26},{10... | collective-permute-start | bytes 393224 | tf_op jit(solution)/shard_map/ppermute | solution.py:15
  41.7 6.3 %collective-permute-done.14.refs_6_ = f32[256,128]{1,0:T(8,128)S(1)} collective-permute-done((f32[256,128]{1,0:T(8,128)S(1)}, f32[256,128]{1,0:T(8,128)S(1)}, u32[]{:S(2)}, u32[]{:S(2)}) %collective-permute-start.14) | collective-permute-done | bytes 131104 | tf_op jit(solution)/shard_map/ppermute | solution.py:15
  48.0 0.0 collective-permute-done.15.refs_7_
  48.0 1.8 %collective-permute-done.16.refs_8_ = f32[256,128]{1,0:T(8,128)S(1)} collective-permute-done((f32[256,128]{1,0:T(8,128)S(1)}, f32[256,128]{1,0:T(8,128)S(1)}, u32[]{:S(2)}, u32[]{:S(2)}) %collective-permute-start.16) | collective-permute-done | bytes 131104 | tf_op jit(solution)/shard_map/ppermute | solution.py:15
  49.9 0.0 collective-permute-done.17.refs_9_
  49.9 0.7 %shard_map.42 = f32[512,128]{1,0:T(8,128)} custom-call(f32[512,128]{1,0:T(8,128)S(1)} %get-tuple-element.17.own_ref, f32[256,128]{1,0:T(8,128)S(1)} %get-tuple-element.21.refs_0_, f32[256,128]{1,0:T(8,128)S(1)} %get-tuple-element.24.refs_1_, bf16[256,1024]{1,0:T(8,128)(2,1)S(1)} %get-tuple-element.25.refs_2_, ...), custom_call_target="tpu_custom_call" | custom-call | tf_op jit(solution)/shard_map/pallas_call | solution.py:19
  (1 shorter events, 0.0 us)
Async XLA Ops:
  0.0 5.2 %copy-start = (f32[64,1024]{1,0:T(8,128)S(1)}, f32[64,1024]{1,0:T(8,128)}, u32[]{:S(2)}) copy-start(f32[64,1024]{1,0:T(8,128)} %refs_0_.5) | copy-start | bytes 786436
  0.0 12.4 %copy-start.1 = (f32[512,128]{1,0:T(8,128)S(1)}, f32[512,128]{1,0:T(8,128)}, u32[]{:S(2)}) copy-start(f32[512,128]{1,0:T(8,128)} %refs_0_.3) | copy-start | bytes 786436
  1.1 33.4 %copy-start.2 = (s32[1024]{0:T(1024)S(1)}, s32[1024]{0:T(1024)}, u32[]{:S(2)}) copy-start(s32[1024]{0:T(1024)} %param.5) | copy-start | bytes 12292
  1.1 11.3 %collective-permute-start.6 = (f32[32,1024]{1,0:T(8,128)S(1)}, f32[32,1024]{1,0:T(8,128)S(1)}, u32[]{:S(2)}, u32[]{:S(2)}) collective-permute-start(f32[32,1024]{1,0:T(8,128)S(1)} %get-tuple-element.30), channel_id=1, source_target_pairs={{0,4},{1,5},{2,6},{3,7},{4,0},{5,1},{6,2},{7,3},{8,12},{9,13},{10,... | collective-permute-start | bytes 393224 | tf_op jit(solution)/shard_map/ppermute | solution.py:15
  5.2 24.0 %collective-permute-start.4 = (f32[64,1024]{1,0:T(8,128)S(1)}, f32[64,1024]{1,0:T(8,128)S(1)}, u32[]{:S(2)}, u32[]{:S(2)}) collective-permute-start(f32[64,1024]{1,0:T(8,128)S(1)} %copy-done), channel_id=1, source_target_pairs={{0,2},{1,3},{2,0},{3,1},{4,6},{5,7},{6,4},{7,5},{8,10},{9,11},{10,... | collective-permute-start | bytes 786440 | tf_op jit(solution)/shard_map/ppermute | solution.py:15
  6.8 12.6 %collective-permute-start.8 = (f32[32,1024]{1,0:T(8,128)S(1)}, f32[32,1024]{1,0:T(8,128)S(1)}, u32[]{:S(2)}, u32[]{:S(2)}) collective-permute-start(f32[32,1024]{1,0:T(8,128)S(1)} %get-tuple-element.30), channel_id=1, source_target_pairs={{0,6},{1,7},{2,4},{3,5},{4,2},{5,3},{6,0},{7,1},{8,14},{9,15},{10,... | collective-permute-start | bytes 393224 | tf_op jit(solution)/shard_map/ppermute | solution.py:15
  6.8 19.6 %collective-permute-start.10 = (f32[32,1024]{1,0:T(8,128)S(1)}, f32[32,1024]{1,0:T(8,128)S(1)}, u32[]{:S(2)}, u32[]{:S(2)}) collective-permute-start(f32[32,1024]{1,0:T(8,128)S(1)} %get-tuple-element.29), channel_id=1, source_target_pairs={{0,4},{1,5},{2,6},{3,7},{4,0},{5,1},{6,2},{7,3},{8,12},{9,13},{10,... | collective-permute-start | bytes 393224 | tf_op jit(solution)/shard_map/ppermute | solution.py:15
  8.7 20.5 %collective-permute-start.12 = (f32[32,1024]{1,0:T(8,128)S(1)}, f32[32,1024]{1,0:T(8,128)S(1)}, u32[]{:S(2)}, u32[]{:S(2)}) collective-permute-start(f32[32,1024]{1,0:T(8,128)S(1)} %get-tuple-element.29), channel_id=1, source_target_pairs={{0,6},{1,7},{2,4},{3,5},{4,2},{5,3},{6,0},{7,1},{8,14},{9,15},{10,... | collective-permute-start | bytes 393224 | tf_op jit(solution)/shard_map/ppermute | solution.py:15
  12.4 17.3 %collective-permute-start = (f32[512,128]{1,0:T(8,128)S(1)}, f32[512,128]{1,0:T(8,128)S(1)}, u32[]{:S(2)}, u32[]{:S(2)}) collective-permute-start(f32[512,128]{1,0:T(8,128)S(1)} %copy-done.1), channel_id=1, source_target_pairs={{0,8},{8,0},{16,24},{24,16},{1,9},{9,1},{17,25},{25,17},{2,10},{10... | collective-permute-start | bytes 786440 | tf_op jit(solution)/shard_map/ppermute | solution.py:15
  19.4 10.3 %collective-permute-start.1 = (f32[512,128]{1,0:T(8,128)S(1)}, f32[512,128]{1,0:T(8,128)S(1)}, u32[]{:S(2)}, u32[]{:S(2)}) collective-permute-start(f32[512,128]{1,0:T(8,128)S(1)} %copy-done.1), channel_id=1, source_target_pairs={{0,16},{8,24},{16,0},{24,8},{1,17},{9,25},{17,1},{25,9},{2,18},{10... | collective-permute-start | bytes 786440 | tf_op jit(solution)/shard_map/ppermute | solution.py:15
  26.4 7.5 %collective-permute-start.2 = (f32[512,128]{1,0:T(8,128)S(1)}, f32[512,128]{1,0:T(8,128)S(1)}, u32[]{:S(2)}, u32[]{:S(2)}) collective-permute-start(f32[512,128]{1,0:T(8,128)S(1)} %copy-done.1), channel_id=1, source_target_pairs={{0,24},{8,16},{16,8},{24,0},{1,25},{9,17},{17,9},{25,1},{2,26},{10... | collective-permute-start | bytes 786440 | tf_op jit(solution)/shard_map/ppermute | solution.py:15
  29.2 4.8 %collective-permute-start.3 = (f32[64,1024]{1,0:T(8,128)S(1)}, f32[64,1024]{1,0:T(8,128)S(1)}, u32[]{:S(2)}, u32[]{:S(2)}) collective-permute-start(f32[64,1024]{1,0:T(8,128)S(1)} %copy-done), channel_id=1, source_target_pairs={{0,1},{1,0},{2,3},{3,2},{4,5},{5,4},{6,7},{7,6},{8,9},{9,8},{10,11... | collective-permute-start | bytes 786440 | tf_op jit(solution)/shard_map/ppermute | solution.py:15
  29.2 6.2 %collective-permute-start.5 = (f32[64,1024]{1,0:T(8,128)S(1)}, f32[64,1024]{1,0:T(8,128)S(1)}, u32[]{:S(2)}, u32[]{:S(2)}) collective-permute-start(f32[64,1024]{1,0:T(8,128)S(1)} %collective-permute-done.4.refs_2_), channel_id=1, source_target_pairs={{0,1},{1,0},{2,3},{3,2},{4,5},{5,4},{6,7},{7,6},{8,9},{9,8},{10,11... | collective-permute-start | bytes 786440 | tf_op jit(solution)/shard_map/ppermute | solution.py:15
  29.7 5.7 %collective-permute-start.7 = (f32[32,1024]{1,0:T(8,128)S(1)}, f32[32,1024]{1,0:T(8,128)S(1)}, u32[]{:S(2)}, u32[]{:S(2)}) collective-permute-start(f32[32,1024]{1,0:T(8,128)S(1)} %collective-permute-done.6.refs_0_), channel_id=1, source_target_pairs={{0,1},{1,0},{2,3},{3,2},{4,5},{5,4},{6,7},{7,6},{8,9},{9,8},{10,11... | collective-permute-start | bytes 393224 | tf_op jit(solution)/shard_map/ppermute | solution.py:15
  29.7 5.7 %collective-permute-start.9 = (f32[32,1024]{1,0:T(8,128)S(1)}, f32[32,1024]{1,0:T(8,128)S(1)}, u32[]{:S(2)}, u32[]{:S(2)}) collective-permute-start(f32[32,1024]{1,0:T(8,128)S(1)} %collective-permute-done.8.refs_2_), channel_id=1, source_target_pairs={{0,1},{1,0},{2,3},{3,2},{4,5},{5,4},{6,7},{7,6},{8,9},{9,8},{10,11... | collective-permute-start | bytes 393224 | tf_op jit(solution)/shard_map/ppermute | solution.py:15
  33.9 5.2 %collective-permute-start.11 = (f32[32,1024]{1,0:T(8,128)S(1)}, f32[32,1024]{1,0:T(8,128)S(1)}, u32[]{:S(2)}, u32[]{:S(2)}) collective-permute-start(f32[32,1024]{1,0:T(8,128)S(1)} %collective-permute-done.10.refs_0_), channel_id=1, source_target_pairs={{0,1},{1,0},{2,3},{3,2},{4,5},{5,4},{6,7},{7,6},{8,9},{9,8},{10,11... | collective-permute-start | bytes 393224 | tf_op jit(solution)/shard_map/ppermute | solution.py:15
  33.9 5.2 %collective-permute-start.13 = (f32[32,1024]{1,0:T(8,128)S(1)}, f32[32,1024]{1,0:T(8,128)S(1)}, u32[]{:S(2)}, u32[]{:S(2)}) collective-permute-start(f32[32,1024]{1,0:T(8,128)S(1)} %collective-permute-done.12.refs_2_), channel_id=1, source_target_pairs={{0,1},{1,0},{2,3},{3,2},{4,5},{5,4},{6,7},{7,6},{8,9},{9,8},{10,11... | collective-permute-start | bytes 393224 | tf_op jit(solution)/shard_map/ppermute | solution.py:15
  36.0 12.1 %collective-permute-start.14 = (f32[256,128]{1,0:T(8,128)S(1)}, f32[256,128]{1,0:T(8,128)S(1)}, u32[]{:S(2)}, u32[]{:S(2)}) collective-permute-start(f32[256,128]{1,0:T(8,128)S(1)} %get-tuple-element.21.refs_0_), channel_id=1, source_target_pairs={{0,16},{8,24},{16,0},{24,8},{1,17},{9,25},{17,1},{25,9},{2,18},{10... | collective-permute-start | bytes 393224 | tf_op jit(solution)/shard_map/ppermute | solution.py:15
  37.2 10.9 %collective-permute-start.15 = (f32[256,128]{1,0:T(8,128)S(1)}, f32[256,128]{1,0:T(8,128)S(1)}, u32[]{:S(2)}, u32[]{:S(2)}) collective-permute-start(f32[256,128]{1,0:T(8,128)S(1)} %get-tuple-element.21.refs_0_), channel_id=1, source_target_pairs={{0,24},{8,16},{16,8},{24,0},{1,25},{9,17},{17,9},{25,1},{2,26},{10... | collective-permute-start | bytes 393224 | tf_op jit(solution)/shard_map/ppermute | solution.py:15
  39.7 10.2 %collective-permute-start.16 = (f32[256,128]{1,0:T(8,128)S(1)}, f32[256,128]{1,0:T(8,128)S(1)}, u32[]{:S(2)}, u32[]{:S(2)}) collective-permute-start(f32[256,128]{1,0:T(8,128)S(1)} %get-tuple-element.24.refs_1_), channel_id=1, source_target_pairs={{0,16},{8,24},{16,0},{24,8},{1,17},{9,25},{17,1},{25,9},{2,18},{10... | collective-permute-start | bytes 393224 | tf_op jit(solution)/shard_map/ppermute | solution.py:15
  40.4 9.5 %collective-permute-start.17 = (f32[256,128]{1,0:T(8,128)S(1)}, f32[256,128]{1,0:T(8,128)S(1)}, u32[]{:S(2)}, u32[]{:S(2)}) collective-permute-start(f32[256,128]{1,0:T(8,128)S(1)} %get-tuple-element.24.refs_1_), channel_id=1, source_target_pairs={{0,24},{8,16},{16,8},{24,0},{1,25},{9,17},{17,9},{25,1},{2,26},{10... | collective-permute-start | bytes 393224 | tf_op jit(solution)/shard_map/ppermute | solution.py:15

commit v2 on v1

--- a/solution.py
+++ b/solution.py
@@ -11,8 +11,9 @@
 VMEM = pl.BlockSpec(memory_space=pltpu.VMEM)
 
 
-def swap(block, axis, mask):
-    return lax.ppermute(block, axis, [(i, i ^ mask) for i in range(lax.axis_size(axis))])
+def swap(block, axis, mask, among=None):
+    ids = range(lax.axis_size(axis)) if among is None else (among, among ^ mask)
+    return lax.ppermute(block, axis, [(i, i ^ mask) for i in ids])
 
 
 def call(kernel, out_shape, scratch, *args):
@@ -39,6 +40,19 @@
     cols = pair.shape[1] // 2
     both = dot(high, pair)
     return both[:, :cols] + (both[:, cols:] + dot(low, pair[:, :cols]))
+
+
+def halve(rows, panel_ref, first_ref, rest_ref, whole_ref):
+    unit = first_ref.shape[0]
+    first_ref[...] = panel_ref[pl.ds(0, unit), :]
+
+    @pl.when(lax.axis_index("prow") == 0)
+    def _():
+        first_ref[:, pl.ds(rows, rows)] = panel_ref[pl.ds(unit, unit), pl.ds(0, rows)]
+
+    rest_ref[...] = panel_ref[pl.ds(unit, unit), :]
+    whole_ref[pl.ds(0, unit), :] = first_ref[...]
+    whole_ref[pl.ds(unit, unit), :] = rest_ref[...]
 
 
 def prepare(n_rows, sources, piv_row, *refs):
@@ -90,20 +104,36 @@
     collect(order, unit, chunk, lax.axis_index("pcol"), pieces, high, low)
 
 
-def solve(sources, order, unit, chunk, top_ref, early_high, early_low, *refs):
-    *pieces, out_ref, high, low = refs
+def solve(fold, order, unit, chunk, top_ref, early_high, early_low, *refs):
+    pieces, outs = refs[: len(order)], refs[len(order) :]
+    *solved, high, low = outs
+    me = lax.axis_index("pcol")
     for mask in range(order[0]):
-        at = pl.ds(pl.multiple_of((lax.axis_index("pcol") ^ mask) * unit, unit), unit)
+        at = pl.ds(pl.multiple_of((me ^ mask) * unit, unit), unit)
         high[at, :], low[at, :] = early_high[at, :], early_low[at, :]
-    collect(order, unit, chunk, lax.axis_index("pcol"), pieces, high, low)
-
-    @pl.when(lax.axis_index("prow") < sources)
-    def _():
-        out_ref[...] = product(high[...], low[...], top_ref[...])
-
-
-def update(sources, masks, chunks, n_cols, own_ref, *refs):
-    solved, refs = refs[:chunks], refs[chunks:]
+    collect(order, unit, chunk, me, pieces, high, low)
+    sources = top_ref.shape[0] // (high.shape[0] * (2 if fold else 1))
+    row = lax.axis_index("prow")
+    first = 1 if fold else 0
+
+    @pl.when((row >= first) & (row < sources))
+    def _():
+        solved[0][...] = product(high[...], low[...], top_ref[...])
+
+    if fold and chunk == 0:
+        half = top_ref.shape[0] // 2
+
+        @pl.when(row == 0)
+        def _():
+            for i, out in enumerate(solved):
+                at = pl.ds(i * half, half)
+                out[...] = product(high[:, at], low[:, at], top_ref[pl.ds(0, half), :])
+
+
+def update(sources, masks, fold, n_cols, own_ref, *refs):
+    chunks = 2 if fold else 1
+    count = 3 if fold else 1
+    solved, refs = refs[:count], refs[count:]
     split, refs = refs[: 2 * chunks], refs[2 * chunks :]
     *got, out_ref, upper = refs
     rows, _ = own_ref.shape
@@ -111,11 +141,22 @@
     unit = depth // chunks
     me = lax.axis_index("prow")
 
+    def place(dest, base, chunk, ref):
+        for i in range(n_cols):
+            at = base + (i * depth + chunk * unit)
+            at = at if isinstance(at, int) else pl.multiple_of(at, unit)
+            dest[pl.ds(at, unit), :] = ref[pl.ds(i * unit, unit), :]
+
     @pl.when(me < sources)
     def _():
-        for chunk in range(chunks):
-            for i in range(n_cols):
-                out_ref[pl.ds(i * depth + chunk * unit, unit), :] = solved[chunk][pl.ds(i * unit, unit), :]
+        place(out_ref, 0, 0, solved[0])
+
+    if fold:
+        for source in range(sources):
+
+            @pl.when(me == source)
+            def _():
+                place(out_ref, 0, 1, solved[1 + source])
 
     @pl.when(me >= sources)
     def _():
@@ -124,11 +165,14 @@
 
             @pl.when(source < sources)
             def _():
-                for chunk in range(chunks):
-                    ref = got[chunk * len(masks) + m]
-                    for i in range(n_cols):
-                        at = pl.multiple_of(source * rows, rows) + (i * depth + chunk * unit)
-                        upper[pl.ds(pl.multiple_of(at, unit), unit), :] = ref[pl.ds(i * unit, unit), :]
+                place(upper, pl.multiple_of(source * rows, rows), 0, got[m])
+
+            if fold:
+                for s in range(sources):
+
+                    @pl.when(source == s)
+                    def _():
+                        place(upper, s * rows, 1, got[len(masks) * (1 + s) + m])
 
         pair = jnp.concatenate(halves(upper[...]), axis=1)
         for chunk in range(chunks):
@@ -144,17 +188,27 @@
     depth = panel.shape[0]
     n_rows, n_cols = lax.axis_size("prow"), lax.axis_size("pcol")
     sources = block // rows
-    chunks = 2 if depth % 32 == 0 else 1
+    fold = sources == 2 and depth % 32 == 0
+    chunks = 2 if fold else 1
     unit = depth // chunks
     f32, bf16 = jnp.float32, jnp.bfloat16
 
+    if fold:
+        *parts, panel = call(
+            functools.partial(halve, rows),
+            [pltpu.VMEM((unit, block), f32)] * 2 + [pltpu.VMEM((depth, block), f32)],
+            [],
+            panel,
+        )
+    else:
+        parts = [panel]
+
+    far = []
+    for chunk in range(chunks):
+        got = [swap(parts[chunk], "pcol", mask) for mask in range(4, n_cols, 2)]
+        far.append([piece for block_ in got for piece in (block_, swap(block_, "pcol", 1))])
     near = [panel, swap(panel, "pcol", 2)]
     near = [piece for block_ in near for piece in (block_, swap(block_, "pcol", 1))]
-    far = []
-    for chunk in range(chunks):
-        part = panel[chunk * unit : (chunk + 1) * unit]
-        got = [swap(part, "pcol", mask) for mask in range(4, n_cols, 2)]
-        far.append([piece for block_ in got for piece in (block_, swap(block_, "pcol", 1))])
     blocks = [matrix] + [swap(matrix, "prow", mask) for mask in range(1, n_rows)]
 
     top, own = call(
@@ -169,18 +223,21 @@
     for chunk in range(chunks):
         terms = [pltpu.VMEM((rows // chunks, block), bf16)] * 2
         high, low = call(functools.partial(early, range(len(near)), unit, chunk), terms, [], *near)
-        piece, high, low = call(
-            functools.partial(solve, sources, tuple(range(len(near), n_cols)), unit, chunk),
-            [pltpu.VMEM((rows // chunks, cols), f32)] + terms,
+        count = 2 if fold and chunk == 0 else 1
+        *pieces, high, low = call(
+            functools.partial(solve, fold, tuple(range(len(near), n_cols)), unit, chunk),
+            [pltpu.VMEM((rows // chunks, cols), f32)] * count + terms,
             [],
             top, high, low, *far[chunk],
         )
-        solved.append(piece)
+        solved += pieces
         split += [high, low]
-        got += [swap(piece, "prow", mask) for mask in masks]
+    got = [swap(solved[0], "prow", mask) for mask in masks]
+    for source, piece in enumerate(solved[1:]):
+        got += [swap(piece, "prow", mask, source) for mask in masks]
 
     return call(
-        functools.partial(update, sources, masks, chunks, n_cols),
+        functools.partial(update, sources, masks, fold, n_cols),
         jax.ShapeDtypeStruct((rows, cols), f32),
         [pltpu.VMEM((block, cols), f32)],
         own, *solved, *split, *got,

time: 50.8 us -> 51.2 us (level)
  the two profiles are of different devices: /device:TPU:0 before, /device:TPU:10 now
where the time goes in v2:
time: 51.2 us; the launch traced here: 50.9 us
  starting transfers between devices  26.7 us (52%)
  waiting for transfers between devices  20.2 us (39%)
  Pallas kernels  2.88 us (6%)
  local copies, waits for them, and re-layouts  0.96 us (2%)
    ppermute x20, starting transfers between devices, swap(): return lax.ppermute(block, axis, [(i, i ^ mask) for i in ids])  26.7 us
    ppermute x20, waiting for transfers between devices, swap(): return lax.ppermute(block, axis, [(i, i ^ mask) for i in ids])  20.2 us
    pallas_call x7, Pallas kernels, call(): pl.pallas_call(kernel, out_shape=out_shape, in_specs=[VMEM] * len(args),...  2.88 us
  transfers between devices with their start and end apart: 20, of which 7 were waited for; matrix products, arithmetic and copies ran while one was open for 0% of the time, Pallas kernels for 4%

profile of v2, /device:TPU:10, one launch (start us, length us, event | category | flops | bytes accessed | tf_op | source)
XLA Modules:
  0.0 50.9 jit_solution(14979783818813043316)
XLA Ops:
  0.0 0.9 %copy-done = f32[64,1024]{1,0:T(8,128)S(1)} copy-done((f32[64,1024]{1,0:T(8,128)S(1)}, f32[64,1024]{1,0:T(8,128)}, u32[]{:S(2)}) %copy-start) | copy-done | bytes 262168
  1.0 0.0 copy-start.2
  1.0 2.7 %collective-permute-start.6 = (f32[32,1024]{1,0:T(8,128)S(1)}, f32[32,1024]{1,0:T(8,128)S(1)}, u32[]{:S(2)}, u32[]{:S(2)}) collective-permute-start(f32[32,1024]{1,0:T(8,128)S(1)} %get-tuple-element.26), channel_id=1, source_target_pairs={{0,4},{1,5},{2,6},{3,7},{4,0},{5,1},{6,2},{7,3},{8,12},{9,13},{10,... | collective-permute-start | bytes 393224 | tf_op jit(solution)/shard_map/ppermute | solution.py:16
  3.7 0.4 collective-permute-start.4
  4.1 0.5 collective-permute-start.8
  4.6 0.5 %collective-permute-start = (f32[512,128]{1,0:T(8,128)S(1)}, f32[512,128]{1,0:T(8,128)S(1)}, u32[]{:S(2)}, u32[]{:S(2)}) collective-permute-start(f32[512,128]{1,0:T(8,128)S(1)} %copy-done.1), channel_id=1, source_target_pairs={{0,8},{8,0},{16,24},{24,16},{1,9},{9,1},{17,25},{25,17},{2,10},{10... | collective-permute-start | bytes 786440 | tf_op jit(solution)/shard_map/ppermute | solution.py:16
  5.1 3.5 %collective-permute-start.10 = (f32[32,1024]{1,0:T(8,128)S(1)}, f32[32,1024]{1,0:T(8,128)S(1)}, u32[]{:S(2)}, u32[]{:S(2)}) collective-permute-start(f32[32,1024]{1,0:T(8,128)S(1)} %get-tuple-element.31), channel_id=1, source_target_pairs={{0,4},{1,5},{2,6},{3,7},{4,0},{5,1},{6,2},{7,3},{8,12},{9,13},{10,... | collective-permute-start | bytes 393224 | tf_op jit(solution)/shard_map/ppermute | solution.py:16
  8.6 0.7 %collective-permute-done.6.refs_0_ = f32[32,1024]{1,0:T(8,128)S(1)} collective-permute-done((f32[32,1024]{1,0:T(8,128)S(1)}, f32[32,1024]{1,0:T(8,128)S(1)}, u32[]{:S(2)}, u32[]{:S(2)}) %collective-permute-start.6) | collective-permute-done | bytes 131104 | tf_op jit(solution)/shard_map/ppermute | solution.py:16
  9.3 1.5 %collective-permute-start.1 = (f32[512,128]{1,0:T(8,128)S(1)}, f32[512,128]{1,0:T(8,128)S(1)}, u32[]{:S(2)}, u32[]{:S(2)}) collective-permute-start(f32[512,128]{1,0:T(8,128)S(1)} %copy-done.1), channel_id=1, source_target_pairs={{0,16},{8,24},{16,0},{24,8},{1,17},{9,25},{17,1},{25,9},{2,18},{10... | collective-permute-start | bytes 786440 | tf_op jit(solution)/shard_map/ppermute | solution.py:16
  10.8 3.2 %collective-permute-done.8.refs_2_ = f32[32,1024]{1,0:T(8,128)S(1)} collective-permute-done((f32[32,1024]{1,0:T(8,128)S(1)}, f32[32,1024]{1,0:T(8,128)S(1)}, u32[]{:S(2)}, u32[]{:S(2)}) %collective-permute-start.8) | collective-permute-done | bytes 131104 | tf_op jit(solution)/shard_map/ppermute | solution.py:16
  14.0 1.5 %collective-permute-start.2 = (f32[512,128]{1,0:T(8,128)S(1)}, f32[512,128]{1,0:T(8,128)S(1)}, u32[]{:S(2)}, u32[]{:S(2)}) collective-permute-start(f32[512,128]{1,0:T(8,128)S(1)} %copy-done.1), channel_id=1, source_target_pairs={{0,24},{8,16},{16,8},{24,0},{1,25},{9,17},{17,9},{25,1},{2,26},{10... | collective-permute-start | bytes 786440 | tf_op jit(solution)/shard_map/ppermute | solution.py:16
  15.5 4.9 %collective-permute-done.10.refs_0_ = f32[32,1024]{1,0:T(8,128)S(1)} collective-permute-done((f32[32,1024]{1,0:T(8,128)S(1)}, f32[32,1024]{1,0:T(8,128)S(1)}, u32[]{:S(2)}, u32[]{:S(2)}) %collective-permute-start.10) | collective-permute-done | bytes 131104 | tf_op jit(solution)/shard_map/ppermute | solution.py:16
  20.4 0.0 collective-permute-start.3
  20.4 0.0 collective-permute-done.4.refs_2_
  20.4 0.5 collective-permute-start.5
  20.9 0.0 collective-permute-done.refs_1_
  20.9 1.3 %collective-permute-start.12 = (f32[32,1024]{1,0:T(8,128)S(1)}, f32[32,1024]{1,0:T(8,128)S(1)}, u32[]{:S(2)}, u32[]{:S(2)}) collective-permute-start(f32[32,1024]{1,0:T(8,128)S(1)} %get-tuple-element.31), channel_id=1, source_target_pairs={{0,6},{1,7},{2,4},{3,5},{4,2},{5,3},{6,0},{7,1},{8,14},{9,15},{10,... | collective-permute-start | bytes 393224 | tf_op jit(solution)/shard_map/ppermute | solution.py:16
  22.2 0.8 %collective-permute-done.1.refs_2_ = f32[512,128]{1,0:T(8,128)S(1)} collective-permute-done((f32[512,128]{1,0:T(8,128)S(1)}, f32[512,128]{1,0:T(8,128)S(1)}, u32[]{:S(2)}, u32[]{:S(2)}) %collective-permute-start.1) | collective-permute-done | bytes 262176 | tf_op jit(solution)/shard_map/ppermute | solution.py:16
  23.0 0.0 collective-permute-start.7
  23.0 0.0 collective-permute-done.2.refs_3_
  23.0 0.5 collective-permute-start.9
  23.5 0.9 %shard_map.37 = (bf16[1024,256]{1,0:T(8,128)(2,1)S(1)}, f32[512,128]{1,0:T(8,128)S(1)}) custom-call(s32[1,1024]{1,0:T(1,128)S(1)} %bitcast.1, f32[512,128]{1,0:T(8,128)S(1)} %copy-done.1, f32[512,128]{1,0:T(8,128)S(1)} %collective-permute-done.refs_1_, f32[512,128]{1,0:T(8,128)S(1)} %collective-permute-done.1.refs_2_, ...), custom_call_target="tpu_custom_call" | custom-call | tf_op jit(solution)/shard_map/pallas_call | solution.py:20
  24.4 4.8 %collective-permute-done.12.refs_2_ = f32[32,1024]{1,0:T(8,128)S(1)} collective-permute-done((f32[32,1024]{1,0:T(8,128)S(1)}, f32[32,1024]{1,0:T(8,128)S(1)}, u32[]{:S(2)}, u32[]{:S(2)}) %collective-permute-start.12) | collective-permute-done | bytes 131104 | tf_op jit(solution)/shard_map/ppermute | solution.py:16
  29.2 0.0 collective-permute-start.11
  29.2 0.0 collective-permute-done.3.refs_1_
  29.2 0.5 collective-permute-start.13
  29.7 0.0 collective-permute-done.5.refs_3_
  29.7 0.1 shard_map.39
  29.8 0.0 collective-permute-done.7.refs_1_
  29.8 0.0 collective-permute-done.9.refs_3_
  29.8 0.5 %shard_map.40 = (f32[256,128]{1,0:T(8,128)S(1)}, f32[256,128]{1,0:T(8,128)S(1)}, bf16[256,1024]{1,0:T(8,128)(2,1)S(1)}, bf16[256,1024]{1,0:T(8,128)(2,1)S(1)}) custom-call(bf16[1024,256]{1,0:T(8,128)(2,1)S(1)} %get-tuple-element.22.top_ref, bf16[256,1024]{1,0:T(8,128)(2,1)S(1)} %get-tuple-element.24.early_high, ...), custom_call_target="tpu_custom_call" | custom-call | tf_op jit(solution)/shard_map/pallas_call | solution.py:20
  30.4 1.2 %collective-permute-start.14 = (f32[256,128]{1,0:T(8,128)S(1)}, f32[256,128]{1,0:T(8,128)S(1)}, u32[]{:S(2)}, u32[]{:S(2)}) collective-permute-start(f32[256,128]{1,0:T(8,128)S(1)} %get-tuple-element.27.refs_0_), channel_id=1, source_target_pairs={{0,16},{8,24},{16,0},{24,8},{1,17},{9,25},{17,1},{25,9},{2,18},{10... | collective-permute-start | bytes 393224 | tf_op jit(solution)/shard_map/ppermute | solution.py:16
  31.5 1.4 %collective-permute-start.15 = (f32[256,128]{1,0:T(8,128)S(1)}, f32[256,128]{1,0:T(8,128)S(1)}, u32[]{:S(2)}, u32[]{:S(2)}) collective-permute-start(f32[256,128]{1,0:T(8,128)S(1)} %get-tuple-element.27.refs_0_), channel_id=1, source_target_pairs={{0,24},{8,16},{16,8},{24,0},{1,25},{9,17},{17,9},{25,1},{2,26},{10... | collective-permute-start | bytes 393224 | tf_op jit(solution)/shard_map/ppermute | solution.py:16
  32.9 0.7 %collective-permute-start.16 = (f32[256,128]{1,0:T(8,128)S(1)}, f32[256,128]{1,0:T(8,128)S(1)}, u32[]{:S(2)}, u32[]{:S(2)}) collective-permute-start(f32[256,128]{1,0:T(8,128)S(1)} %get-tuple-element.28.refs_1_), channel_id=1, source_target_pairs={{0,16},{16,0},{1,17},{17,1},{2,18},{18,2},{3,19},{19,3},{4,20},{20... | collective-permute-start | bytes 393224 | tf_op jit(solution)/shard_map/ppermute | solution.py:16
  33.6 0.1 shard_map.41
  33.6 0.0 collective-permute-done.11.refs_1_
  33.6 0.7 %collective-permute-start.17 = (f32[256,128]{1,0:T(8,128)S(1)}, f32[256,128]{1,0:T(8,128)S(1)}, u32[]{:S(2)}, u32[]{:S(2)}) collective-permute-start(f32[256,128]{1,0:T(8,128)S(1)} %get-tuple-element.28.refs_1_), channel_id=1, source_target_pairs={{0,24},{24,0},{1,25},{25,1},{2,26},{26,2},{3,27},{27,3},{4,28},{28... | collective-permute-start | bytes 393224 | tf_op jit(solution)/shard_map/ppermute | solution.py:16
  34.3 0.0 collective-permute-done.13.refs_3_
  34.3 0.5 %shard_map.42 = (f32[256,128]{1,0:T(8,128)S(1)}, bf16[256,1024]{1,0:T(8,128)(2,1)S(1)}, bf16[256,1024]{1,0:T(8,128)(2,1)S(1)}) custom-call(bf16[1024,256]{1,0:T(8,128)(2,1)S(1)} %get-tuple-element.22.top_ref, bf16[256,1024]{1,0:T(8,128)(2,1)S(1)} %get-tuple-element.29.early_high, bf16[256,1024]{1,0:T(8,128)(2,1)S(1)} %get-tuple-element.30.early_low, ...), custom_call_target="tpu_custom_call" | custom-call | tf_op jit(solution)/shard_map/pallas_call | solution.py:20
  34.9 7.5 %collective-permute-start.18 = (f32[256,128]{1,0:T(8,128)S(1)}, f32[256,128]{1,0:T(8,128)S(1)}, u32[]{:S(2)}, u32[]{:S(2)}) collective-permute-start(f32[256,128]{1,0:T(8,128)S(1)} %get-tuple-element.32.refs_2_), channel_id=1, source_target_pairs={{8,24},{24,8},{9,25},{25,9},{10,26},{26,10},{11,27},{27,11},{12,28... | collective-permute-start | bytes 393224 | tf_op jit(solution)/shard_map/ppermute | solution.py:16
  42.4 0.0 collective-permute-done.14.refs_7_
  42.4 1.9 %collective-permute-start.19 = (f32[256,128]{1,0:T(8,128)S(1)}, f32[256,128]{1,0:T(8,128)S(1)}, u32[]{:S(2)}, u32[]{:S(2)}) collective-permute-start(f32[256,128]{1,0:T(8,128)S(1)} %get-tuple-element.32.refs_2_), channel_id=1, source_target_pairs={{8,16},{16,8},{9,17},{17,9},{10,18},{18,10},{11,19},{19,11},{12,20... | collective-permute-start | bytes 393224 | tf_op jit(solution)/shard_map/ppermute | solution.py:16
  44.4 0.0 collective-permute-done.15.refs_8_
  44.4 0.0 collective-permute-done.16.refs_9_
  44.4 0.0 collective-permute-done.17.refs_10_
  44.4 1.0 %collective-permute-done.18.refs_11_ = f32[256,128]{1,0:T(8,128)S(1)} collective-permute-done((f32[256,128]{1,0:T(8,128)S(1)}, f32[256,128]{1,0:T(8,128)S(1)}, u32[]{:S(2)}, u32[]{:S(2)}) %collective-permute-start.18) | collective-permute-done | bytes 131104 | tf_op jit(solution)/shard_map/ppermute | solution.py:16
  45.4 4.8 %collective-permute-done.19.refs_12_ = f32[256,128]{1,0:T(8,128)S(1)} collective-permute-done((f32[256,128]{1,0:T(8,128)S(1)}, f32[256,128]{1,0:T(8,128)S(1)}, u32[]{:S(2)}, u32[]{:S(2)}) %collective-permute-start.19) | collective-permute-done | bytes 131104 | tf_op jit(solution)/shard_map/ppermute | solution.py:16
  50.2 0.7 %shard_map.43 = f32[512,128]{1,0:T(8,128)} custom-call(f32[512,128]{1,0:T(8,128)S(1)} %get-tuple-element.21.own_ref, f32[256,128]{1,0:T(8,128)S(1)} %get-tuple-element.27.refs_0_, f32[256,128]{1,0:T(8,128)S(1)} %get-tuple-element.28.refs_1_, f32[256,128]{1,0:T(8,128)S(1)} %get-tuple-element.32.refs_2_, bf16[256,1024]{1,0:T(8,128)(2,1)S(1)} %get-tuple-element.33.refs_3_, ...), custom_call_target="tpu_custom_call" | custom-call | tf_op jit(solution)/shard_map/pallas_call | solution.py:20
  (5 shorter events, 0.0 us)
Async XLA Ops:
  0.0 0.9 %copy-start = (f32[64,1024]{1,0:T(8,128)S(1)}, f32[64,1024]{1,0:T(8,128)}, u32[]{:S(2)}) copy-start(f32[64,1024]{1,0:T(8,128)} %panel_ref.1) | copy-start | bytes 786436
  1.0 3.6 %copy-start.1 = (f32[512,128]{1,0:T(8,128)S(1)}, f32[512,128]{1,0:T(8,128)}, u32[]{:S(2)}) copy-start(f32[512,128]{1,0:T(8,128)} %refs_0_.1) | copy-start | bytes 786436
  1.0 22.5 %copy-start.2 = (s32[1024]{0:T(1024)S(1)}, s32[1024]{0:T(1024)}, u32[]{:S(2)}) copy-start(s32[1024]{0:T(1024)} %param.5) | copy-start | bytes 12292
  1.0 8.2 %collective-permute-start.6 = (f32[32,1024]{1,0:T(8,128)S(1)}, f32[32,1024]{1,0:T(8,128)S(1)}, u32[]{:S(2)}, u32[]{:S(2)}) collective-permute-start(f32[32,1024]{1,0:T(8,128)S(1)} %get-tuple-element.26), channel_id=1, source_target_pairs={{0,4},{1,5},{2,6},{3,7},{4,0},{5,1},{6,2},{7,3},{8,12},{9,13},{10,... | collective-permute-start | bytes 393224 | tf_op jit(solution)/shard_map/ppermute | solution.py:16
  3.7 16.8 %collective-permute-start.4 = (f32[64,1024]{1,0:T(8,128)S(1)}, f32[64,1024]{1,0:T(8,128)S(1)}, u32[]{:S(2)}, u32[]{:S(2)}) collective-permute-start(f32[64,1024]{1,0:T(8,128)S(1)} %get-tuple-element.23.refs_0_), channel_id=1, source_target_pairs={{0,2},{1,3},{2,0},{3,1},{4,6},{5,7},{6,4},{7,5},{8,10},{9,11},{10,... | collective-permute-start | bytes 786440 | tf_op jit(solution)/shard_map/ppermute | solution.py:16
  4.1 9.9 %collective-permute-start.8 = (f32[32,1024]{1,0:T(8,128)S(1)}, f32[32,1024]{1,0:T(8,128)S(1)}, u32[]{:S(2)}, u32[]{:S(2)}) collective-permute-start(f32[32,1024]{1,0:T(8,128)S(1)} %get-tuple-element.26), channel_id=1, source_target_pairs={{0,6},{1,7},{2,4},{3,5},{4,2},{5,3},{6,0},{7,1},{8,14},{9,15},{10,... | collective-permute-start | bytes 393224 | tf_op jit(solution)/shard_map/ppermute | solution.py:16
  4.6 16.3 %collective-permute-start = (f32[512,128]{1,0:T(8,128)S(1)}, f32[512,128]{1,0:T(8,128)S(1)}, u32[]{:S(2)}, u32[]{:S(2)}) collective-permute-start(f32[512,128]{1,0:T(8,128)S(1)} %copy-done.1), channel_id=1, source_target_pairs={{0,8},{8,0},{16,24},{24,16},{1,9},{9,1},{17,25},{25,17},{2,10},{10... | collective-permute-start | bytes 786440 | tf_op jit(solution)/shard_map/ppermute | solution.py:16
  5.1 15.3 %collective-permute-start.10 = (f32[32,1024]{1,0:T(8,128)S(1)}, f32[32,1024]{1,0:T(8,128)S(1)}, u32[]{:S(2)}, u32[]{:S(2)}) collective-permute-start(f32[32,1024]{1,0:T(8,128)S(1)} %get-tuple-element.31), channel_id=1, source_target_pairs={{0,4},{1,5},{2,6},{3,7},{4,0},{5,1},{6,2},{7,3},{8,12},{9,13},{10,... | collective-permute-start | bytes 393224 | tf_op jit(solution)/shard_map/ppermute | solution.py:16
  9.3 13.8 %collective-permute-start.1 = (f32[512,128]{1,0:T(8,128)S(1)}, f32[512,128]{1,0:T(8,128)S(1)}, u32[]{:S(2)}, u32[]{:S(2)}) collective-permute-start(f32[512,128]{1,0:T(8,128)S(1)} %copy-done.1), channel_id=1, source_target_pairs={{0,16},{8,24},{16,0},{24,8},{1,17},{9,25},{17,1},{25,9},{2,18},{10... | collective-permute-start | bytes 786440 | tf_op jit(solution)/shard_map/ppermute | solution.py:16
  14.0 9.0 %collective-permute-start.2 = (f32[512,128]{1,0:T(8,128)S(1)}, f32[512,128]{1,0:T(8,128)S(1)}, u32[]{:S(2)}, u32[]{:S(2)}) collective-permute-start(f32[512,128]{1,0:T(8,128)S(1)} %copy-done.1), channel_id=1, source_target_pairs={{0,24},{8,16},{16,8},{24,0},{1,25},{9,17},{17,9},{25,1},{2,26},{10... | collective-permute-start | bytes 786440 | tf_op jit(solution)/shard_map/ppermute | solution.py:16
  20.4 8.8 %collective-permute-start.3 = (f32[64,1024]{1,0:T(8,128)S(1)}, f32[64,1024]{1,0:T(8,128)S(1)}, u32[]{:S(2)}, u32[]{:S(2)}) collective-permute-start(f32[64,1024]{1,0:T(8,128)S(1)} %get-tuple-element.23.refs_0_), channel_id=1, source_target_pairs={{0,1},{1,0},{2,3},{3,2},{4,5},{5,4},{6,7},{7,6},{8,9},{9,8},{10,11... | collective-permute-start | bytes 786440 | tf_op jit(solution)/shard_map/ppermute | solution.py:16
  20.4 9.3 %collective-permute-start.5 = (f32[64,1024]{1,0:T(8,128)S(1)}, f32[64,1024]{1,0:T(8,128)S(1)}, u32[]{:S(2)}, u32[]{:S(2)}) collective-permute-start(f32[64,1024]{1,0:T(8,128)S(1)} %collective-permute-done.4.refs_2_), channel_id=1, source_target_pairs={{0,1},{1,0},{2,3},{3,2},{4,5},{5,4},{6,7},{7,6},{8,9},{9,8},{10,11... | collective-permute-start | bytes 786440 | tf_op jit(solution)/shard_map/ppermute | solution.py:16
  20.9 8.3 %collective-permute-start.12 = (f32[32,1024]{1,0:T(8,128)S(1)}, f32[32,1024]{1,0:T(8,128)S(1)}, u32[]{:S(2)}, u32[]{:S(2)}) collective-permute-start(f32[32,1024]{1,0:T(8,128)S(1)} %get-tuple-element.31), channel_id=1, source_target_pairs={{0,6},{1,7},{2,4},{3,5},{4,2},{5,3},{6,0},{7,1},{8,14},{9,15},{10,... | collective-permute-start | bytes 393224 | tf_op jit(solution)/shard_map/ppermute | solution.py:16
  23.0 6.8 %collective-permute-start.7 = (f32[32,1024]{1,0:T(8,128)S(1)}, f32[32,1024]{1,0:T(8,128)S(1)}, u32[]{:S(2)}, u32[]{:S(2)}) collective-permute-start(f32[32,1024]{1,0:T(8,128)S(1)} %collective-permute-done.6.refs_0_), channel_id=1, source_target_pairs={{0,1},{1,0},{2,3},{3,2},{4,5},{5,4},{6,7},{7,6},{8,9},{9,8},{10,11... | collective-permute-start | bytes 393224 | tf_op jit(solution)/shard_map/ppermute | solution.py:16
  23.0 6.8 %collective-permute-start.9 = (f32[32,1024]{1,0:T(8,128)S(1)}, f32[32,1024]{1,0:T(8,128)S(1)}, u32[]{:S(2)}, u32[]{:S(2)}) collective-permute-start(f32[32,1024]{1,0:T(8,128)S(1)} %collective-permute-done.8.refs_2_), channel_id=1, source_target_pairs={{0,1},{1,0},{2,3},{3,2},{4,5},{5,4},{6,7},{7,6},{8,9},{9,8},{10,11... | collective-permute-start | bytes 393224 | tf_op jit(solution)/shard_map/ppermute | solution.py:16
  29.2 4.4 %collective-permute-start.11 = (f32[32,1024]{1,0:T(8,128)S(1)}, f32[32,1024]{1,0:T(8,128)S(1)}, u32[]{:S(2)}, u32[]{:S(2)}) collective-permute-start(f32[32,1024]{1,0:T(8,128)S(1)} %collective-permute-done.10.refs_0_), channel_id=1, source_target_pairs={{0,1},{1,0},{2,3},{3,2},{4,5},{5,4},{6,7},{7,6},{8,9},{9,8},{10,11... | collective-permute-start | bytes 393224 | tf_op jit(solution)/shard_map/ppermute | solution.py:16
  29.2 5.1 %collective-permute-start.13 = (f32[32,1024]{1,0:T(8,128)S(1)}, f32[32,1024]{1,0:T(8,128)S(1)}, u32[]{:S(2)}, u32[]{:S(2)}) collective-permute-start(f32[32,1024]{1,0:T(8,128)S(1)} %collective-permute-done.12.refs_2_), channel_id=1, source_target_pairs={{0,1},{1,0},{2,3},{3,2},{4,5},{5,4},{6,7},{7,6},{8,9},{9,8},{10,11... | collective-permute-start | bytes 393224 | tf_op jit(solution)/shard_map/ppermute | solution.py:16
  30.4 12.1 %collective-permute-start.14 = (f32[256,128]{1,0:T(8,128)S(1)}, f32[256,128]{1,0:T(8,128)S(1)}, u32[]{:S(2)}, u32[]{:S(2)}) collective-permute-start(f32[256,128]{1,0:T(8,128)S(1)} %get-tuple-element.27.refs_0_), channel_id=1, source_target_pairs={{0,16},{8,24},{16,0},{24,8},{1,17},{9,25},{17,1},{25,9},{2,18},{10... | collective-permute-start | bytes 393224 | tf_op jit(solution)/shard_map/ppermute | solution.py:16
  31.5 12.8 %collective-permute-start.15 = (f32[256,128]{1,0:T(8,128)S(1)}, f32[256,128]{1,0:T(8,128)S(1)}, u32[]{:S(2)}, u32[]{:S(2)}) collective-permute-start(f32[256,128]{1,0:T(8,128)S(1)} %get-tuple-element.27.refs_0_), channel_id=1, source_target_pairs={{0,24},{8,16},{16,8},{24,0},{1,25},{9,17},{17,9},{25,1},{2,26},{10... | collective-permute-start | bytes 393224 | tf_op jit(solution)/shard_map/ppermute | solution.py:16
  32.9 11.5 %collective-permute-start.16 = (f32[256,128]{1,0:T(8,128)S(1)}, f32[256,128]{1,0:T(8,128)S(1)}, u32[]{:S(2)}, u32[]{:S(2)}) collective-permute-start(f32[256,128]{1,0:T(8,128)S(1)} %get-tuple-element.28.refs_1_), channel_id=1, source_target_pairs={{0,16},{16,0},{1,17},{17,1},{2,18},{18,2},{3,19},{19,3},{4,20},{20... | collective-permute-start | bytes 393224 | tf_op jit(solution)/shard_map/ppermute | solution.py:16
  33.6 10.7 %collective-permute-start.17 = (f32[256,128]{1,0:T(8,128)S(1)}, f32[256,128]{1,0:T(8,128)S(1)}, u32[]{:S(2)}, u32[]{:S(2)}) collective-permute-start(f32[256,128]{1,0:T(8,128)S(1)} %get-tuple-element.28.refs_1_), channel_id=1, source_target_pairs={{0,24},{24,0},{1,25},{25,1},{2,26},{26,2},{3,27},{27,3},{4,28},{28... | collective-permute-start | bytes 393224 | tf_op jit(solution)/shard_map/ppermute | solution.py:16
  34.9 10.5 %collective-permute-start.18 = (f32[256,128]{1,0:T(8,128)S(1)}, f32[256,128]{1,0:T(8,128)S(1)}, u32[]{:S(2)}, u32[]{:S(2)}) collective-permute-start(f32[256,128]{1,0:T(8,128)S(1)} %get-tuple-element.32.refs_2_), channel_id=1, source_target_pairs={{8,24},{24,8},{9,25},{25,9},{10,26},{26,10},{11,27},{27,11},{12,28... | collective-permute-start | bytes 393224 | tf_op jit(solution)/shard_map/ppermute | solution.py:16
  42.4 7.8 %collective-permute-start.19 = (f32[256,128]{1,0:T(8,128)S(1)}, f32[256,128]{1,0:T(8,128)S(1)}, u32[]{:S(2)}, u32[]{:S(2)}) collective-permute-start(f32[256,128]{1,0:T(8,128)S(1)} %get-tuple-element.32.refs_2_), channel_id=1, source_target_pairs={{8,16},{16,8},{9,17},{17,9},{10,18},{18,10},{11,19},{19,11},{12,20... | collective-permute-start | bytes 393224 | tf_op jit(solution)/shard_map/ppermute | solution.py:16

commit v3 on v1

--- a/solution.py
+++ b/solution.py
@@ -78,6 +78,12 @@
         own_ref[...] = jnp.where(named, replaced, blocks[0][...])
 
 
+def cut(panel_ref, *chunk_refs):
+    unit = chunk_refs[0].shape[0]
+    for i, ref in enumerate(chunk_refs):
+        ref[...] = panel_ref[pl.ds(i * unit, unit), :]
+
+
 def collect(order, unit, chunk, me, pieces, high, low):
     for mask, ref in zip(order, pieces):
         at = pl.ds(pl.multiple_of((me ^ mask) * unit, unit), unit)
@@ -148,13 +154,21 @@
     unit = depth // chunks
     f32, bf16 = jnp.float32, jnp.bfloat16
 
-    near = [panel, swap(panel, "pcol", 2)]
-    near = [piece for block_ in near for piece in (block_, swap(block_, "pcol", 1))]
+    parts = [panel]
+    if chunks > 1:
+        parts = call(cut, [pltpu.VMEM((unit, block), f32)] * chunks, [], panel)
+
+    def both(pieces):
+        return [got for piece in pieces for got in (piece, swap(piece, "pcol", 1))]
+
+    near = both([panel, swap(panel, "pcol", 2)])
     far = []
     for chunk in range(chunks):
-        part = panel[chunk * unit : (chunk + 1) * unit]
-        got = [swap(part, "pcol", mask) for mask in range(4, n_cols, 2)]
-        far.append([piece for block_ in got for piece in (block_, swap(block_, "pcol", 1))])
+        pieces = []
+        for mask in range(4, n_cols, 4):
+            pieces.append(swap(parts[chunk], "pcol", mask))
+            pieces.append(swap(pieces[-1], "pcol", 2))
+        far.append(both(pieces))
     blocks = [matrix] + [swap(matrix, "prow", mask) for mask in range(1, n_rows)]
 
     top, own = call(

time: 50.8 us -> 44.8 us (0.88)
  starting transfers between devices: 22.2 us -> 18.1 us
  waiting for transfers between devices: 24.4 us -> 22.5 us
    ppermute x18, starting transfers between devices: 22.2 us -> 18.1 us  [swap(): lax.ppermute(block, axis, [(i, i ^ mask) for i in range(lax.axis_size(axi...]
    ppermute x18, waiting for transfers between devices: 24.4 us -> 22.5 us  [swap(): lax.ppermute(block, axis, [(i, i ^ mask) for i in range(lax.axis_size(axi...]
    slice x1 -> x0, local copies, waits for them, and re-layouts: 1.04 us -> none  [per_device(): part = panel[chunk * unit:(chunk + 1) * unit]]
    unnamed x6 -> x8, local copies, waits for them, and re-layouts: 0.01 us -> 1.03 us
    pallas_call x6 -> x7, Pallas kernels: 2.84 us -> 2.86 us  [call(): pl.pallas_call(kernel, out_shape=out_shape, in_specs=[VMEM] * len(args),...]
  transfers between devices with their start and end apart: 18 -> 18, of which waited for: 6 -> 7; matrix products, arithmetic and copies ran while one was open for 0% -> 0% of each run, Pallas kernels for 4% -> 5%
where the time goes in v3:
time: 44.8 us; the launch traced here: 44.6 us
  waiting for transfers between devices  22.5 us (50%)
  starting transfers between devices  18.1 us (40%)
  Pallas kernels  2.86 us (6%)
  local copies, waits for them, and re-layouts  1.03 us (2%)
    ppermute x18, waiting for transfers between devices, swap(): lax.ppermute(block, axis, [(i, i ^ mask) for i in range(lax.axis_size(axi...  22.5 us
    ppermute x18, starting transfers between devices, swap(): lax.ppermute(block, axis, [(i, i ^ mask) for i in range(lax.axis_size(axi...  18.1 us
    pallas_call x7, Pallas kernels, call(): pl.pallas_call(kernel, out_shape=out_shape, in_specs=[VMEM] * len(args),...  2.86 us
    unnamed x8, local copies, waits for them, and re-layouts  1.03 us
  transfers between devices with their start and end apart: 18, of which 7 were waited for; matrix products, arithmetic and copies ran while one was open for 0% of the time, Pallas kernels for 5%

profile of v3, /device:TPU:0, one launch (start us, length us, event | category | flops | bytes accessed | tf_op | source)
XLA Modules:
  0.0 44.6 jit_solution(5584384395713948433)
XLA Ops:
  0.0 3.1 %collective-permute-start.4 = (f32[64,1024]{1,0:T(8,128)}, f32[64,1024]{1,0:T(8,128)S(1)}, u32[]{:S(2)}, u32[]{:S(2)}) collective-permute-start(f32[64,1024]{1,0:T(8,128)} %refs_0_.5), channel_id=1, source_target_pairs={{0,2},{1,3},{2,0},{3,1},{4,6},{5,7},{6,4},{7,5},{8,10},{9,11},{10,... | collective-permute-start | bytes 786440 | tf_op jit(solution)/shard_map/ppermute | solution.py:15
  3.1 0.0 copy-start
  3.1 1.0 %copy-done = f32[64,1024]{1,0:T(8,128)S(1)} copy-done((f32[64,1024]{1,0:T(8,128)S(1)}, f32[64,1024]{1,0:T(8,128)}, u32[]{:S(2)}) %copy-start) | copy-done | bytes 262168
  4.1 0.0 copy-start.3
  4.1 2.7 %collective-permute-start.6 = (f32[32,1024]{1,0:T(8,128)S(1)}, f32[32,1024]{1,0:T(8,128)S(1)}, u32[]{:S(2)}, u32[]{:S(2)}) collective-permute-start(f32[32,1024]{1,0:T(8,128)S(1)} %get-tuple-element.23), channel_id=1, source_target_pairs={{0,4},{1,5},{2,6},{3,7},{4,0},{5,1},{6,2},{7,3},{8,12},{9,13},{10,... | collective-permute-start | bytes 393224 | tf_op jit(solution)/shard_map/ppermute | solution.py:15
  6.7 0.0 copy-done.2
  6.7 1.5 %collective-permute-start = (f32[512,128]{1,0:T(8,128)S(1)}, f32[512,128]{1,0:T(8,128)S(1)}, u32[]{:S(2)}, u32[]{:S(2)}) collective-permute-start(f32[512,128]{1,0:T(8,128)S(1)} %copy-done.2), channel_id=1, source_target_pairs={{0,8},{8,0},{16,24},{24,16},{1,9},{9,1},{17,25},{25,17},{2,10},{10... | collective-permute-start | bytes 786440 | tf_op jit(solution)/shard_map/ppermute | solution.py:15
  8.2 0.8 %collective-permute-start.10 = (f32[32,1024]{1,0:T(8,128)S(1)}, f32[32,1024]{1,0:T(8,128)S(1)}, u32[]{:S(2)}, u32[]{:S(2)}) collective-permute-start(f32[32,1024]{1,0:T(8,128)S(1)} %get-tuple-element.27), channel_id=1, source_target_pairs={{0,4},{1,5},{2,6},{3,7},{4,0},{5,1},{6,2},{7,3},{8,12},{9,13},{10,... | collective-permute-start | bytes 393224 | tf_op jit(solution)/shard_map/ppermute | solution.py:15
  9.1 1.5 %collective-permute-start.1 = (f32[512,128]{1,0:T(8,128)S(1)}, f32[512,128]{1,0:T(8,128)S(1)}, u32[]{:S(2)}, u32[]{:S(2)}) collective-permute-start(f32[512,128]{1,0:T(8,128)S(1)} %copy-done.2), channel_id=1, source_target_pairs={{0,16},{8,24},{16,0},{24,8},{1,17},{9,25},{17,1},{25,9},{2,18},{10... | collective-permute-start | bytes 786440 | tf_op jit(solution)/shard_map/ppermute | solution.py:15
  10.6 2.2 %collective-permute-done.6.refs_0_ = f32[32,1024]{1,0:T(8,128)S(1)} collective-permute-done((f32[32,1024]{1,0:T(8,128)S(1)}, f32[32,1024]{1,0:T(8,128)S(1)}, u32[]{:S(2)}, u32[]{:S(2)}) %collective-permute-start.6) | collective-permute-done | bytes 131104 | tf_op jit(solution)/shard_map/ppermute | solution.py:15
  12.8 2.4 %collective-permute-start.2 = (f32[512,128]{1,0:T(8,128)S(1)}, f32[512,128]{1,0:T(8,128)S(1)}, u32[]{:S(2)}, u32[]{:S(2)}) collective-permute-start(f32[512,128]{1,0:T(8,128)S(1)} %copy-done.2), channel_id=1, source_target_pairs={{0,24},{8,16},{16,8},{24,0},{1,25},{9,17},{17,9},{25,1},{2,26},{10... | collective-permute-start | bytes 786440 | tf_op jit(solution)/shard_map/ppermute | solution.py:15
  15.3 3.8 %collective-permute-done.10.refs_0_ = f32[32,1024]{1,0:T(8,128)S(1)} collective-permute-done((f32[32,1024]{1,0:T(8,128)S(1)}, f32[32,1024]{1,0:T(8,128)S(1)}, u32[]{:S(2)}, u32[]{:S(2)}) %collective-permute-start.10) | collective-permute-done | bytes 131104 | tf_op jit(solution)/shard_map/ppermute | solution.py:15
  19.1 0.0 collective-permute-start.3
  19.1 0.0 collective-permute-done.4.refs_2_
  19.1 0.5 %collective-permute-start.5 = (f32[64,1024]{1,0:T(8,128)S(1)}, f32[64,1024]{1,0:T(8,128)S(1)}, u32[]{:S(2)}, u32[]{:S(2)}) collective-permute-start(f32[64,1024]{1,0:T(8,128)S(1)} %collective-permute-done.4.refs_2_), channel_id=1, source_target_pairs={{0,1},{1,0},{2,3},{3,2},{4,5},{5,4},{6,7},{7,6},{8,9},{9,8},{10,11... | collective-permute-start | bytes 786440 | tf_op jit(solution)/shard_map/ppermute | solution.py:15
  19.6 0.0 collective-permute-done.refs_1_
  19.6 0.0 collective-permute-start.8
  19.6 2.3 %collective-permute-done.1.refs_2_ = f32[512,128]{1,0:T(8,128)S(1)} collective-permute-done((f32[512,128]{1,0:T(8,128)S(1)}, f32[512,128]{1,0:T(8,128)S(1)}, u32[]{:S(2)}, u32[]{:S(2)}) %collective-permute-start.1) | collective-permute-done | bytes 262176 | tf_op jit(solution)/shard_map/ppermute | solution.py:15
  21.9 0.0 collective-permute-start.12
  21.9 0.0 collective-permute-done.2.refs_3_
  21.9 0.0 collective-permute-start.7
  21.9 4.1 %collective-permute-done.8.refs_2_ = f32[32,1024]{1,0:T(8,128)S(1)} collective-permute-done((f32[32,1024]{1,0:T(8,128)S(1)}, f32[32,1024]{1,0:T(8,128)S(1)}, u32[]{:S(2)}, u32[]{:S(2)}) %collective-permute-start.8) | collective-permute-done | bytes 131104 | tf_op jit(solution)/shard_map/ppermute | solution.py:15
  26.0 0.0 collective-permute-start.9
  26.0 0.0 collective-permute-done.3.refs_1_
  26.0 0.5 %collective-permute-start.11 = (f32[32,1024]{1,0:T(8,128)S(1)}, f32[32,1024]{1,0:T(8,128)S(1)}, u32[]{:S(2)}, u32[]{:S(2)}) collective-permute-start(f32[32,1024]{1,0:T(8,128)S(1)} %collective-permute-done.10.refs_0_), channel_id=1, source_target_pairs={{0,1},{1,0},{2,3},{3,2},{4,5},{5,4},{6,7},{7,6},{8,9},{9,8},{10,11... | collective-permute-start | bytes 393224 | tf_op jit(solution)/shard_map/ppermute | solution.py:15
  26.5 1.4 %collective-permute-done.12.refs_2_ = f32[32,1024]{1,0:T(8,128)S(1)} collective-permute-done((f32[32,1024]{1,0:T(8,128)S(1)}, f32[32,1024]{1,0:T(8,128)S(1)}, u32[]{:S(2)}, u32[]{:S(2)}) %collective-permute-start.12) | collective-permute-done | bytes 131104 | tf_op jit(solution)/shard_map/ppermute | solution.py:15
  27.9 0.0 collective-permute-start.13
  27.9 0.0 copy-done.3
  27.9 0.9 %shard_map.37 = (bf16[1024,256]{1,0:T(8,128)(2,1)S(1)}, f32[512,128]{1,0:T(8,128)S(1)}) custom-call(s32[1,1024]{1,0:T(1,128)S(1)} %bitcast.1, f32[512,128]{1,0:T(8,128)S(1)} %copy-done.2, f32[512,128]{1,0:T(8,128)S(1)} %collective-permute-done.refs_1_, f32[512,128]{1,0:T(8,128)S(1)} %collective-permute-done.1.refs_2_, ...), custom_call_target="tpu_custom_call" | custom-call | tf_op jit(solution)/shard_map/pallas_call | solution.py:19
  28.8 0.0 collective-permute-done.5.refs_3_
  28.8 0.0 copy-done.1
  28.9 0.1 shard_map.38
  28.9 0.0 collective-permute-done.7.refs_1_
  28.9 0.0 collective-permute-done.9.refs_3_
  28.9 0.5 %shard_map.40 = (f32[256,128]{1,0:T(8,128)S(1)}, bf16[256,1024]{1,0:T(8,128)(2,1)S(1)}, bf16[256,1024]{1,0:T(8,128)(2,1)S(1)}) custom-call(bf16[1024,256]{1,0:T(8,128)(2,1)S(1)} %get-tuple-element.20.top_ref, bf16[256,1024]{1,0:T(8,128)(2,1)S(1)} %get-tuple-element.21.early_high, bf16[256,1024]{1,0:T(8,128)(2,1)S(1)} %get-tuple-element.22.early_low, ...), custom_call_target="tpu_custom_call" | custom-call | tf_op jit(solution)/shard_map/pallas_call | solution.py:19
  29.5 1.2 %collective-permute-start.14 = (f32[256,128]{1,0:T(8,128)S(1)}, f32[256,128]{1,0:T(8,128)S(1)}, u32[]{:S(2)}, u32[]{:S(2)}) collective-permute-start(f32[256,128]{1,0:T(8,128)S(1)} %get-tuple-element.24.refs_0_), channel_id=1, source_target_pairs={{0,16},{8,24},{16,0},{24,8},{1,17},{9,25},{17,1},{25,9},{2,18},{10... | collective-permute-start | bytes 393224 | tf_op jit(solution)/shard_map/ppermute | solution.py:15
  30.6 1.2 %collective-permute-start.15 = (f32[256,128]{1,0:T(8,128)S(1)}, f32[256,128]{1,0:T(8,128)S(1)}, u32[]{:S(2)}, u32[]{:S(2)}) collective-permute-start(f32[256,128]{1,0:T(8,128)S(1)} %get-tuple-element.24.refs_0_), channel_id=1, source_target_pairs={{0,24},{8,16},{16,8},{24,0},{1,25},{9,17},{17,9},{25,1},{2,26},{10... | collective-permute-start | bytes 393224 | tf_op jit(solution)/shard_map/ppermute | solution.py:15
  31.9 0.1 shard_map.41
  32.0 0.0 collective-permute-done.11.refs_1_
  32.0 0.0 collective-permute-done.13.refs_3_
  32.0 0.5 %shard_map.42 = (f32[256,128]{1,0:T(8,128)S(1)}, bf16[256,1024]{1,0:T(8,128)(2,1)S(1)}, bf16[256,1024]{1,0:T(8,128)(2,1)S(1)}) custom-call(bf16[1024,256]{1,0:T(8,128)(2,1)S(1)} %get-tuple-element.20.top_ref, bf16[256,1024]{1,0:T(8,128)(2,1)S(1)} %get-tuple-element.25.early_high, bf16[256,1024]{1,0:T(8,128)(2,1)S(1)} %get-tuple-element.26.early_low, ...), custom_call_target="tpu_custom_call" | custom-call | tf_op jit(solution)/shard_map/pallas_call | solution.py:19
  32.5 0.7 %collective-permute-start.16 = (f32[256,128]{1,0:T(8,128)S(1)}, f32[256,128]{1,0:T(8,128)S(1)}, u32[]{:S(2)}, u32[]{:S(2)}) collective-permute-start(f32[256,128]{1,0:T(8,128)S(1)} %get-tuple-element.28.refs_1_), channel_id=1, source_target_pairs={{0,16},{8,24},{16,0},{24,8},{1,17},{9,25},{17,1},{25,9},{2,18},{10... | collective-permute-start | bytes 393224 | tf_op jit(solution)/shard_map/ppermute | solution.py:15
  33.3 2.0 %collective-permute-start.17 = (f32[256,128]{1,0:T(8,128)S(1)}, f32[256,128]{1,0:T(8,128)S(1)}, u32[]{:S(2)}, u32[]{:S(2)}) collective-permute-start(f32[256,128]{1,0:T(8,128)S(1)} %get-tuple-element.28.refs_1_), channel_id=1, source_target_pairs={{0,24},{8,16},{16,8},{24,0},{1,25},{9,17},{17,9},{25,1},{2,26},{10... | collective-permute-start | bytes 393224 | tf_op jit(solution)/shard_map/ppermute | solution.py:15
  35.2 6.3 %collective-permute-done.14.refs_6_ = f32[256,128]{1,0:T(8,128)S(1)} collective-permute-done((f32[256,128]{1,0:T(8,128)S(1)}, f32[256,128]{1,0:T(8,128)S(1)}, u32[]{:S(2)}, u32[]{:S(2)}) %collective-permute-start.14) | collective-permute-done | bytes 131104 | tf_op jit(solution)/shard_map/ppermute | solution.py:15
  41.5 0.0 collective-permute-done.15.refs_7_
  41.5 2.3 %collective-permute-done.16.refs_8_ = f32[256,128]{1,0:T(8,128)S(1)} collective-permute-done((f32[256,128]{1,0:T(8,128)S(1)}, f32[256,128]{1,0:T(8,128)S(1)}, u32[]{:S(2)}, u32[]{:S(2)}) %collective-permute-start.16) | collective-permute-done | bytes 131104 | tf_op jit(solution)/shard_map/ppermute | solution.py:15
  43.9 0.0 collective-permute-done.17.refs_9_
  43.9 0.7 %shard_map.43 = f32[512,128]{1,0:T(8,128)} custom-call(f32[512,128]{1,0:T(8,128)S(1)} %get-tuple-element.19.own_ref, f32[256,128]{1,0:T(8,128)S(1)} %get-tuple-element.24.refs_0_, f32[256,128]{1,0:T(8,128)S(1)} %get-tuple-element.28.refs_1_, bf16[256,1024]{1,0:T(8,128)(2,1)S(1)} %get-tuple-element.29.refs_2_, ...), custom_call_target="tpu_custom_call" | custom-call | tf_op jit(solution)/shard_map/pallas_call | solution.py:19
  (3 shorter events, 0.0 us)
Async XLA Ops:
  0.0 19.1 %collective-permute-start.4 = (f32[64,1024]{1,0:T(8,128)}, f32[64,1024]{1,0:T(8,128)S(1)}, u32[]{:S(2)}, u32[]{:S(2)}) collective-permute-start(f32[64,1024]{1,0:T(8,128)} %refs_0_.5), channel_id=1, source_target_pairs={{0,2},{1,3},{2,0},{3,1},{4,6},{5,7},{6,4},{7,5},{8,10},{9,11},{10,... | collective-permute-start | bytes 786440 | tf_op jit(solution)/shard_map/ppermute | solution.py:15
  3.1 1.0 %copy-start = (f32[64,1024]{1,0:T(8,128)S(1)}, f32[64,1024]{1,0:T(8,128)}, u32[]{:S(2)}) copy-start(f32[64,1024]{1,0:T(8,128)} %refs_0_.5) | copy-start | bytes 786436
  4.0 2.7 %copy-start.2 = (f32[512,128]{1,0:T(8,128)S(1)}, f32[512,128]{1,0:T(8,128)}, u32[]{:S(2)}) copy-start(f32[512,128]{1,0:T(8,128)} %refs_0_.3) | copy-start | bytes 786436
  4.1 23.8 %copy-start.3 = (s32[1024]{0:T(1024)S(1)}, s32[1024]{0:T(1024)}, u32[]{:S(2)}) copy-start(s32[1024]{0:T(1024)} %param.5) | copy-start | bytes 12292
  4.1 8.7 %collective-permute-start.6 = (f32[32,1024]{1,0:T(8,128)S(1)}, f32[32,1024]{1,0:T(8,128)S(1)}, u32[]{:S(2)}, u32[]{:S(2)}) collective-permute-start(f32[32,1024]{1,0:T(8,128)S(1)} %get-tuple-element.23), channel_id=1, source_target_pairs={{0,4},{1,5},{2,6},{3,7},{4,0},{5,1},{6,2},{7,3},{8,12},{9,13},{10,... | collective-permute-start | bytes 393224 | tf_op jit(solution)/shard_map/ppermute | solution.py:15
  6.7 12.9 %collective-permute-start = (f32[512,128]{1,0:T(8,128)S(1)}, f32[512,128]{1,0:T(8,128)S(1)}, u32[]{:S(2)}, u32[]{:S(2)}) collective-permute-start(f32[512,128]{1,0:T(8,128)S(1)} %copy-done.2), channel_id=1, source_target_pairs={{0,8},{8,0},{16,24},{24,16},{1,9},{9,1},{17,25},{25,17},{2,10},{10... | collective-permute-start | bytes 786440 | tf_op jit(solution)/shard_map/ppermute | solution.py:15
  8.2 10.9 %collective-permute-start.10 = (f32[32,1024]{1,0:T(8,128)S(1)}, f32[32,1024]{1,0:T(8,128)S(1)}, u32[]{:S(2)}, u32[]{:S(2)}) collective-permute-start(f32[32,1024]{1,0:T(8,128)S(1)} %get-tuple-element.27), channel_id=1, source_target_pairs={{0,4},{1,5},{2,6},{3,7},{4,0},{5,1},{6,2},{7,3},{8,12},{9,13},{10,... | collective-permute-start | bytes 393224 | tf_op jit(solution)/shard_map/ppermute | solution.py:15
  9.1 12.8 %collective-permute-start.1 = (f32[512,128]{1,0:T(8,128)S(1)}, f32[512,128]{1,0:T(8,128)S(1)}, u32[]{:S(2)}, u32[]{:S(2)}) collective-permute-start(f32[512,128]{1,0:T(8,128)S(1)} %copy-done.2), channel_id=1, source_target_pairs={{0,16},{8,24},{16,0},{24,8},{1,17},{9,25},{17,1},{25,9},{2,18},{10... | collective-permute-start | bytes 786440 | tf_op jit(solution)/shard_map/ppermute | solution.py:15
  12.8 9.1 %collective-permute-start.2 = (f32[512,128]{1,0:T(8,128)S(1)}, f32[512,128]{1,0:T(8,128)S(1)}, u32[]{:S(2)}, u32[]{:S(2)}) collective-permute-start(f32[512,128]{1,0:T(8,128)S(1)} %copy-done.2), channel_id=1, source_target_pairs={{0,24},{8,16},{16,8},{24,0},{1,25},{9,17},{17,9},{25,1},{2,26},{10... | collective-permute-start | bytes 786440 | tf_op jit(solution)/shard_map/ppermute | solution.py:15
  19.1 6.9 %collective-permute-start.3 = (f32[64,1024]{1,0:T(8,128)S(1)}, f32[64,1024]{1,0:T(8,128)S(1)}, u32[]{:S(2)}, u32[]{:S(2)}) collective-permute-start(f32[64,1024]{1,0:T(8,128)S(1)} %copy-done), channel_id=1, source_target_pairs={{0,1},{1,0},{2,3},{3,2},{4,5},{5,4},{6,7},{7,6},{8,9},{9,8},{10,11... | collective-permute-start | bytes 786440 | tf_op jit(solution)/shard_map/ppermute | solution.py:15
  19.1 9.7 %collective-permute-start.5 = (f32[64,1024]{1,0:T(8,128)S(1)}, f32[64,1024]{1,0:T(8,128)S(1)}, u32[]{:S(2)}, u32[]{:S(2)}) collective-permute-start(f32[64,1024]{1,0:T(8,128)S(1)} %collective-permute-done.4.refs_2_), channel_id=1, source_target_pairs={{0,1},{1,0},{2,3},{3,2},{4,5},{5,4},{6,7},{7,6},{8,9},{9,8},{10,11... | collective-permute-start | bytes 786440 | tf_op jit(solution)/shard_map/ppermute | solution.py:15
  19.6 6.4 %collective-permute-start.8 = (f32[32,1024]{1,0:T(8,128)S(1)}, f32[32,1024]{1,0:T(8,128)S(1)}, u32[]{:S(2)}, u32[]{:S(2)}) collective-permute-start(f32[32,1024]{1,0:T(8,128)S(1)} %collective-permute-done.6.refs_0_), channel_id=1, source_target_pairs={{0,2},{1,3},{2,0},{3,1},{4,6},{5,7},{6,4},{7,5},{8,10},{9,11},{10,... | collective-permute-start | bytes 393224 | tf_op jit(solution)/shard_map/ppermute | solution.py:15
  21.9 6.0 %collective-permute-start.12 = (f32[32,1024]{1,0:T(8,128)S(1)}, f32[32,1024]{1,0:T(8,128)S(1)}, u32[]{:S(2)}, u32[]{:S(2)}) collective-permute-start(f32[32,1024]{1,0:T(8,128)S(1)} %collective-permute-done.10.refs_0_), channel_id=1, source_target_pairs={{0,2},{1,3},{2,0},{3,1},{4,6},{5,7},{6,4},{7,5},{8,10},{9,11},{10,... | collective-permute-start | bytes 393224 | tf_op jit(solution)/shard_map/ppermute | solution.py:15
  21.9 7.0 %collective-permute-start.7 = (f32[32,1024]{1,0:T(8,128)S(1)}, f32[32,1024]{1,0:T(8,128)S(1)}, u32[]{:S(2)}, u32[]{:S(2)}) collective-permute-start(f32[32,1024]{1,0:T(8,128)S(1)} %collective-permute-done.6.refs_0_), channel_id=1, source_target_pairs={{0,1},{1,0},{2,3},{3,2},{4,5},{5,4},{6,7},{7,6},{8,9},{9,8},{10,11... | collective-permute-start | bytes 393224 | tf_op jit(solution)/shard_map/ppermute | solution.py:15
  26.0 2.9 %collective-permute-start.9 = (f32[32,1024]{1,0:T(8,128)S(1)}, f32[32,1024]{1,0:T(8,128)S(1)}, u32[]{:S(2)}, u32[]{:S(2)}) collective-permute-start(f32[32,1024]{1,0:T(8,128)S(1)} %collective-permute-done.8.refs_2_), channel_id=1, source_target_pairs={{0,1},{1,0},{2,3},{3,2},{4,5},{5,4},{6,7},{7,6},{8,9},{9,8},{10,11... | collective-permute-start | bytes 393224 | tf_op jit(solution)/shard_map/ppermute | solution.py:15
  26.0 6.0 %collective-permute-start.11 = (f32[32,1024]{1,0:T(8,128)S(1)}, f32[32,1024]{1,0:T(8,128)S(1)}, u32[]{:S(2)}, u32[]{:S(2)}) collective-permute-start(f32[32,1024]{1,0:T(8,128)S(1)} %collective-permute-done.10.refs_0_), channel_id=1, source_target_pairs={{0,1},{1,0},{2,3},{3,2},{4,5},{5,4},{6,7},{7,6},{8,9},{9,8},{10,11... | collective-permute-start | bytes 393224 | tf_op jit(solution)/shard_map/ppermute | solution.py:15
  27.9 4.1 %collective-permute-start.13 = (f32[32,1024]{1,0:T(8,128)S(1)}, f32[32,1024]{1,0:T(8,128)S(1)}, u32[]{:S(2)}, u32[]{:S(2)}) collective-permute-start(f32[32,1024]{1,0:T(8,128)S(1)} %collective-permute-done.12.refs_2_), channel_id=1, source_target_pairs={{0,1},{1,0},{2,3},{3,2},{4,5},{5,4},{6,7},{7,6},{8,9},{9,8},{10,11... | collective-permute-start | bytes 393224 | tf_op jit(solution)/shard_map/ppermute | solution.py:15
  27.9 1.0 %copy-start.1 = (f32[64,1024]{1,0:T(8,128)S(1)}, f32[64,1024]{1,0:T(8,128)}, u32[]{:S(2)}) copy-start(f32[64,1024]{1,0:T(8,128)} %refs_0_.5) | copy-start | bytes 786436
  29.5 12.1 %collective-permute-start.14 = (f32[256,128]{1,0:T(8,128)S(1)}, f32[256,128]{1,0:T(8,128)S(1)}, u32[]{:S(2)}, u32[]{:S(2)}) collective-permute-start(f32[256,128]{1,0:T(8,128)S(1)} %get-tuple-element.24.refs_0_), channel_id=1, source_target_pairs={{0,16},{8,24},{16,0},{24,8},{1,17},{9,25},{17,1},{25,9},{2,18},{10... | collective-permute-start | bytes 393224 | tf_op jit(solution)/shard_map/ppermute | solution.py:15
  30.6 10.9 %collective-permute-start.15 = (f32[256,128]{1,0:T(8,128)S(1)}, f32[256,128]{1,0:T(8,128)S(1)}, u32[]{:S(2)}, u32[]{:S(2)}) collective-permute-start(f32[256,128]{1,0:T(8,128)S(1)} %get-tuple-element.24.refs_0_), channel_id=1, source_target_pairs={{0,24},{8,16},{16,8},{24,0},{1,25},{9,17},{17,9},{25,1},{2,26},{10... | collective-permute-start | bytes 393224 | tf_op jit(solution)/shard_map/ppermute | solution.py:15
  32.5 11.4 %collective-permute-start.16 = (f32[256,128]{1,0:T(8,128)S(1)}, f32[256,128]{1,0:T(8,128)S(1)}, u32[]{:S(2)}, u32[]{:S(2)}) collective-permute-start(f32[256,128]{1,0:T(8,128)S(1)} %get-tuple-element.28.refs_1_), channel_id=1, source_target_pairs={{0,16},{8,24},{16,0},{24,8},{1,17},{9,25},{17,1},{25,9},{2,18},{10... | collective-permute-start | bytes 393224 | tf_op jit(solution)/shard_map/ppermute | solution.py:15
  33.3 10.6 %collective-permute-start.17 = (f32[256,128]{1,0:T(8,128)S(1)}, f32[256,128]{1,0:T(8,128)S(1)}, u32[]{:S(2)}, u32[]{:S(2)}) collective-permute-start(f32[256,128]{1,0:T(8,128)S(1)} %get-tuple-element.28.refs_1_), channel_id=1, source_target_pairs={{0,24},{8,16},{16,8},{24,0},{1,25},{9,17},{17,9},{25,1},{2,26},{10... | collective-permute-start | bytes 393224 | tf_op jit(solution)/shard_map/ppermute | solution.py:15

commit v4 on v3

--- a/solution.py
+++ b/solution.py
@@ -84,64 +84,74 @@
         ref[...] = panel_ref[pl.ds(i * unit, unit), :]
 
 
-def collect(order, unit, chunk, me, pieces, high, low):
-    for mask, ref in zip(order, pieces):
-        at = pl.ds(pl.multiple_of((me ^ mask) * unit, unit), unit)
-        start = 0 if ref.shape[0] == unit else chunk * unit
-        high[at, :], low[at, :] = halves(ref[pl.ds(start, unit), :])
-
-
-def early(order, unit, chunk, *refs):
+def collect(pieces, high, low):
+    start = 0
+    for ref in pieces:
+        at = pl.ds(start, ref.shape[0])
+        high[at, :], low[at, :] = halves(ref[...])
+        start += ref.shape[0]
+
+
+def early(*refs):
     *pieces, high, low = refs
-    collect(order, unit, chunk, lax.axis_index("pcol"), pieces, high, low)
-
-
-def solve(sources, order, unit, chunk, top_ref, early_high, early_low, *refs):
-    *pieces, out_ref, high, low = refs
-    for mask in range(order[0]):
-        at = pl.ds(pl.multiple_of((lax.axis_index("pcol") ^ mask) * unit, unit), unit)
-        high[at, :], low[at, :] = early_high[at, :], early_low[at, :]
-    collect(order, unit, chunk, lax.axis_index("pcol"), pieces, high, low)
+    collect(pieces, high, low)
+
+
+def solve(ready, sources, top_ref, *refs):
+    *refs, out_ref, high, low = refs
+    ready, pieces = refs[: 2 * ready], refs[2 * ready :]
+    collect(pieces, high, low)
 
     @pl.when(lax.axis_index("prow") < sources)
     def _():
-        out_ref[...] = product(high[...], low[...], top_ref[...])
-
-
-def update(sources, masks, chunks, n_cols, own_ref, *refs):
-    solved, refs = refs[:chunks], refs[chunks:]
-    split, refs = refs[: 2 * chunks], refs[2 * chunks :]
+        start = 0
+        for high_ref, low_ref in (*zip(ready[::2], ready[1::2]), (high, low)):
+            at = pl.ds(start, high_ref.shape[0])
+            out_ref[at, :] = product(high_ref[...], low_ref[...], top_ref[...])
+            start += high_ref.shape[0]
+
+
+def update(sources, masks, groups, n_split, own_ref, *refs):
+    solved, refs = refs[: len(groups)], refs[len(groups) :]
+    split, refs = refs[: 2 * n_split], refs[2 * n_split :]
     *got, out_ref, upper = refs
     rows, _ = own_ref.shape
-    depth = rows // n_cols
-    unit = depth // chunks
-    me = lax.axis_index("prow")
-
-    @pl.when(me < sources)
-    def _():
-        for chunk in range(chunks):
-            for i in range(n_cols):
-                out_ref[pl.ds(i * depth + chunk * unit, unit), :] = solved[chunk][pl.ds(i * unit, unit), :]
-
-    @pl.when(me >= sources)
+    row, col = lax.axis_index("prow"), lax.axis_index("pcol")
+    depth = rows // lax.axis_size("pcol")
+
+    def places(group):
+        start = 0
+        for mask, first, count in group:
+            yield pl.multiple_of((col ^ mask) * depth + first, count), start, count
+            start += count
+
+    @pl.when(row < sources)
+    def _():
+        for group, ref in zip(groups, solved):
+            for at, start, count in places(group):
+                out_ref[pl.ds(at, count), :] = ref[pl.ds(start, count), :]
+
+    @pl.when(row >= sources)
     def _():
         for m, mask in enumerate(masks):
-            source = me ^ mask
+            source = row ^ mask
 
             @pl.when(source < sources)
             def _():
-                for chunk in range(chunks):
-                    ref = got[chunk * len(masks) + m]
-                    for i in range(n_cols):
-                        at = pl.multiple_of(source * rows, rows) + (i * depth + chunk * unit)
-                        upper[pl.ds(pl.multiple_of(at, unit), unit), :] = ref[pl.ds(i * unit, unit), :]
+                for g, group in enumerate(groups):
+                    ref = got[g * len(masks) + m]
+                    for at, start, count in places(group):
+                        at = pl.multiple_of(source * rows + at, count)
+                        upper[pl.ds(at, count), :] = ref[pl.ds(start, count), :]
 
         pair = jnp.concatenate(halves(upper[...]), axis=1)
-        for chunk in range(chunks):
-            part = product(split[2 * chunk][...], split[2 * chunk + 1][...], pair)
-            for i in range(n_cols):
-                at = pl.ds(i * depth + chunk * unit, unit)
-                out_ref[at, :] = own_ref[at, :] - part[i * unit : (i + 1) * unit]
+        done = jnp.concatenate([product(split[2 * i][...], split[2 * i + 1][...], pair) for i in range(n_split)], axis=0)
+        base = 0
+        for group in groups:
+            for at, start, count in places(group):
+                at = pl.ds(at, count)
+                out_ref[at, :] = own_ref[at, :] - done[base + start : base + start + count]
+            base += sum(count for _, _, count in group)
 
 
 def per_device(matrix, panel, pivots):
@@ -158,17 +168,19 @@
     if chunks > 1:
         parts = call(cut, [pltpu.VMEM((unit, block), f32)] * chunks, [], panel)
 
-    def both(pieces):
-        return [got for piece in pieces for got in (piece, swap(piece, "pcol", 1))]
-
-    near = both([panel, swap(panel, "pcol", 2)])
-    far = []
-    for chunk in range(chunks):
-        pieces = []
-        for mask in range(4, n_cols, 4):
-            pieces.append(swap(parts[chunk], "pcol", mask))
-            pieces.append(swap(pieces[-1], "pcol", 2))
-        far.append(both(pieces))
+    def both(piece):
+        return [piece, swap(piece, "pcol", 1)]
+
+    near = both(panel) + both(swap(panel, "pcol", 2))
+    near_at = [(mask, 0, depth) for mask in range(4)]
+    far, relayed, far_at, relayed_at = [], [], [], []
+    for mask in range(4, n_cols, 4):
+        for chunk in range(chunks):
+            piece = swap(parts[chunk], "pcol", mask)
+            far += both(piece)
+            far_at += [(mask, chunk * unit, unit), (mask + 1, chunk * unit, unit)]
+            relayed += both(swap(piece, "pcol", 2))
+            relayed_at += [(mask + 2, chunk * unit, unit), (mask + 3, chunk * unit, unit)]
     blocks = [matrix] + [swap(matrix, "prow", mask) for mask in range(1, n_rows)]
 
     top, own = call(
@@ -178,26 +190,28 @@
         pivots.reshape(1, block), *blocks,
     )
 
+    def terms(group):
+        return [pltpu.VMEM((sum(count for _, _, count in group), block), bf16)] * 2
+
+    def result(group):
+        return [pltpu.VMEM((sum(count for _, _, count in group), cols), f32)]
+
+    groups = (near_at, far_at + relayed_at)
+    first, *split0 = call(functools.partial(solve, 0, sources), result(near_at) + terms(near_at), [], top, *near)
+    split1 = call(early, terms(far_at), [], *far)
+    second, *split2 = call(
+        functools.partial(solve, 1, sources), result(groups[1]) + terms(relayed_at), [],
+        top, *split1, *relayed,
+    )
     masks = tuple(range(sources, n_rows))
-    solved, split, got = [], [], []
-    for chunk in range(chunks):
-        terms = [pltpu.VMEM((rows // chunks, block), bf16)] * 2
-        high, low = call(functools.partial(early, range(len(near)), unit, chunk), terms, [], *near)
-        piece, high, low = call(
-            functools.partial(solve, sources, tuple(range(len(near), n_cols)), unit, chunk),
-            [pltpu.VMEM((rows // chunks, cols), f32)] + terms,
-            [],
-            top, high, low, *far[chunk],
-        )
-        solved.append(piece)
-        split += [high, low]
-        got += [swap(piece, "prow", mask) for mask in masks]
+    solved = [first, second]
+    got = [swap(piece, "prow", mask) for piece in solved for mask in masks]
 
     return call(
-        functools.partial(update, sources, masks, chunks, n_cols),
+        functools.partial(update, sources, masks, groups, 3),
         jax.ShapeDtypeStruct((rows, cols), f32),
         [pltpu.VMEM((block, cols), f32)],
-        own, *solved, *split, *got,
+        own, *solved, *split0, *split1, *split2, *got,
     )
 
 

time: 44.8 us -> 47.8 us (1.067)
  waiting for transfers between devices: 22.5 us -> 25.6 us
  Pallas kernels: 2.86 us -> 4.72 us
  local copies, waits for them, and re-layouts: 1.03 us -> 0.01 us
  starting transfers between devices: 18.1 us -> 17.2 us
    ppermute x18, waiting for transfers between devices: 22.5 us -> 25.6 us  [swap(): lax.ppermute(block, axis, [(i, i ^ mask) for i in range(lax.axis_size(axi...]
    pallas_call x7 -> x6, Pallas kernels: 2.86 us -> 4.72 us  [call(): pl.pallas_call(kernel, out_shape=out_shape, in_specs=[VMEM] * len(args),...]
    unnamed x8 -> x4, local copies, waits for them, and re-layouts: 1.03 us -> 0.01 us
    ppermute x18, starting transfers between devices: 18.1 us -> 17.2 us  [swap(): lax.ppermute(block, axis, [(i, i ^ mask) for i in range(lax.axis_size(axi...]
  transfers between devices with their start and end apart: 18 -> 18, of which waited for: 7 -> 7; matrix products, arithmetic and copies ran while one was open for 0% -> 0% of each run, Pallas kernels for 5% -> 8%
where the time goes in v4:
time: 47.8 us; the launch traced here: 47.6 us
  waiting for transfers between devices  25.6 us (54%)
  starting transfers between devices  17.2 us (36%)
  Pallas kernels  4.72 us (10%)
    ppermute x18, waiting for transfers between devices, swap(): lax.ppermute(block, axis, [(i, i ^ mask) for i in range(lax.axis_size(axi...  25.6 us
    ppermute x18, starting transfers between devices, swap(): lax.ppermute(block, axis, [(i, i ^ mask) for i in range(lax.axis_size(axi...  17.2 us
    pallas_call x6, Pallas kernels, call(): pl.pallas_call(kernel, out_shape=out_shape, in_specs=[VMEM] * len(args),...  4.72 us
  transfers between devices with their start and end apart: 18, of which 7 were waited for; matrix products, arithmetic and copies ran while one was open for 0% of the time, Pallas kernels for 8%

profile of v4, /device:TPU:0, one launch (start us, length us, event | category | flops | bytes accessed | tf_op | source)
XLA Modules:
  0.0 47.6 jit_solution(8825074640186114093)
XLA Ops:
  0.0 0.0 copy-start
  0.0 3.0 %collective-permute-start = (f32[512,128]{1,0:T(8,128)}, f32[512,128]{1,0:T(8,128)S(1)}, u32[]{:S(2)}, u32[]{:S(2)}) collective-permute-start(f32[512,128]{1,0:T(8,128)} %refs_0_.2), channel_id=1, source_target_pairs={{0,8},{8,0},{16,24},{24,16},{1,9},{9,1},{17,25},{25,17},{2,10},{10... | collective-permute-start | bytes 786440 | tf_op jit(solution)/shard_map/ppermute | solution.py:15
  3.0 1.5 %collective-permute-start.1 = (f32[512,128]{1,0:T(8,128)}, f32[512,128]{1,0:T(8,128)S(1)}, u32[]{:S(2)}, u32[]{:S(2)}) collective-permute-start(f32[512,128]{1,0:T(8,128)} %refs_0_.2), channel_id=1, source_target_pairs={{0,16},{8,24},{16,0},{24,8},{1,17},{9,25},{17,1},{25,9},{2,18},{10... | collective-permute-start | bytes 786440 | tf_op jit(solution)/shard_map/ppermute | solution.py:15
  4.5 1.6 %collective-permute-start.4 = (f32[64,1024]{1,0:T(8,128)}, f32[64,1024]{1,0:T(8,128)S(1)}, u32[]{:S(2)}, u32[]{:S(2)}) collective-permute-start(f32[64,1024]{1,0:T(8,128)} %panel_ref.1), channel_id=1, source_target_pairs={{0,2},{1,3},{2,0},{3,1},{4,6},{5,7},{6,4},{7,5},{8,10},{9,11},{10,... | collective-permute-start | bytes 786440 | tf_op jit(solution)/shard_map/ppermute | solution.py:15
  6.1 1.0 %shard_map.39 = (f32[32,1024]{1,0:T(8,128)S(1)}, f32[32,1024]{1,0:T(8,128)S(1)}) custom-call(f32[64,1024]{1,0:T(8,128)} %panel_ref.1), custom_call_target="tpu_custom_call" | custom-call | tf_op jit(solution)/shard_map/pallas_call | solution.py:19
  7.1 2.7 %collective-permute-start.6 = (f32[32,1024]{1,0:T(8,128)S(1)}, f32[32,1024]{1,0:T(8,128)S(1)}, u32[]{:S(2)}, u32[]{:S(2)}) collective-permute-start(f32[32,1024]{1,0:T(8,128)S(1)} %get-tuple-element.20), channel_id=1, source_target_pairs={{0,4},{1,5},{2,6},{3,7},{4,0},{5,1},{6,2},{7,3},{8,12},{9,13},{10,... | collective-permute-start | bytes 393224 | tf_op jit(solution)/shard_map/ppermute | solution.py:15
  9.7 0.3 collective-permute-start.8
  10.1 5.6 %collective-permute-done.6.refs_0_ = f32[32,1024]{1,0:T(8,128)S(1)} collective-permute-done((f32[32,1024]{1,0:T(8,128)S(1)}, f32[32,1024]{1,0:T(8,128)S(1)}, u32[]{:S(2)}, u32[]{:S(2)}) %collective-permute-start.6) | collective-permute-done | bytes 131104 | tf_op jit(solution)/shard_map/ppermute | solution.py:15
  15.6 0.0 collective-permute-start.7
  15.6 5.8 %collective-permute-done.8.refs_2_ = f32[32,1024]{1,0:T(8,128)S(1)} collective-permute-done((f32[32,1024]{1,0:T(8,128)S(1)}, f32[32,1024]{1,0:T(8,128)S(1)}, u32[]{:S(2)}, u32[]{:S(2)}) %collective-permute-start.8) | collective-permute-done | bytes 131104 | tf_op jit(solution)/shard_map/ppermute | solution.py:15
  21.4 0.0 collective-permute-start.9
  21.4 0.0 collective-permute-done.refs_1_
  21.4 0.0 copy-done
  21.4 0.5 %collective-permute-start.2 = (f32[512,128]{1,0:T(8,128)S(1)}, f32[512,128]{1,0:T(8,128)S(1)}, u32[]{:S(2)}, u32[]{:S(2)}) collective-permute-start(f32[512,128]{1,0:T(8,128)S(1)} %copy-done), channel_id=1, source_target_pairs={{0,24},{8,16},{16,8},{24,0},{1,25},{9,17},{17,9},{25,1},{2,26},{10... | collective-permute-start | bytes 786440 | tf_op jit(solution)/shard_map/ppermute | solution.py:15
  22.0 0.0 collective-permute-done.1.refs_2_
  22.0 0.0 collective-permute-start.10
  22.0 0.0 collective-permute-done.4.refs_2_
  22.0 2.0 %collective-permute-start.12 = (f32[32,1024]{1,0:T(8,128)S(1)}, f32[32,1024]{1,0:T(8,128)S(1)}, u32[]{:S(2)}, u32[]{:S(2)}) collective-permute-start(f32[32,1024]{1,0:T(8,128)S(1)} %collective-permute-done.8.refs_2_), channel_id=1, source_target_pairs={{0,2},{1,3},{2,0},{3,1},{4,6},{5,7},{6,4},{7,5},{8,10},{9,11},{10,... | collective-permute-start | bytes 393224 | tf_op jit(solution)/shard_map/ppermute | solution.py:15
  24.0 0.0 collective-permute-done.7.refs_1_
  24.0 0.0 collective-permute-start.3
  24.0 0.0 collective-permute-done.9.refs_3_
  24.0 0.5 %collective-permute-start.5 = (f32[64,1024]{1,0:T(8,128)S(1)}, f32[64,1024]{1,0:T(8,128)S(1)}, u32[]{:S(2)}, u32[]{:S(2)}) collective-permute-start(f32[64,1024]{1,0:T(8,128)S(1)} %collective-permute-done.4.refs_2_), channel_id=1, source_target_pairs={{0,1},{1,0},{2,3},{3,2},{4,5},{5,4},{6,7},{7,6},{8,9},{9,8},{10,11... | collective-permute-start | bytes 786440 | tf_op jit(solution)/shard_map/ppermute | solution.py:15
  24.5 3.8 %collective-permute-done.10.refs_2_ = f32[32,1024]{1,0:T(8,128)S(1)} collective-permute-done((f32[32,1024]{1,0:T(8,128)S(1)}, f32[32,1024]{1,0:T(8,128)S(1)}, u32[]{:S(2)}, u32[]{:S(2)}) %collective-permute-start.10) | collective-permute-done | bytes 131104 | tf_op jit(solution)/shard_map/ppermute | solution.py:15
  28.4 0.0 collective-permute-start.11
  28.4 2.0 %collective-permute-done.12.refs_4_ = f32[32,1024]{1,0:T(8,128)S(1)} collective-permute-done((f32[32,1024]{1,0:T(8,128)S(1)}, f32[32,1024]{1,0:T(8,128)S(1)}, u32[]{:S(2)}, u32[]{:S(2)}) %collective-permute-start.12) | collective-permute-done | bytes 131104 | tf_op jit(solution)/shard_map/ppermute | solution.py:15
  30.4 0.0 collective-permute-start.13
  30.4 0.0 copy-start.1
  30.4 0.1 shard_map.40
  30.4 0.6 %collective-permute-done.2.refs_3_ = f32[512,128]{1,0:T(8,128)S(1)} collective-permute-done((f32[512,128]{1,0:T(8,128)S(1)}, f32[512,128]{1,0:T(8,128)S(1)}, u32[]{:S(2)}, u32[]{:S(2)}) %collective-permute-start.2) | collective-permute-done | bytes 262176 | tf_op jit(solution)/shard_map/ppermute | solution.py:15
  31.1 0.0 copy-done.1
  31.1 0.9 %shard_map.37 = (bf16[1024,256]{1,0:T(8,128)(2,1)S(1)}, f32[512,128]{1,0:T(8,128)S(1)}) custom-call(s32[1,1024]{1,0:T(1,128)S(1)} %bitcast.1, f32[512,128]{1,0:T(8,128)S(1)} %copy-done, f32[512,128]{1,0:T(8,128)S(1)} %collective-permute-done.refs_1_, f32[512,128]{1,0:T(8,128)S(1)} %collective-permute-done.1.refs_2_, ...), custom_call_target="tpu_custom_call" | custom-call | tf_op jit(solution)/shard_map/pallas_call | solution.py:19
  32.0 0.0 collective-permute-done.11.refs_3_
  32.0 0.0 collective-permute-done.13.refs_5_
  32.0 0.5 %shard_map.41 = (f32[256,128]{1,0:T(8,128)S(1)}, bf16[128,1024]{1,0:T(8,128)(2,1)S(1)}, bf16[128,1024]{1,0:T(8,128)(2,1)S(1)}) custom-call(bf16[1024,256]{1,0:T(8,128)(2,1)S(1)} %get-tuple-element.18.top_ref, bf16[128,1024]{1,0:T(8,128)(2,1)S(1)} %get-tuple-element.22.refs_0_.refs_4_, bf16[128,1024]{1,0:T(8,128)(2,1)S(1)} %get-tuple-element.23.refs_1_.refs_5_, ...), custom_call_target="tpu_custom_call" | custom-call | tf_op jit(solution)/shard_map/pallas_call | solution.py:19
  32.5 1.1 %collective-permute-start.16 = (f32[256,128]{1,0:T(8,128)S(1)}, f32[256,128]{1,0:T(8,128)S(1)}, u32[]{:S(2)}, u32[]{:S(2)}) collective-permute-start(f32[256,128]{1,0:T(8,128)S(1)} %get-tuple-element.24.refs_1_), channel_id=1, source_target_pairs={{0,16},{8,24},{16,0},{24,8},{1,17},{9,25},{17,1},{25,9},{2,18},{10... | collective-permute-start | bytes 393224 | tf_op jit(solution)/shard_map/ppermute | solution.py:15
  33.6 1.9 %collective-permute-start.17 = (f32[256,128]{1,0:T(8,128)S(1)}, f32[256,128]{1,0:T(8,128)S(1)}, u32[]{:S(2)}, u32[]{:S(2)}) collective-permute-start(f32[256,128]{1,0:T(8,128)S(1)} %get-tuple-element.24.refs_1_), channel_id=1, source_target_pairs={{0,24},{8,16},{16,8},{24,0},{1,25},{9,17},{17,9},{25,1},{2,26},{10... | collective-permute-start | bytes 393224 | tf_op jit(solution)/shard_map/ppermute | solution.py:15
  35.5 0.0 collective-permute-done.3.refs_1_
  35.5 0.0 collective-permute-done.5.refs_3_
  35.5 1.5 %shard_map.38 = (f32[256,128]{1,0:T(8,128)S(1)}, bf16[256,1024]{1,0:T(8,128)(2,1)S(1)}, bf16[256,1024]{1,0:T(8,128)(2,1)S(1)}) custom-call(bf16[1024,256]{1,0:T(8,128)(2,1)S(1)} %get-tuple-element.18.top_ref, f32[64,1024]{1,0:T(8,128)} %panel_ref.1, f32[64,1024]{1,0:T(8,128)S(1)} %collective-permute-done.3.refs_1_, ...), custom_call_target="tpu_custom_call" | custom-call | tf_op jit(solution)/shard_map/pallas_call | solution.py:19
  37.0 0.7 %collective-permute-start.14 = (f32[256,128]{1,0:T(8,128)S(1)}, f32[256,128]{1,0:T(8,128)S(1)}, u32[]{:S(2)}, u32[]{:S(2)}) collective-permute-start(f32[256,128]{1,0:T(8,128)S(1)} %get-tuple-element.19.refs_0_), channel_id=1, source_target_pairs={{0,16},{8,24},{16,0},{24,8},{1,17},{9,25},{17,1},{25,9},{2,18},{10... | collective-permute-start | bytes 393224 | tf_op jit(solution)/shard_map/ppermute | solution.py:15
  37.7 1.4 %collective-permute-start.15 = (f32[256,128]{1,0:T(8,128)S(1)}, f32[256,128]{1,0:T(8,128)S(1)}, u32[]{:S(2)}, u32[]{:S(2)}) collective-permute-start(f32[256,128]{1,0:T(8,128)S(1)} %get-tuple-element.19.refs_0_), channel_id=1, source_target_pairs={{0,24},{8,16},{16,8},{24,0},{1,25},{9,17},{17,9},{25,1},{2,26},{10... | collective-permute-start | bytes 393224 | tf_op jit(solution)/shard_map/ppermute | solution.py:15
  39.1 5.4 %collective-permute-done.16.refs_10_ = f32[256,128]{1,0:T(8,128)S(1)} collective-permute-done((f32[256,128]{1,0:T(8,128)S(1)}, f32[256,128]{1,0:T(8,128)S(1)}, u32[]{:S(2)}, u32[]{:S(2)}) %collective-permute-start.16) | collective-permute-done | bytes 131104 | tf_op jit(solution)/shard_map/ppermute | solution.py:15
  44.5 0.0 collective-permute-done.17.refs_11_
  44.5 2.3 %collective-permute-done.14.refs_8_ = f32[256,128]{1,0:T(8,128)S(1)} collective-permute-done((f32[256,128]{1,0:T(8,128)S(1)}, f32[256,128]{1,0:T(8,128)S(1)}, u32[]{:S(2)}, u32[]{:S(2)}) %collective-permute-start.14) | collective-permute-done | bytes 131104 | tf_op jit(solution)/shard_map/ppermute | solution.py:15
  46.9 0.0 collective-permute-done.15.refs_9_
  46.9 0.7 %shard_map.42 = f32[512,128]{1,0:T(8,128)} custom-call(f32[512,128]{1,0:T(8,128)S(1)} %get-tuple-element.17.own_ref, f32[256,128]{1,0:T(8,128)S(1)} %get-tuple-element.19.refs_0_, f32[256,128]{1,0:T(8,128)S(1)} %get-tuple-element.24.refs_1_, bf16[256,1024]{1,0:T(8,128)(2,1)S(1)} %get-tuple-element.25.refs_2_, ...), custom_call_target="tpu_custom_call" | custom-call | tf_op jit(solution)/shard_map/pallas_call | solution.py:19
Async XLA Ops:
  0.0 21.4 %copy-start = (f32[512,128]{1,0:T(8,128)S(1)}, f32[512,128]{1,0:T(8,128)}, u32[]{:S(2)}) copy-start(f32[512,128]{1,0:T(8,128)} %refs_0_.2) | copy-start | bytes 786436
  0.0 21.4 %collective-permute-start = (f32[512,128]{1,0:T(8,128)}, f32[512,128]{1,0:T(8,128)S(1)}, u32[]{:S(2)}, u32[]{:S(2)}) collective-permute-start(f32[512,128]{1,0:T(8,128)} %refs_0_.2), channel_id=1, source_target_pairs={{0,8},{8,0},{16,24},{24,16},{1,9},{9,1},{17,25},{25,17},{2,10},{10... | collective-permute-start | bytes 786440 | tf_op jit(solution)/shard_map/ppermute | solution.py:15
  3.0 19.0 %collective-permute-start.1 = (f32[512,128]{1,0:T(8,128)}, f32[512,128]{1,0:T(8,128)S(1)}, u32[]{:S(2)}, u32[]{:S(2)}) collective-permute-start(f32[512,128]{1,0:T(8,128)} %refs_0_.2), channel_id=1, source_target_pairs={{0,16},{8,24},{16,0},{24,8},{1,17},{9,25},{17,1},{25,9},{2,18},{10... | collective-permute-start | bytes 786440 | tf_op jit(solution)/shard_map/ppermute | solution.py:15
  4.5 17.5 %collective-permute-start.4 = (f32[64,1024]{1,0:T(8,128)}, f32[64,1024]{1,0:T(8,128)S(1)}, u32[]{:S(2)}, u32[]{:S(2)}) collective-permute-start(f32[64,1024]{1,0:T(8,128)} %panel_ref.1), channel_id=1, source_target_pairs={{0,2},{1,3},{2,0},{3,1},{4,6},{5,7},{6,4},{7,5},{8,10},{9,11},{10,... | collective-permute-start | bytes 786440 | tf_op jit(solution)/shard_map/ppermute | solution.py:15
  7.1 8.6 %collective-permute-start.6 = (f32[32,1024]{1,0:T(8,128)S(1)}, f32[32,1024]{1,0:T(8,128)S(1)}, u32[]{:S(2)}, u32[]{:S(2)}) collective-permute-start(f32[32,1024]{1,0:T(8,128)S(1)} %get-tuple-element.20), channel_id=1, source_target_pairs={{0,4},{1,5},{2,6},{3,7},{4,0},{5,1},{6,2},{7,3},{8,12},{9,13},{10,... | collective-permute-start | bytes 393224 | tf_op jit(solution)/shard_map/ppermute | solution.py:15
  9.7 11.7 %collective-permute-start.8 = (f32[32,1024]{1,0:T(8,128)S(1)}, f32[32,1024]{1,0:T(8,128)S(1)}, u32[]{:S(2)}, u32[]{:S(2)}) collective-permute-start(f32[32,1024]{1,0:T(8,128)S(1)} %get-tuple-element.21), channel_id=1, source_target_pairs={{0,4},{1,5},{2,6},{3,7},{4,0},{5,1},{6,2},{7,3},{8,12},{9,13},{10,... | collective-permute-start | bytes 393224 | tf_op jit(solution)/shard_map/ppermute | solution.py:15
  15.6 8.4 %collective-permute-start.7 = (f32[32,1024]{1,0:T(8,128)S(1)}, f32[32,1024]{1,0:T(8,128)S(1)}, u32[]{:S(2)}, u32[]{:S(2)}) collective-permute-start(f32[32,1024]{1,0:T(8,128)S(1)} %collective-permute-done.6.refs_0_), channel_id=1, source_target_pairs={{0,1},{1,0},{2,3},{3,2},{4,5},{5,4},{6,7},{7,6},{8,9},{9,8},{10,11... | collective-permute-start | bytes 393224 | tf_op jit(solution)/shard_map/ppermute | solution.py:15
  21.4 2.6 %collective-permute-start.9 = (f32[32,1024]{1,0:T(8,128)S(1)}, f32[32,1024]{1,0:T(8,128)S(1)}, u32[]{:S(2)}, u32[]{:S(2)}) collective-permute-start(f32[32,1024]{1,0:T(8,128)S(1)} %collective-permute-done.8.refs_2_), channel_id=1, source_target_pairs={{0,1},{1,0},{2,3},{3,2},{4,5},{5,4},{6,7},{7,6},{8,9},{9,8},{10,11... | collective-permute-start | bytes 393224 | tf_op jit(solution)/shard_map/ppermute | solution.py:15
  21.4 9.6 %collective-permute-start.2 = (f32[512,128]{1,0:T(8,128)S(1)}, f32[512,128]{1,0:T(8,128)S(1)}, u32[]{:S(2)}, u32[]{:S(2)}) collective-permute-start(f32[512,128]{1,0:T(8,128)S(1)} %copy-done), channel_id=1, source_target_pairs={{0,24},{8,16},{16,8},{24,0},{1,25},{9,17},{17,9},{25,1},{2,26},{10... | collective-permute-start | bytes 786440 | tf_op jit(solution)/shard_map/ppermute | solution.py:15
  22.0 6.4 %collective-permute-start.10 = (f32[32,1024]{1,0:T(8,128)S(1)}, f32[32,1024]{1,0:T(8,128)S(1)}, u32[]{:S(2)}, u32[]{:S(2)}) collective-permute-start(f32[32,1024]{1,0:T(8,128)S(1)} %collective-permute-done.6.refs_0_), channel_id=1, source_target_pairs={{0,2},{1,3},{2,0},{3,1},{4,6},{5,7},{6,4},{7,5},{8,10},{9,11},{10,... | collective-permute-start | bytes 393224 | tf_op jit(solution)/shard_map/ppermute | solution.py:15
  22.0 8.4 %collective-permute-start.12 = (f32[32,1024]{1,0:T(8,128)S(1)}, f32[32,1024]{1,0:T(8,128)S(1)}, u32[]{:S(2)}, u32[]{:S(2)}) collective-permute-start(f32[32,1024]{1,0:T(8,128)S(1)} %collective-permute-done.8.refs_2_), channel_id=1, source_target_pairs={{0,2},{1,3},{2,0},{3,1},{4,6},{5,7},{6,4},{7,5},{8,10},{9,11},{10,... | collective-permute-start | bytes 393224 | tf_op jit(solution)/shard_map/ppermute | solution.py:15
  24.0 11.5 %collective-permute-start.3 = (f32[64,1024]{1,0:T(8,128)}, f32[64,1024]{1,0:T(8,128)S(1)}, u32[]{:S(2)}, u32[]{:S(2)}) collective-permute-start(f32[64,1024]{1,0:T(8,128)} %panel_ref.1), channel_id=1, source_target_pairs={{0,1},{1,0},{2,3},{3,2},{4,5},{5,4},{6,7},{7,6},{8,9},{9,8},{10,11... | collective-permute-start | bytes 786440 | tf_op jit(solution)/shard_map/ppermute | solution.py:15
  24.0 11.5 %collective-permute-start.5 = (f32[64,1024]{1,0:T(8,128)S(1)}, f32[64,1024]{1,0:T(8,128)S(1)}, u32[]{:S(2)}, u32[]{:S(2)}) collective-permute-start(f32[64,1024]{1,0:T(8,128)S(1)} %collective-permute-done.4.refs_2_), channel_id=1, source_target_pairs={{0,1},{1,0},{2,3},{3,2},{4,5},{5,4},{6,7},{7,6},{8,9},{9,8},{10,11... | collective-permute-start | bytes 786440 | tf_op jit(solution)/shard_map/ppermute | solution.py:15
  28.4 3.6 %collective-permute-start.11 = (f32[32,1024]{1,0:T(8,128)S(1)}, f32[32,1024]{1,0:T(8,128)S(1)}, u32[]{:S(2)}, u32[]{:S(2)}) collective-permute-start(f32[32,1024]{1,0:T(8,128)S(1)} %collective-permute-done.10.refs_2_), channel_id=1, source_target_pairs={{0,1},{1,0},{2,3},{3,2},{4,5},{5,4},{6,7},{7,6},{8,9},{9,8},{10,11... | collective-permute-start | bytes 393224 | tf_op jit(solution)/shard_map/ppermute | solution.py:15
  30.4 1.6 %collective-permute-start.13 = (f32[32,1024]{1,0:T(8,128)S(1)}, f32[32,1024]{1,0:T(8,128)S(1)}, u32[]{:S(2)}, u32[]{:S(2)}) collective-permute-start(f32[32,1024]{1,0:T(8,128)S(1)} %collective-permute-done.12.refs_4_), channel_id=1, source_target_pairs={{0,1},{1,0},{2,3},{3,2},{4,5},{5,4},{6,7},{7,6},{8,9},{9,8},{10,11... | collective-permute-start | bytes 393224 | tf_op jit(solution)/shard_map/ppermute | solution.py:15
  30.4 0.7 %copy-start.1 = (s32[1024]{0:T(1024)S(1)}, s32[1024]{0:T(1024)}, u32[]{:S(2)}) copy-start(s32[1024]{0:T(1024)} %param.5) | copy-start | bytes 12292
  32.5 12.1 %collective-permute-start.16 = (f32[256,128]{1,0:T(8,128)S(1)}, f32[256,128]{1,0:T(8,128)S(1)}, u32[]{:S(2)}, u32[]{:S(2)}) collective-permute-start(f32[256,128]{1,0:T(8,128)S(1)} %get-tuple-element.24.refs_1_), channel_id=1, source_target_pairs={{0,16},{8,24},{16,0},{24,8},{1,17},{9,25},{17,1},{25,9},{2,18},{10... | collective-permute-start | bytes 393224 | tf_op jit(solution)/shard_map/ppermute | solution.py:15
  33.6 10.9 %collective-permute-start.17 = (f32[256,128]{1,0:T(8,128)S(1)}, f32[256,128]{1,0:T(8,128)S(1)}, u32[]{:S(2)}, u32[]{:S(2)}) collective-permute-start(f32[256,128]{1,0:T(8,128)S(1)} %get-tuple-element.24.refs_1_), channel_id=1, source_target_pairs={{0,24},{8,16},{16,8},{24,0},{1,25},{9,17},{17,9},{25,1},{2,26},{10... | collective-permute-start | bytes 393224 | tf_op jit(solution)/shard_map/ppermute | solution.py:15
  37.0 9.8 %collective-permute-start.14 = (f32[256,128]{1,0:T(8,128)S(1)}, f32[256,128]{1,0:T(8,128)S(1)}, u32[]{:S(2)}, u32[]{:S(2)}) collective-permute-start(f32[256,128]{1,0:T(8,128)S(1)} %get-tuple-element.19.refs_0_), channel_id=1, source_target_pairs={{0,16},{8,24},{16,0},{24,8},{1,17},{9,25},{17,1},{25,9},{2,18},{10... | collective-permute-start | bytes 393224 | tf_op jit(solution)/shard_map/ppermute | solution.py:15
  37.7 9.1 %collective-permute-start.15 = (f32[256,128]{1,0:T(8,128)S(1)}, f32[256,128]{1,0:T(8,128)S(1)}, u32[]{:S(2)}, u32[]{:S(2)}) collective-permute-start(f32[256,128]{1,0:T(8,128)S(1)} %get-tuple-element.19.refs_0_), channel_id=1, source_target_pairs={{0,24},{8,16},{16,8},{24,0},{1,25},{9,17},{17,9},{25,1},{2,26},{10... | collective-permute-start | bytes 393224 | tf_op jit(solution)/shard_map/ppermute | solution.py:15

commit v5 on v4

v5 whole, which is shorter than its diff:
```python
import functools

import jax
import jax.numpy as jnp
from jax import lax
from jax.experimental import pallas as pl
from jax.experimental.pallas import tpu as pltpu
from jax.sharding import PartitionSpec as P


VMEM = pl.BlockSpec(memory_space=pltpu.VMEM)
HBM = pl.BlockSpec(memory_space=pltpu.HBM)


def swap(block, axis, mask):
    return lax.ppermute(block, axis, [(i, i ^ mask) for i in range(lax.axis_size(axis))])


def call(kernel, out_shape, scratch, *args, inside=True):
    return pl.pallas_call(
        kernel,
        out_shape=out_shape,
        in_specs=[VMEM if inside else HBM] * len(args),
        out_specs=jax.tree.map(lambda _: VMEM, out_shape),
        scratch_shapes=scratch,
        compiler_params=pltpu.CompilerParams(vmem_limit_bytes=16 * 2**20),
    )(*(pltpu.with_memory_space_constraint(arg, pltpu.VMEM if inside else pltpu.HBM) for arg in args))


def halves(value):
    high = value.astype(jnp.bfloat16)
    return high, (value - high.astype(jnp.float32)).astype(jnp.bfloat16)


def dot(a, b):
    return lax.dot_general(a, b, (((1,), (0,)), ((), ())), preferred_element_type=jnp.float32)


def product(high, low, pair):
    cols = pair.shape[1] // 2
    both = dot(high, pair)
    return both[:, :cols] + (both[:, cols:] + dot(low, pair[:, :cols]))


def exact(chosen, table):
    cols = table.shape[1]
    high, middle = halves(table)
    low = (table - high.astype(jnp.float32) - middle.astype(jnp.float32)).astype(jnp.bfloat16)
    terms = dot(chosen, jnp.concatenate([high, middle, low], axis=1))
    return terms[:, :cols] + terms[:, cols : 2 * cols] + terms[:, 2 * cols :]


def hot(match):
    return match.astype(jnp.float32).astype(jnp.bfloat16)


def rank(piv_row, sources, rows, slot):
    shape = slot.shape
    first = (lax.broadcasted_iota(jnp.int32, shape, 0) + sources) * rows
    pivot = jnp.broadcast_to(piv_row[...], shape)
    member = (pivot >= first) & (pivot < first + rows)
    count = member.astype(jnp.int32)
    lane = lax.broadcasted_iota(jnp.int32, shape, 1)
    step = 1
    while step < shape[1]:
        count = count + jnp.where(lane >= step, pltpu.roll(count, step, 1), 0)
        step *= 2
    slot[...] = jnp.where(member, count - 1, -1)


def pack(sources, masks, piv_hbm, matrix_hbm, *refs):
    *outs, col_ref, piv_row, matrix_ref, slot, sems = refs
    copies = [
        pltpu.make_async_copy(piv_hbm, piv_row, sems.at[0]),
        pltpu.make_async_copy(matrix_hbm, matrix_ref, sems.at[1]),
    ]
    for copy in copies:
        copy.start()
    for copy in copies:
        copy.wait()
    rows = matrix_ref.shape[0]
    block = piv_row.shape[1]
    cap = outs[0].shape[0]
    me = lax.axis_index("prow")
    rank(piv_row, sources, rows, slot)
    places = lax.broadcasted_iota(jnp.int32, (cap, rows), 0)

    @pl.when(me < sources)
    def _():
        for mask, out in zip(masks, outs):
            mine = slot[pl.ds((me ^ mask) - sources, 1), pl.ds(pl.multiple_of(me * rows, rows), rows)]
            out[...] = exact(hot(places == mine), matrix_ref[...])

    @pl.when(me >= sources)
    def _():
        ids = lax.broadcasted_iota(jnp.int32, (rows, block), 0) + me * rows
        mine = jnp.where(piv_row[...] == ids, slot[pl.ds(me - sources, 1), :], -1)
        col_ref[...] = jnp.broadcast_to(jnp.max(mine, axis=1, keepdims=True), col_ref.shape)
        packed = exact(hot(places == col_ref[...].T[:1, :]), matrix_ref[...])
        for out in outs:
            out[...] = packed


def prepare(sources, masks, piv_row, *refs):
    *refs, top_ref, whole, table, slot = refs
    blocks, packs = refs[:sources], refs[sources:]
    rows = blocks[0].shape[0]
    block = piv_row.shape[1]
    cap = packs[0].shape[0]
    lanes = 128
    me = lax.axis_index("prow")

    @pl.when(me < sources)
    def _():
        table[...] = jnp.zeros_like(table)
        for mask, ref in enumerate(blocks):
            whole[pl.ds(pl.multiple_of((me ^ mask) * rows, rows), rows), :] = ref[...]
        rank(piv_row, sources, rows, slot)
        pivot = jnp.broadcast_to(piv_row[...], (lanes, block)).T
        high, low = halves(whole[...])
        picked = jnp.concatenate([high.astype(jnp.float32), low.astype(jnp.float32)], axis=1)
        picked = jnp.where(pivot[:, :1] < block, picked, 0.0)
        lane = lax.broadcasted_iota(jnp.int32, (block, lanes), 1)
        for mask, ref in zip(masks, packs):
            table[pl.ds(0, cap), :] = ref[...]
            column = jnp.broadcast_to(slot[pl.ds((me ^ mask) - sources, 1), :], (lanes, block)).T
            chosen = [hot(column - i == lane) for i in range(0, table.shape[0], lanes)]
            picked = picked + dot(jnp.concatenate(chosen, axis=1), jnp.concatenate(halves(table[...]), axis=1))
        top_ref[...] = picked.astype(jnp.bfloat16)


def lower(sources, masks, col_ref, matrix_ref, *refs):
    *packs, own_ref, table = refs
    rows, lanes = col_ref.shape
    cap = packs[0].shape[0]
    me = lax.axis_index("prow")

    @pl.when(me >= sources)
    def _():
        table[...] = jnp.zeros_like(table)
        for mask, ref in zip(masks, packs):

            @pl.when((me ^ mask) < sources)
            def _():
                table[pl.ds(0, cap), :] += ref[...]

        column = col_ref[...]
        lane = lax.broadcasted_iota(jnp.int32, (rows, lanes), 1)
        chosen = [hot(column - i == lane) for i in range(0, table.shape[0], lanes)]
        replaced = exact(jnp.concatenate(chosen, axis=1), table[...])
        own_ref[...] = jnp.where(column[:, :1] >= 0, replaced, matrix_ref[...])


def collect(pieces, high, low):
    start = 0
    for ref in pieces:
        at = pl.ds(start, ref.shape[0])
        high[at, :], low[at, :] = halves(ref[...])
        start += ref.shape[0]


def early(*refs):
    *pieces, high, low = refs
    collect(pieces, high, low)


def solve(ready, sources, top_ref, *refs):
    ready, refs = refs[: 2 * ready], refs[2 * ready :]
    out_ref = refs[0]
    split = list(zip(ready[::2], ready[1::2]))
    if len(refs) > 1:
        *pieces, out_ref, high, low = refs
        collect(pieces, high, low)
        split.append((high, low))

    @pl.when(lax.axis_index("prow") < sources)
    def _():
        start = 0
        for high, low in split:
            at = pl.ds(start, high.shape[0])
            out_ref[at, :] = product(high[...], low[...], top_ref[...])
            start += high.shape[0]


def update(sources, masks, groups, n_split, own_ref, *refs):
    solved, refs = refs[: len(groups)], refs[len(groups) :]
    split, refs = refs[: 2 * n_split], refs[2 * n_split :]
    *got, out_ref, upper = refs
    rows, _ = own_ref.shape
    row, col = lax.axis_index("prow"), lax.axis_index("pcol")
    depth = rows // lax.axis_size("pcol")

    def places(group):
        start = 0
        for mask, first, count in group:
            yield pl.multiple_of((col ^ mask) * depth + first, count), start, count
            start += count

    @pl.when(row < sources)
    def _():
        for group, ref in zip(groups, solved):
            for at, start, count in places(group):
                out_ref[pl.ds(at, count), :] = ref[pl.ds(start, count), :]

    @pl.when(row >= sources)
    def _():
        for m, mask in enumerate(masks):
            source = row ^ mask

            @pl.when(source < sources)
            def _():
                for g, group in enumerate(groups):
                    ref = got[g * len(masks) + m]
                    for at, start, count in places(group):
                        at = pl.multiple_of(source * rows + at, count)
                        upper[pl.ds(at, count), :] = ref[pl.ds(start, count), :]

        pair = jnp.concatenate(halves(upper[...]), axis=1)
        done = jnp.concatenate([product(split[2 * i][...], split[2 * i + 1][...], pair) for i in range(n_split)], axis=0)
        base = 0
        for group in groups:
            for at, start, count in places(group):
                at = pl.ds(at, count)
                out_ref[at, :] = own_ref[at, :] - done[base + start : base + start + count]
            base += sum(count for _, _, count in group)


def per_device(matrix, panel, pivots):
    rows, cols = matrix.shape
    block = pivots.shape[0]
    depth = panel.shape[0]
    n_rows, n_cols = lax.axis_size("prow"), lax.axis_size("pcol")
    sources = block // rows
    f32, bf16 = jnp.float32, jnp.bfloat16

    def both(piece):
        return [piece, swap(piece, "pcol", 1)]

    near = both(panel) + both(swap(panel, "pcol", 2))
    first_at = [(mask, 0, depth) for mask in range(4)]
    far, relayed, relayed_at = [], [], []
    for mask in range(4, n_cols, 4):
        piece = swap(panel, "pcol", mask)
        far += both(piece)
        first_at += [(mask, 0, depth), (mask + 1, 0, depth)]
        relayed += both(swap(piece, "pcol", 2))
        relayed_at += [(mask + 2, 0, depth), (mask + 3, 0, depth)]

    lanes = 128
    masks = tuple(range(sources, n_rows))
    below = n_rows - sources
    cap = -(-(block // 2 // below + 8) // 8) * 8
    slot = pltpu.VMEM((-(-below // 8) * 8, block), jnp.int32)
    *packs, column, pivot_row, held = call(
        functools.partial(pack, sources, masks),
        [pltpu.VMEM((cap, cols), f32)] * below
        + [pltpu.VMEM((rows, lanes), jnp.int32), pltpu.VMEM((1, block), jnp.int32), pltpu.VMEM((rows, cols), f32)],
        [slot, pltpu.SemaphoreType.DMA((2,))],
        pivots.reshape(1, block), matrix,
        inside=False,
    )
    blocks = [held] + [swap(matrix, "prow", mask) for mask in range(1, sources)]
    packs = [swap(piece, "prow", mask) for mask, piece in zip(masks, packs)]

    table = pltpu.VMEM((-(-cap // lanes) * lanes, cols), f32)
    top = call(
        functools.partial(prepare, sources, masks),
        pltpu.VMEM((block, 2 * cols), bf16),
        [pltpu.VMEM((block, cols), f32), table, slot],
        pivot_row, *blocks, *packs,
    )
    own = call(
        functools.partial(lower, sources, masks),
        pltpu.VMEM((rows, cols), f32),
        [table],
        column, held, *packs,
    )

    def terms(group):
        return [pltpu.VMEM((sum(count for _, _, count in group), block), bf16)] * 2

    def result(group):
        return pltpu.VMEM((sum(count for _, _, count in group), cols), f32)

    groups = (first_at, relayed_at)
    split0 = call(early, terms(first_at), [], *near, *far)
    first = call(functools.partial(solve, 1, sources), result(first_at), [], top, *split0)
    second, *split1 = call(
        functools.partial(solve, 0, sources), [result(relayed_at)] + terms(relayed_at), [],
        top, *relayed,
    )
    solved = [first, second]
    got = [swap(piece, "prow", mask) for piece in solved for mask in masks]

    return call(
        functools.partial(update, sources, masks, groups, 2),
        jax.ShapeDtypeStruct((rows, cols), f32),
        [pltpu.VMEM((block, cols), f32)],
        own, *solved, *split0, *split1, *got,
    )


def solution(mesh):
    placed = (P("prow", "pcol"), P(("prow", "pcol"), None), P())
    return jax.shard_map(
        per_device, mesh=mesh, in_specs=placed, out_specs=P("prow", "pcol"), check_vma=False
    )
```

time: 47.8 us -> 41.3 us (0.86)
  waiting for transfers between devices: 25.6 us -> 19.4 us
  starting transfers between devices: 17.2 us -> 16.4 us
  Pallas kernels: 4.72 us -> 5.25 us
    ppermute x18 -> x14, waiting for transfers between devices: 25.6 us -> 19.4 us  [swap(): lax.ppermute(block, axis, [(i, i ^ mask) for i in range(lax.axis_size(axi...]
    ppermute x18 -> x14, starting transfers between devices: 17.2 us -> 16.4 us  [swap(): lax.ppermute(block, axis, [(i, i ^ mask) for i in range(lax.axis_size(axi...]
    pallas_call x6 -> x7, Pallas kernels: 4.72 us -> 5.25 us  [call(): pl.pallas_call(kernel, out_shape=out_shape, in_specs=[VMEM if inside else...]
  transfers between devices with their start and end apart: 18 -> 14, of which waited for: 7 -> 5; matrix products, arithmetic and copies ran while one was open for 0% -> 0% of each run, Pallas kernels for 8% -> 11%
where the time goes in v5:
time: 41.3 us; the launch traced here: 41.2 us
  waiting for transfers between devices  19.4 us (47%)
  starting transfers between devices  16.4 us (40%)
  Pallas kernels  5.25 us (13%)
    ppermute x14, waiting for transfers between devices, swap(): lax.ppermute(block, axis, [(i, i ^ mask) for i in range(lax.axis_size(axi...  19.4 us
    ppermute x14, starting transfers between devices, swap(): lax.ppermute(block, axis, [(i, i ^ mask) for i in range(lax.axis_size(axi...  16.4 us
    pallas_call x7, Pallas kernels, call(): pl.pallas_call(kernel, out_shape=out_shape, in_specs=[VMEM if inside else...  5.25 us
  transfers between devices with their start and end apart: 14, of which 5 were waited for; matrix products, arithmetic and copies ran while one was open for 0% of the time, Pallas kernels for 11%

profile of v5, /device:TPU:0, one launch (start us, length us, event | category | flops | bytes accessed | tf_op | source)
XLA Modules:
  0.0 41.2 jit_solution(16943449568615293599)
XLA Ops:
  0.0 0.0 copy-start
  0.0 4.1 %collective-permute-start.6 = (f32[64,1024]{1,0:T(8,128)}, f32[64,1024]{1,0:T(8,128)S(1)}, u32[]{:S(2)}, u32[]{:S(2)}) collective-permute-start(f32[64,1024]{1,0:T(8,128)} %refs_0_.1), channel_id=1, source_target_pairs={{0,4},{1,5},{2,6},{3,7},{4,0},{5,1},{6,2},{7,3},{8,12},{9,13},{10,... | collective-permute-start | bytes 786440 | tf_op jit(solution)/shard_map/ppermute | solution.py:16
  4.1 1.6 %collective-permute-start.4 = (f32[64,1024]{1,0:T(8,128)}, f32[64,1024]{1,0:T(8,128)S(1)}, u32[]{:S(2)}, u32[]{:S(2)}) collective-permute-start(f32[64,1024]{1,0:T(8,128)} %refs_0_.1), channel_id=1, source_target_pairs={{0,2},{1,3},{2,0},{3,1},{4,6},{5,7},{6,4},{7,5},{8,10},{9,11},{10,... | collective-permute-start | bytes 786440 | tf_op jit(solution)/shard_map/ppermute | solution.py:16
  5.6 2.0 %shard_map.37 = (f32[264,128]{1,0:T(8,128)S(1)}, f32[264,128]{1,0:T(8,128)S(1)}, s32[512,128]{1,0:T(8,128)S(1)}, s32[1,1024]{1,0:T(1,128)S(1)}, f32[512,128]{1,0:T(8,128)S(1)}) custom-call(s32[1,1024]{1,0:T(1,128)} %bitcast.1, f32[512,128]{1,0:T(8,128)} %matrix_hbm.1), custom_call_target="tpu_custom_call" | custom-call | tf_op jit(solution)/shard_map/pallas_call | solution.py:20
  7.6 1.9 %collective-permute-start = (f32[264,128]{1,0:T(8,128)S(1)}, f32[264,128]{1,0:T(8,128)S(1)}, u32[]{:S(2)}, u32[]{:S(2)}) collective-permute-start(f32[264,128]{1,0:T(8,128)S(1)} %get-tuple-element.17), channel_id=1, source_target_pairs={{0,16},{8,24},{16,0},{24,8},{1,17},{9,25},{17,1},{25,9},{2,18},{10... | collective-permute-start | bytes 405512 | tf_op jit(solution)/shard_map/ppermute | solution.py:16
  9.5 1.1 %collective-permute-start.1 = (f32[264,128]{1,0:T(8,128)S(1)}, f32[264,128]{1,0:T(8,128)S(1)}, u32[]{:S(2)}, u32[]{:S(2)}) collective-permute-start(f32[264,128]{1,0:T(8,128)S(1)} %get-tuple-element.18), channel_id=1, source_target_pairs={{0,24},{8,16},{16,8},{24,0},{1,25},{9,17},{17,9},{25,1},{2,26},{10... | collective-permute-start | bytes 405512 | tf_op jit(solution)/shard_map/ppermute | solution.py:16
  10.6 5.7 %collective-permute-done.6.refs_4_ = f32[64,1024]{1,0:T(8,128)S(1)} collective-permute-done((f32[64,1024]{1,0:T(8,128)}, f32[64,1024]{1,0:T(8,128)S(1)}, u32[]{:S(2)}, u32[]{:S(2)}) %collective-permute-start.6) | collective-permute-done | bytes 262176 | tf_op jit(solution)/shard_map/ppermute | solution.py:16
  16.4 0.7 %collective-permute-start.8 = (f32[64,1024]{1,0:T(8,128)S(1)}, f32[64,1024]{1,0:T(8,128)S(1)}, u32[]{:S(2)}, u32[]{:S(2)}) collective-permute-start(f32[64,1024]{1,0:T(8,128)S(1)} %collective-permute-done.6.refs_4_), channel_id=1, source_target_pairs={{0,2},{1,3},{2,0},{3,1},{4,6},{5,7},{6,4},{7,5},{8,10},{9,11},{10,... | collective-permute-start | bytes 786440 | tf_op jit(solution)/shard_map/ppermute | solution.py:16
  17.0 1.5 %collective-permute-start.2 = (f32[512,128]{1,0:T(8,128)}, f32[512,128]{1,0:T(8,128)S(1)}, u32[]{:S(2)}, u32[]{:S(2)}) collective-permute-start(f32[512,128]{1,0:T(8,128)} %matrix_hbm.1), channel_id=1, source_target_pairs={{0,8},{8,0},{16,24},{24,16},{1,9},{9,1},{17,25},{25,17},{2,10},{10... | collective-permute-start | bytes 786440 | tf_op jit(solution)/shard_map/ppermute | solution.py:16
  18.5 0.0 collective-permute-done.refs_0_.refs_2_
  18.5 0.0 copy-done
  18.5 0.0 collective-permute-start.3
  18.5 0.0 collective-permute-done.4.refs_2_
  18.5 0.5 %collective-permute-start.5 = (f32[64,1024]{1,0:T(8,128)S(1)}, f32[64,1024]{1,0:T(8,128)S(1)}, u32[]{:S(2)}, u32[]{:S(2)}) collective-permute-start(f32[64,1024]{1,0:T(8,128)S(1)} %collective-permute-done.4.refs_2_), channel_id=1, source_target_pairs={{0,1},{1,0},{2,3},{3,2},{4,5},{5,4},{6,7},{7,6},{8,9},{9,8},{10,11... | collective-permute-start | bytes 786440 | tf_op jit(solution)/shard_map/ppermute | solution.py:16
  19.0 0.0 collective-permute-done.1.refs_1_.refs_3_
  19.0 0.1 collective-permute-start.7
  19.1 4.7 %collective-permute-done.8.refs_0_ = f32[64,1024]{1,0:T(8,128)S(1)} collective-permute-done((f32[64,1024]{1,0:T(8,128)S(1)}, f32[64,1024]{1,0:T(8,128)S(1)}, u32[]{:S(2)}, u32[]{:S(2)}) %collective-permute-start.8) | collective-permute-done | bytes 262176 | tf_op jit(solution)/shard_map/ppermute | solution.py:16
  23.8 0.0 collective-permute-start.9
  23.8 1.4 %collective-permute-done.2.refs_1_ = f32[512,128]{1,0:T(8,128)S(1)} collective-permute-done((f32[512,128]{1,0:T(8,128)}, f32[512,128]{1,0:T(8,128)S(1)}, u32[]{:S(2)}, u32[]{:S(2)}) %collective-permute-start.2) | collective-permute-done | bytes 262176 | tf_op jit(solution)/shard_map/ppermute | solution.py:16
  25.2 1.3 %shard_map.39.top_ref = bf16[1024,256]{1,0:T(8,128)(2,1)S(1)} custom-call(s32[1,1024]{1,0:T(1,128)S(1)} %get-tuple-element.19.piv_row, f32[512,128]{1,0:T(8,128)S(1)} %get-tuple-element.16.matrix_ref.refs_0_, f32[512,128]{1,0:T(8,128)S(1)} %collective-permute-done.2.refs_1_, f32[264,128]{1,0:T(8,128)S(1)} %collective-permute-done.refs_0_.refs_2_, ...), custom_call_target="tpu_custom_call" | custom-call | tf_op jit(solution)/shard_map/pallas_call | solution.py:20
  26.5 0.0 collective-permute-done.3.refs_1_
  26.6 0.0 collective-permute-done.5.refs_3_
  26.6 0.0 collective-permute-done.7.refs_5_
  26.6 0.2 shard_map.40
  26.8 0.6 %shard_map.41.refs_0_ = f32[384,128]{1,0:T(8,128)S(1)} custom-call(bf16[1024,256]{1,0:T(8,128)(2,1)S(1)} %shard_map.39.top_ref, bf16[384,1024]{1,0:T(8,128)(2,1)S(1)} %get-tuple-element.20.refs_0_.refs_2_, bf16[384,1024]{1,0:T(8,128)(2,1)S(1)} %get-tuple-element.21.refs_1_.refs_3_), custom_call_target="tpu_custom_call" | custom-call | tf_op jit(solution)/shard_map/pallas_call | solution.py:20
  27.4 0.1 collective-permute-start.10
  27.5 2.9 %collective-permute-start.11 = (f32[384,128]{1,0:T(8,128)S(1)}, f32[384,128]{1,0:T(8,128)S(1)}, u32[]{:S(2)}, u32[]{:S(2)}) collective-permute-start(f32[384,128]{1,0:T(8,128)S(1)} %shard_map.41.refs_0_), channel_id=1, source_target_pairs={{0,24},{8,16},{16,8},{24,0},{1,25},{9,17},{17,9},{25,1},{2,26},{10... | collective-permute-start | bytes 589832 | tf_op jit(solution)/shard_map/ppermute | solution.py:16
  30.4 0.0 collective-permute-done.9.refs_1_
  30.4 0.4 shard_map.42
  30.8 0.1 collective-permute-start.12
  30.9 2.0 %collective-permute-start.13 = (f32[128,128]{1,0:T(8,128)S(1)}, f32[128,128]{1,0:T(8,128)S(1)}, u32[]{:S(2)}, u32[]{:S(2)}) collective-permute-start(f32[128,128]{1,0:T(8,128)S(1)} %get-tuple-element.22.refs_1_), channel_id=1, source_target_pairs={{0,24},{8,16},{16,8},{24,0},{1,25},{9,17},{17,9},{25,1},{2,26},{10... | collective-permute-start | bytes 196616 | tf_op jit(solution)/shard_map/ppermute | solution.py:16
  32.9 6.8 %collective-permute-done.10.refs_6_ = f32[384,128]{1,0:T(8,128)S(1)} collective-permute-done((f32[384,128]{1,0:T(8,128)S(1)}, f32[384,128]{1,0:T(8,128)S(1)}, u32[]{:S(2)}, u32[]{:S(2)}) %collective-permute-start.10) | collective-permute-done | bytes 196640 | tf_op jit(solution)/shard_map/ppermute | solution.py:16
  39.7 0.0 collective-permute-done.11.refs_7_
  39.7 0.7 %collective-permute-done.12.refs_8_ = f32[128,128]{1,0:T(8,128)S(1)} collective-permute-done((f32[128,128]{1,0:T(8,128)S(1)}, f32[128,128]{1,0:T(8,128)S(1)}, u32[]{:S(2)}, u32[]{:S(2)}) %collective-permute-start.12) | collective-permute-done | bytes 65568 | tf_op jit(solution)/shard_map/ppermute | solution.py:16
  40.4 0.0 collective-permute-done.13.refs_9_
  40.4 0.7 %shard_map.43 = f32[512,128]{1,0:T(8,128)} custom-call(f32[512,128]{1,0:T(8,128)S(1)} %shard_map.38.own_ref, f32[384,128]{1,0:T(8,128)S(1)} %shard_map.41.refs_0_, f32[128,128]{1,0:T(8,128)S(1)} %get-tuple-element.22.refs_1_, bf16[384,1024]{1,0:T(8,128)(2,1)S(1)} %get-tuple-element.20.refs_0_.refs_2_, ...), custom_call_target="tpu_custom_call" | custom-call | tf_op jit(solution)/shard_map/pallas_call | solution.py:20
  (1 shorter events, 0.0 us)
Async XLA Ops:
  0.0 18.5 %copy-start = (f32[64,1024]{1,0:T(8,128)S(1)}, f32[64,1024]{1,0:T(8,128)}, u32[]{:S(2)}) copy-start(f32[64,1024]{1,0:T(8,128)} %refs_0_.1) | copy-start | bytes 786436
  0.0 16.4 %collective-permute-start.6 = (f32[64,1024]{1,0:T(8,128)}, f32[64,1024]{1,0:T(8,128)S(1)}, u32[]{:S(2)}, u32[]{:S(2)}) collective-permute-start(f32[64,1024]{1,0:T(8,128)} %refs_0_.1), channel_id=1, source_target_pairs={{0,4},{1,5},{2,6},{3,7},{4,0},{5,1},{6,2},{7,3},{8,12},{9,13},{10,... | collective-permute-start | bytes 786440 | tf_op jit(solution)/shard_map/ppermute | solution.py:16
  4.1 14.5 %collective-permute-start.4 = (f32[64,1024]{1,0:T(8,128)}, f32[64,1024]{1,0:T(8,128)S(1)}, u32[]{:S(2)}, u32[]{:S(2)}) collective-permute-start(f32[64,1024]{1,0:T(8,128)} %refs_0_.1), channel_id=1, source_target_pairs={{0,2},{1,3},{2,0},{3,1},{4,6},{5,7},{6,4},{7,5},{8,10},{9,11},{10,... | collective-permute-start | bytes 786440 | tf_op jit(solution)/shard_map/ppermute | solution.py:16
  7.6 10.9 %collective-permute-start = (f32[264,128]{1,0:T(8,128)S(1)}, f32[264,128]{1,0:T(8,128)S(1)}, u32[]{:S(2)}, u32[]{:S(2)}) collective-permute-start(f32[264,128]{1,0:T(8,128)S(1)} %get-tuple-element.17), channel_id=1, source_target_pairs={{0,16},{8,24},{16,0},{24,8},{1,17},{9,25},{17,1},{25,9},{2,18},{10... | collective-permute-start | bytes 405512 | tf_op jit(solution)/shard_map/ppermute | solution.py:16
  9.5 9.5 %collective-permute-start.1 = (f32[264,128]{1,0:T(8,128)S(1)}, f32[264,128]{1,0:T(8,128)S(1)}, u32[]{:S(2)}, u32[]{:S(2)}) collective-permute-start(f32[264,128]{1,0:T(8,128)S(1)} %get-tuple-element.18), channel_id=1, source_target_pairs={{0,24},{8,16},{16,8},{24,0},{1,25},{9,17},{17,9},{25,1},{2,26},{10... | collective-permute-start | bytes 405512 | tf_op jit(solution)/shard_map/ppermute | solution.py:16
  16.4 7.4 %collective-permute-start.8 = (f32[64,1024]{1,0:T(8,128)S(1)}, f32[64,1024]{1,0:T(8,128)S(1)}, u32[]{:S(2)}, u32[]{:S(2)}) collective-permute-start(f32[64,1024]{1,0:T(8,128)S(1)} %collective-permute-done.6.refs_4_), channel_id=1, source_target_pairs={{0,2},{1,3},{2,0},{3,1},{4,6},{5,7},{6,4},{7,5},{8,10},{9,11},{10,... | collective-permute-start | bytes 786440 | tf_op jit(solution)/shard_map/ppermute | solution.py:16
  17.0 8.2 %collective-permute-start.2 = (f32[512,128]{1,0:T(8,128)}, f32[512,128]{1,0:T(8,128)S(1)}, u32[]{:S(2)}, u32[]{:S(2)}) collective-permute-start(f32[512,128]{1,0:T(8,128)} %matrix_hbm.1), channel_id=1, source_target_pairs={{0,8},{8,0},{16,24},{24,16},{1,9},{9,1},{17,25},{25,17},{2,10},{10... | collective-permute-start | bytes 786440 | tf_op jit(solution)/shard_map/ppermute | solution.py:16
  18.5 8.0 %collective-permute-start.3 = (f32[64,1024]{1,0:T(8,128)S(1)}, f32[64,1024]{1,0:T(8,128)S(1)}, u32[]{:S(2)}, u32[]{:S(2)}) collective-permute-start(f32[64,1024]{1,0:T(8,128)S(1)} %copy-done), channel_id=1, source_target_pairs={{0,1},{1,0},{2,3},{3,2},{4,5},{5,4},{6,7},{7,6},{8,9},{9,8},{10,11... | collective-permute-start | bytes 786440 | tf_op jit(solution)/shard_map/ppermute | solution.py:16
  18.5 8.0 %collective-permute-start.5 = (f32[64,1024]{1,0:T(8,128)S(1)}, f32[64,1024]{1,0:T(8,128)S(1)}, u32[]{:S(2)}, u32[]{:S(2)}) collective-permute-start(f32[64,1024]{1,0:T(8,128)S(1)} %collective-permute-done.4.refs_2_), channel_id=1, source_target_pairs={{0,1},{1,0},{2,3},{3,2},{4,5},{5,4},{6,7},{7,6},{8,9},{9,8},{10,11... | collective-permute-start | bytes 786440 | tf_op jit(solution)/shard_map/ppermute | solution.py:16
  19.0 7.5 %collective-permute-start.7 = (f32[64,1024]{1,0:T(8,128)S(1)}, f32[64,1024]{1,0:T(8,128)S(1)}, u32[]{:S(2)}, u32[]{:S(2)}) collective-permute-start(f32[64,1024]{1,0:T(8,128)S(1)} %collective-permute-done.6.refs_4_), channel_id=1, source_target_pairs={{0,1},{1,0},{2,3},{3,2},{4,5},{5,4},{6,7},{7,6},{8,9},{9,8},{10,11... | collective-permute-start | bytes 786440 | tf_op jit(solution)/shard_map/ppermute | solution.py:16
  23.8 6.7 %collective-permute-start.9 = (f32[64,1024]{1,0:T(8,128)S(1)}, f32[64,1024]{1,0:T(8,128)S(1)}, u32[]{:S(2)}, u32[]{:S(2)}) collective-permute-start(f32[64,1024]{1,0:T(8,128)S(1)} %collective-permute-done.8.refs_0_), channel_id=1, source_target_pairs={{0,1},{1,0},{2,3},{3,2},{4,5},{5,4},{6,7},{7,6},{8,9},{9,8},{10,11... | collective-permute-start | bytes 786440 | tf_op jit(solution)/shard_map/ppermute | solution.py:16
  27.4 12.3 %collective-permute-start.10 = (f32[384,128]{1,0:T(8,128)S(1)}, f32[384,128]{1,0:T(8,128)S(1)}, u32[]{:S(2)}, u32[]{:S(2)}) collective-permute-start(f32[384,128]{1,0:T(8,128)S(1)} %shard_map.41.refs_0_), channel_id=1, source_target_pairs={{0,16},{8,24},{16,0},{24,8},{1,17},{9,25},{17,1},{25,9},{2,18},{10... | collective-permute-start | bytes 589832 | tf_op jit(solution)/shard_map/ppermute | solution.py:16
  27.5 12.2 %collective-permute-start.11 = (f32[384,128]{1,0:T(8,128)S(1)}, f32[384,128]{1,0:T(8,128)S(1)}, u32[]{:S(2)}, u32[]{:S(2)}) collective-permute-start(f32[384,128]{1,0:T(8,128)S(1)} %shard_map.41.refs_0_), channel_id=1, source_target_pairs={{0,24},{8,16},{16,8},{24,0},{1,25},{9,17},{17,9},{25,1},{2,26},{10... | collective-permute-start | bytes 589832 | tf_op jit(solution)/shard_map/ppermute | solution.py:16
  30.8 9.6 %collective-permute-start.12 = (f32[128,128]{1,0:T(8,128)S(1)}, f32[128,128]{1,0:T(8,128)S(1)}, u32[]{:S(2)}, u32[]{:S(2)}) collective-permute-start(f32[128,128]{1,0:T(8,128)S(1)} %get-tuple-element.22.refs_1_), channel_id=1, source_target_pairs={{0,16},{8,24},{16,0},{24,8},{1,17},{9,25},{17,1},{25,9},{2,18},{10... | collective-permute-start | bytes 196616 | tf_op jit(solution)/shard_map/ppermute | solution.py:16
  30.9 9.5 %collective-permute-start.13 = (f32[128,128]{1,0:T(8,128)S(1)}, f32[128,128]{1,0:T(8,128)S(1)}, u32[]{:S(2)}, u32[]{:S(2)}) collective-permute-start(f32[128,128]{1,0:T(8,128)S(1)} %get-tuple-element.22.refs_1_), channel_id=1, source_target_pairs={{0,24},{8,16},{16,8},{24,0},{1,25},{9,17},{17,9},{25,1},{2,26},{10... | collective-permute-start | bytes 196616 | tf_op jit(solution)/shard_map/ppermute | solution.py:16

commit v6 on v5

--- a/solution.py
+++ b/solution.py
@@ -76,13 +76,20 @@
     ]
     for copy in copies:
         copy.start()
-    for copy in copies:
-        copy.wait()
     rows = matrix_ref.shape[0]
     block = piv_row.shape[1]
     cap = outs[0].shape[0]
     me = lax.axis_index("prow")
+    copies[0].wait()
     rank(piv_row, sources, rows, slot)
+
+    @pl.when(me >= sources)
+    def _():
+        ids = lax.broadcasted_iota(jnp.int32, (rows, block), 0) + me * rows
+        mine = jnp.where(piv_row[...] == ids, slot[pl.ds(me - sources, 1), :], -1)
+        col_ref[...] = jnp.broadcast_to(jnp.max(mine, axis=1, keepdims=True), col_ref.shape)
+
+    copies[1].wait()
     places = lax.broadcasted_iota(jnp.int32, (cap, rows), 0)
 
     @pl.when(me < sources)
@@ -93,40 +100,49 @@
 
     @pl.when(me >= sources)
     def _():
-        ids = lax.broadcasted_iota(jnp.int32, (rows, block), 0) + me * rows
-        mine = jnp.where(piv_row[...] == ids, slot[pl.ds(me - sources, 1), :], -1)
-        col_ref[...] = jnp.broadcast_to(jnp.max(mine, axis=1, keepdims=True), col_ref.shape)
         packed = exact(hot(places == col_ref[...].T[:1, :]), matrix_ref[...])
         for out in outs:
             out[...] = packed
 
 
-def prepare(sources, masks, piv_row, *refs):
-    *refs, top_ref, whole, table, slot = refs
+def hots(sources, masks, piv_row, chosen_ref, keep_ref, slot):
+    block, lanes = keep_ref.shape
+    rows = block // sources
+    span = chosen_ref.shape[1] // len(masks)
+    me = lax.axis_index("prow")
+
+    @pl.when(me < sources)
+    def _():
+        rank(piv_row, sources, rows, slot)
+        pivot = jnp.broadcast_to(piv_row[...], (lanes, block)).T
+        keep_ref[...] = (pivot < block).astype(jnp.float32)
+        lane = lax.broadcasted_iota(jnp.int32, (block, lanes), 1)
+        for m, mask in enumerate(masks):
+            column = jnp.broadcast_to(slot[pl.ds((me ^ mask) - sources, 1), :], (lanes, block)).T
+            for i in range(0, span, lanes):
+                chosen_ref[:, pl.ds(m * span + i, lanes)] = hot(column - i == lane)
+
+
+def prepare(sources, masks, chosen_ref, keep_ref, *refs):
+    *refs, top_ref, whole, table = refs
     blocks, packs = refs[:sources], refs[sources:]
-    rows = blocks[0].shape[0]
-    block = piv_row.shape[1]
+    rows, cols = blocks[0].shape
     cap = packs[0].shape[0]
-    lanes = 128
+    span = table.shape[0] // len(masks)
     me = lax.axis_index("prow")
 
     @pl.when(me < sources)
     def _():
-        table[...] = jnp.zeros_like(table)
         for mask, ref in enumerate(blocks):
             whole[pl.ds(pl.multiple_of((me ^ mask) * rows, rows), rows), :] = ref[...]
-        rank(piv_row, sources, rows, slot)
-        pivot = jnp.broadcast_to(piv_row[...], (lanes, block)).T
-        high, low = halves(whole[...])
-        picked = jnp.concatenate([high.astype(jnp.float32), low.astype(jnp.float32)], axis=1)
-        picked = jnp.where(pivot[:, :1] < block, picked, 0.0)
-        lane = lax.broadcasted_iota(jnp.int32, (block, lanes), 1)
-        for mask, ref in zip(masks, packs):
-            table[pl.ds(0, cap), :] = ref[...]
-            column = jnp.broadcast_to(slot[pl.ds((me ^ mask) - sources, 1), :], (lanes, block)).T
-            chosen = [hot(column - i == lane) for i in range(0, table.shape[0], lanes)]
-            picked = picked + dot(jnp.concatenate(chosen, axis=1), jnp.concatenate(halves(table[...]), axis=1))
-        top_ref[...] = picked.astype(jnp.bfloat16)
+        for m, ref in enumerate(packs):
+            table[pl.ds(m * span, cap), :] = ref[...]
+            if span > cap:
+                table[pl.ds(m * span + cap, span - cap), :] = jnp.zeros((span - cap, cols), jnp.float32)
+        high, low = halves(jnp.where(keep_ref[:, :1] > 0.0, whole[...], 0.0))
+        old = jnp.concatenate([high.astype(jnp.float32), low.astype(jnp.float32)], axis=1)
+        new = dot(chosen_ref[...], jnp.concatenate(halves(table[...]), axis=1))
+        top_ref[...] = (old + new).astype(jnp.bfloat16)
 
 
 def lower(sources, masks, col_ref, matrix_ref, *refs):
@@ -182,36 +198,39 @@
             start += high.shape[0]
 
 
-def update(sources, masks, groups, n_split, own_ref, *refs):
-    solved, refs = refs[: len(groups)], refs[len(groups) :]
+def places(group, col, depth):
+    start = 0
+    for mask, first, count in group:
+        yield pl.multiple_of((col ^ mask) * depth + first, count), start, count
+        start += count
+
+
+def update(sources, masks, groups, later, n_split, own_ref, *refs):
+    solved, refs = refs[: len(groups) - later], refs[len(groups) - later :]
     split, refs = refs[: 2 * n_split], refs[2 * n_split :]
     *got, out_ref, upper = refs
-    rows, _ = own_ref.shape
+    rows = own_ref.shape[0]
     row, col = lax.axis_index("prow"), lax.axis_index("pcol")
     depth = rows // lax.axis_size("pcol")
 
-    def places(group):
-        start = 0
-        for mask, first, count in group:
-            yield pl.multiple_of((col ^ mask) * depth + first, count), start, count
-            start += count
-
     @pl.when(row < sources)
     def _():
         for group, ref in zip(groups, solved):
-            for at, start, count in places(group):
+            for at, start, count in places(group, col, depth):
                 out_ref[pl.ds(at, count), :] = ref[pl.ds(start, count), :]
 
     @pl.when(row >= sources)
     def _():
+        if later:
+            upper[...] = jnp.zeros_like(upper)
         for m, mask in enumerate(masks):
             source = row ^ mask
 
             @pl.when(source < sources)
             def _():
-                for g, group in enumerate(groups):
+                for g, group in enumerate(groups[: len(groups) - later]):
                     ref = got[g * len(masks) + m]
-                    for at, start, count in places(group):
+                    for at, start, count in places(group, col, depth):
                         at = pl.multiple_of(source * rows + at, count)
                         upper[pl.ds(at, count), :] = ref[pl.ds(start, count), :]
 
@@ -219,9 +238,53 @@
         done = jnp.concatenate([product(split[2 * i][...], split[2 * i + 1][...], pair) for i in range(n_split)], axis=0)
         base = 0
         for group in groups:
-            for at, start, count in places(group):
+            for at, start, count in places(group, col, depth):
                 at = pl.ds(at, count)
                 out_ref[at, :] = own_ref[at, :] - done[base + start : base + start + count]
+            base += sum(count for _, _, count in group)
+
+
+def finish(sources, masks, groups, n_split, so_far_ref, solved_ref, *refs):
+    split, refs = refs[: 2 * n_split], refs[2 * n_split :]
+    *got, out_ref, part = refs
+    rows = so_far_ref.shape[0]
+    row, col = lax.axis_index("prow"), lax.axis_index("pcol")
+    depth = rows // lax.axis_size("pcol")
+    last = groups[-1]
+
+    @pl.when(row < sources)
+    def _():
+        out_ref[...] = so_far_ref[...]
+        for at, start, count in places(last, col, depth):
+            out_ref[pl.ds(at, count), :] = solved_ref[pl.ds(start, count), :]
+
+    @pl.when(row >= sources)
+    def _():
+        height = solved_ref.shape[0]
+        for m, mask in enumerate(masks):
+            source = row ^ mask
+
+            @pl.when(source < sources)
+            def _():
+                for piece, (distance, _, count) in enumerate(last):
+                    at = source * height + (piece // 2 * 2 + ((col ^ distance) & 1)) * count
+                    part[pl.ds(pl.multiple_of(at, count), count), :] = got[m][pl.ds(piece * count, count), :]
+
+        total = None
+        for source in range(sources):
+            for i in range(0, len(last), 2):
+                at = pl.multiple_of(source * rows + ((col ^ last[i][0]) // 2) * (2 * depth), 2 * depth)
+                at = pl.ds(at, 2 * depth)
+                mine = part[pl.ds(source * height + i * depth, 2 * depth), :]
+                pair = jnp.concatenate(halves(mine), axis=1)
+                done = [product(split[2 * j][:, at], split[2 * j + 1][:, at], pair) for j in range(n_split)]
+                done = jnp.concatenate(done, axis=0)
+                total = done if total is None else total + done
+        base = 0
+        for group in groups:
+            for at, start, count in places(group, col, depth):
+                at = pl.ds(at, count)
+                out_ref[at, :] = so_far_ref[at, :] - total[base + start : base + start + count]
             base += sum(count for _, _, count in group)
 
 
@@ -262,17 +325,23 @@
     blocks = [held] + [swap(matrix, "prow", mask) for mask in range(1, sources)]
     packs = [swap(piece, "prow", mask) for mask, piece in zip(masks, packs)]
 
-    table = pltpu.VMEM((-(-cap // lanes) * lanes, cols), f32)
+    span = -(-cap // lanes) * lanes
+    chosen, keep = call(
+        functools.partial(hots, sources, masks),
+        [pltpu.VMEM((block, below * span), bf16), pltpu.VMEM((block, lanes), f32)],
+        [slot],
+        pivot_row,
+    )
     top = call(
         functools.partial(prepare, sources, masks),
         pltpu.VMEM((block, 2 * cols), bf16),
-        [pltpu.VMEM((block, cols), f32), table, slot],
-        pivot_row, *blocks, *packs,
+        [pltpu.VMEM((block, cols), f32), pltpu.VMEM((below * span, cols), f32)],
+        chosen, keep, *blocks, *packs,
     )
     own = call(
         functools.partial(lower, sources, masks),
         pltpu.VMEM((rows, cols), f32),
-        [table],
+        [pltpu.VMEM((span, cols), f32)],
         column, held, *packs,
     )
 
@@ -292,11 +361,25 @@
     solved = [first, second]
     got = [swap(piece, "prow", mask) for piece in solved for mask in masks]
 
+    scratch = [pltpu.VMEM((block, cols), f32)]
+    if 2 * depth % lanes:
+        return call(
+            functools.partial(update, sources, masks, groups, 0, 2),
+            jax.ShapeDtypeStruct((rows, cols), f32),
+            scratch,
+            own, *solved, *split0, *split1, *got,
+        )
+    so_far = call(
+        functools.partial(update, sources, masks, groups, 1, 2),
+        pltpu.VMEM((rows, cols), f32),
+        scratch,
+        own, *solved[:-1], *split0, *split1, *got[: -len(masks)],
+    )
     return call(
-        functools.partial(update, sources, masks, groups, 2),
+        functools.partial(finish, sources, masks, groups, 2),
         jax.ShapeDtypeStruct((rows, cols), f32),
-        [pltpu.VMEM((block, cols), f32)],
-        own, *solved, *split0, *split1, *got,
+        [pltpu.VMEM((sources * solved[-1].shape[0], cols), f32)],
+        so_far, solved[-1], *split0, *split1, *got[-len(masks) :],
     )
 
 

time: 41.3 us -> 41.9 us (1.015)
    pallas_call x7 -> x9, Pallas kernels: 5.25 us -> 5.35 us  [call(): pl.pallas_call(kernel, out_shape=out_shape, in_specs=[VMEM if inside else...]
where the time goes in v6:
time: 41.9 us; the launch traced here: 41.7 us
  waiting for transfers between devices  19.5 us (47%)
  starting transfers between devices  16.5 us (39%)
  Pallas kernels  5.35 us (13%)
    ppermute x14, waiting for transfers between devices, swap(): lax.ppermute(block, axis, [(i, i ^ mask) for i in range(lax.axis_size(axi...  19.5 us
    ppermute x14, starting transfers between devices, swap(): lax.ppermute(block, axis, [(i, i ^ mask) for i in range(lax.axis_size(axi...  16.5 us
    pallas_call x9, Pallas kernels, call(): pl.pallas_call(kernel, out_shape=out_shape, in_specs=[VMEM if inside else...  5.35 us
  transfers between devices with their start and end apart: 14, of which 5 were waited for; matrix products, arithmetic and copies ran while one was open for 0% of the time, Pallas kernels for 11%

profile of v6, /device:TPU:0, one launch (start us, length us, event | category | flops | bytes accessed | tf_op | source)
XLA Modules:
  0.0 41.7 jit_solution(15652774291091123532)
XLA Ops:
  0.0 4.1 %collective-permute-start.6 = (f32[64,1024]{1,0:T(8,128)}, f32[64,1024]{1,0:T(8,128)S(1)}, u32[]{:S(2)}, u32[]{:S(2)}) collective-permute-start(f32[64,1024]{1,0:T(8,128)} %refs_0_.1), channel_id=1, source_target_pairs={{0,4},{1,5},{2,6},{3,7},{4,0},{5,1},{6,2},{7,3},{8,12},{9,13},{10,... | collective-permute-start | bytes 786440 | tf_op jit(solution)/shard_map/ppermute | solution.py:16
  4.1 1.6 %collective-permute-start.4 = (f32[64,1024]{1,0:T(8,128)}, f32[64,1024]{1,0:T(8,128)S(1)}, u32[]{:S(2)}, u32[]{:S(2)}) collective-permute-start(f32[64,1024]{1,0:T(8,128)} %refs_0_.1), channel_id=1, source_target_pairs={{0,2},{1,3},{2,0},{3,1},{4,6},{5,7},{6,4},{7,5},{8,10},{9,11},{10,... | collective-permute-start | bytes 786440 | tf_op jit(solution)/shard_map/ppermute | solution.py:16
  5.6 1.7 %shard_map.37 = (f32[264,128]{1,0:T(8,128)S(1)}, f32[264,128]{1,0:T(8,128)S(1)}, s32[512,128]{1,0:T(8,128)S(1)}, s32[1,1024]{1,0:T(1,128)S(1)}, f32[512,128]{1,0:T(8,128)S(1)}) custom-call(s32[1,1024]{1,0:T(1,128)} %bitcast.1, f32[512,128]{1,0:T(8,128)} %matrix_hbm.1), custom_call_target="tpu_custom_call" | custom-call | tf_op jit(solution)/shard_map/pallas_call | solution.py:20
  7.3 1.9 %collective-permute-start = (f32[264,128]{1,0:T(8,128)S(1)}, f32[264,128]{1,0:T(8,128)S(1)}, u32[]{:S(2)}, u32[]{:S(2)}) collective-permute-start(f32[264,128]{1,0:T(8,128)S(1)} %get-tuple-element.19), channel_id=1, source_target_pairs={{0,16},{8,24},{16,0},{24,8},{1,17},{9,25},{17,1},{25,9},{2,18},{10... | collective-permute-start | bytes 405512 | tf_op jit(solution)/shard_map/ppermute | solution.py:16
  9.3 1.1 %collective-permute-start.1 = (f32[264,128]{1,0:T(8,128)S(1)}, f32[264,128]{1,0:T(8,128)S(1)}, u32[]{:S(2)}, u32[]{:S(2)}) collective-permute-start(f32[264,128]{1,0:T(8,128)S(1)} %get-tuple-element.20), channel_id=1, source_target_pairs={{0,24},{8,16},{16,8},{24,0},{1,25},{9,17},{17,9},{25,1},{2,26},{10... | collective-permute-start | bytes 405512 | tf_op jit(solution)/shard_map/ppermute | solution.py:16
  10.4 5.9 %collective-permute-done.6.refs_4_ = f32[64,1024]{1,0:T(8,128)S(1)} collective-permute-done((f32[64,1024]{1,0:T(8,128)}, f32[64,1024]{1,0:T(8,128)S(1)}, u32[]{:S(2)}, u32[]{:S(2)}) %collective-permute-start.6) | collective-permute-done | bytes 262176 | tf_op jit(solution)/shard_map/ppermute | solution.py:16
  16.3 0.7 %collective-permute-start.8 = (f32[64,1024]{1,0:T(8,128)S(1)}, f32[64,1024]{1,0:T(8,128)S(1)}, u32[]{:S(2)}, u32[]{:S(2)}) collective-permute-start(f32[64,1024]{1,0:T(8,128)S(1)} %collective-permute-done.6.refs_4_), channel_id=1, source_target_pairs={{0,2},{1,3},{2,0},{3,1},{4,6},{5,7},{6,4},{7,5},{8,10},{9,11},{10,... | collective-permute-start | bytes 786440 | tf_op jit(solution)/shard_map/ppermute | solution.py:16
  17.0 1.5 %collective-permute-start.2 = (f32[512,128]{1,0:T(8,128)}, f32[512,128]{1,0:T(8,128)S(1)}, u32[]{:S(2)}, u32[]{:S(2)}) collective-permute-start(f32[512,128]{1,0:T(8,128)} %matrix_hbm.1), channel_id=1, source_target_pairs={{0,8},{8,0},{16,24},{24,16},{1,9},{9,1},{17,25},{25,17},{2,10},{10... | collective-permute-start | bytes 786440 | tf_op jit(solution)/shard_map/ppermute | solution.py:16
  18.5 0.0 collective-permute-done.refs_0_.refs_2_
  18.5 0.0 collective-permute-start.3
  18.5 0.0 collective-permute-done.4.refs_2_
  18.5 0.5 %collective-permute-start.5 = (f32[64,1024]{1,0:T(8,128)S(1)}, f32[64,1024]{1,0:T(8,128)S(1)}, u32[]{:S(2)}, u32[]{:S(2)}) collective-permute-start(f32[64,1024]{1,0:T(8,128)S(1)} %collective-permute-done.4.refs_2_), channel_id=1, source_target_pairs={{0,1},{1,0},{2,3},{3,2},{4,5},{5,4},{6,7},{7,6},{8,9},{9,8},{10,11... | collective-permute-start | bytes 786440 | tf_op jit(solution)/shard_map/ppermute | solution.py:16
  19.0 0.0 collective-permute-done.1.refs_1_.refs_3_
  19.0 0.1 collective-permute-start.7
  19.1 4.6 %collective-permute-done.8.refs_0_ = f32[64,1024]{1,0:T(8,128)S(1)} collective-permute-done((f32[64,1024]{1,0:T(8,128)S(1)}, f32[64,1024]{1,0:T(8,128)S(1)}, u32[]{:S(2)}, u32[]{:S(2)}) %collective-permute-start.8) | collective-permute-done | bytes 262176 | tf_op jit(solution)/shard_map/ppermute | solution.py:16
  23.7 0.0 collective-permute-start.9
  23.7 1.1 %shard_map.39 = (bf16[1024,768]{1,0:T(8,128)(2,1)S(1)}, f32[1024,128]{1,0:T(8,128)S(1)}) custom-call(s32[1,1024]{1,0:T(1,128)S(1)} %get-tuple-element.21.piv_row), custom_call_target="tpu_custom_call" | custom-call | tf_op jit(solution)/shard_map/pallas_call | solution.py:20
  24.8 0.4 collective-permute-done.2.refs_1_
  25.2 0.0 copy-start
  25.2 0.6 %shard_map.40.top_ref = bf16[1024,256]{1,0:T(8,128)(2,1)S(1)} custom-call(bf16[1024,768]{1,0:T(8,128)(2,1)S(1)} %get-tuple-element.22.chosen_ref, f32[1024,128]{1,0:T(8,128)S(1)} %get-tuple-element.23.keep_ref, f32[512,128]{1,0:T(8,128)S(1)} %get-tuple-element.18.matrix_ref.refs_0_, f32[512,128]{1,0:T(8,128)S(1)} %collective-permute-done.2.refs_1_, ...), custom_call_target="tpu_custom_call" | custom-call | tf_op jit(solution)/shard_map/pallas_call | solution.py:20
  25.8 0.0 collective-permute-done.3.refs_1_
  25.8 0.0 collective-permute-done.5.refs_3_
  25.9 0.0 collective-permute-done.7.refs_5_
  25.9 0.3 copy-done
  26.1 0.2 shard_map.41
  26.4 0.6 %shard_map.42.refs_0_ = f32[384,128]{1,0:T(8,128)S(1)} custom-call(bf16[1024,256]{1,0:T(8,128)(2,1)S(1)} %shard_map.40.top_ref, bf16[384,1024]{1,0:T(8,128)(2,1)S(1)} %get-tuple-element.24.refs_0_.refs_1_, bf16[384,1024]{1,0:T(8,128)(2,1)S(1)} %get-tuple-element.25.refs_1_.refs_2_), custom_call_target="tpu_custom_call" | custom-call | tf_op jit(solution)/shard_map/pallas_call | solution.py:20
  27.0 1.0 %collective-permute-start.10 = (f32[384,128]{1,0:T(8,128)S(1)}, f32[384,128]{1,0:T(8,128)S(1)}, u32[]{:S(2)}, u32[]{:S(2)}) collective-permute-start(f32[384,128]{1,0:T(8,128)S(1)} %shard_map.42.refs_0_), channel_id=1, source_target_pairs={{0,16},{8,24},{16,0},{24,8},{1,17},{9,25},{17,1},{25,9},{2,18},{10... | collective-permute-start | bytes 589832 | tf_op jit(solution)/shard_map/ppermute | solution.py:16
  28.0 2.0 %collective-permute-start.11 = (f32[384,128]{1,0:T(8,128)S(1)}, f32[384,128]{1,0:T(8,128)S(1)}, u32[]{:S(2)}, u32[]{:S(2)}) collective-permute-start(f32[384,128]{1,0:T(8,128)S(1)} %shard_map.42.refs_0_), channel_id=1, source_target_pairs={{0,24},{8,16},{16,8},{24,0},{1,25},{9,17},{17,9},{25,1},{2,26},{10... | collective-permute-start | bytes 589832 | tf_op jit(solution)/shard_map/ppermute | solution.py:16
  30.0 0.0 collective-permute-done.9.refs_1_
  30.0 0.4 shard_map.43
  30.4 0.7 %collective-permute-start.12 = (f32[128,128]{1,0:T(8,128)S(1)}, f32[128,128]{1,0:T(8,128)S(1)}, u32[]{:S(2)}, u32[]{:S(2)}) collective-permute-start(f32[128,128]{1,0:T(8,128)S(1)} %get-tuple-element.28.solved_ref), channel_id=1, source_target_pairs={{0,16},{8,24},{16,0},{24,8},{1,17},{9,25},{17,1},{25,9},{2,18},{10... | collective-permute-start | bytes 196616 | tf_op jit(solution)/shard_map/ppermute | solution.py:16
  31.1 1.3 %collective-permute-start.13 = (f32[128,128]{1,0:T(8,128)S(1)}, f32[128,128]{1,0:T(8,128)S(1)}, u32[]{:S(2)}, u32[]{:S(2)}) collective-permute-start(f32[128,128]{1,0:T(8,128)S(1)} %get-tuple-element.28.solved_ref), channel_id=1, source_target_pairs={{0,24},{8,16},{16,8},{24,0},{1,25},{9,17},{17,9},{25,1},{2,26},{10... | collective-permute-start | bytes 196616 | tf_op jit(solution)/shard_map/ppermute | solution.py:16
  32.4 7.9 %collective-permute-done.10.refs_5_ = f32[384,128]{1,0:T(8,128)S(1)} collective-permute-done((f32[384,128]{1,0:T(8,128)S(1)}, f32[384,128]{1,0:T(8,128)S(1)}, u32[]{:S(2)}, u32[]{:S(2)}) %collective-permute-start.10) | collective-permute-done | bytes 196640 | tf_op jit(solution)/shard_map/ppermute | solution.py:16
  40.3 0.0 collective-permute-done.11.refs_6_
  40.3 0.7 %collective-permute-done.12.refs_4_ = f32[128,128]{1,0:T(8,128)S(1)} collective-permute-done((f32[128,128]{1,0:T(8,128)S(1)}, f32[128,128]{1,0:T(8,128)S(1)}, u32[]{:S(2)}, u32[]{:S(2)}) %collective-permute-start.12) | collective-permute-done | bytes 65568 | tf_op jit(solution)/shard_map/ppermute | solution.py:16
  41.0 0.0 collective-permute-done.13.refs_5_
  41.0 0.7 %shard_map.45 = f32[512,128]{1,0:T(8,128)} custom-call(f32[512,128]{1,0:T(8,128)S(1)} %shard_map.44.so_far_ref, f32[128,128]{1,0:T(8,128)S(1)} %get-tuple-element.28.solved_ref, bf16[384,1024]{1,0:T(8,128)(2,1)S(1)} %get-tuple-element.24.refs_0_.refs_1_, bf16[384,1024]{1,0:T(8,128)(2,1)S(1)} %get-tuple-element.25.refs_1_.refs_2_, ...), custom_call_target="tpu_custom_call" | custom-call | tf_op jit(solution)/shard_map/pallas_call | solution.py:20
  (2 shorter events, 0.0 us)
Async XLA Ops:
  0.0 16.3 %collective-permute-start.6 = (f32[64,1024]{1,0:T(8,128)}, f32[64,1024]{1,0:T(8,128)S(1)}, u32[]{:S(2)}, u32[]{:S(2)}) collective-permute-start(f32[64,1024]{1,0:T(8,128)} %refs_0_.1), channel_id=1, source_target_pairs={{0,4},{1,5},{2,6},{3,7},{4,0},{5,1},{6,2},{7,3},{8,12},{9,13},{10,... | collective-permute-start | bytes 786440 | tf_op jit(solution)/shard_map/ppermute | solution.py:16
  4.1 14.5 %collective-permute-start.4 = (f32[64,1024]{1,0:T(8,128)}, f32[64,1024]{1,0:T(8,128)S(1)}, u32[]{:S(2)}, u32[]{:S(2)}) collective-permute-start(f32[64,1024]{1,0:T(8,128)} %refs_0_.1), channel_id=1, source_target_pairs={{0,2},{1,3},{2,0},{3,1},{4,6},{5,7},{6,4},{7,5},{8,10},{9,11},{10,... | collective-permute-start | bytes 786440 | tf_op jit(solution)/shard_map/ppermute | solution.py:16
  7.3 11.2 %collective-permute-start = (f32[264,128]{1,0:T(8,128)S(1)}, f32[264,128]{1,0:T(8,128)S(1)}, u32[]{:S(2)}, u32[]{:S(2)}) collective-permute-start(f32[264,128]{1,0:T(8,128)S(1)} %get-tuple-element.19), channel_id=1, source_target_pairs={{0,16},{8,24},{16,0},{24,8},{1,17},{9,25},{17,1},{25,9},{2,18},{10... | collective-permute-start | bytes 405512 | tf_op jit(solution)/shard_map/ppermute | solution.py:16
  9.3 9.8 %collective-permute-start.1 = (f32[264,128]{1,0:T(8,128)S(1)}, f32[264,128]{1,0:T(8,128)S(1)}, u32[]{:S(2)}, u32[]{:S(2)}) collective-permute-start(f32[264,128]{1,0:T(8,128)S(1)} %get-tuple-element.20), channel_id=1, source_target_pairs={{0,24},{8,16},{16,8},{24,0},{1,25},{9,17},{17,9},{25,1},{2,26},{10... | collective-permute-start | bytes 405512 | tf_op jit(solution)/shard_map/ppermute | solution.py:16
  16.3 7.4 %collective-permute-start.8 = (f32[64,1024]{1,0:T(8,128)S(1)}, f32[64,1024]{1,0:T(8,128)S(1)}, u32[]{:S(2)}, u32[]{:S(2)}) collective-permute-start(f32[64,1024]{1,0:T(8,128)S(1)} %collective-permute-done.6.refs_4_), channel_id=1, source_target_pairs={{0,2},{1,3},{2,0},{3,1},{4,6},{5,7},{6,4},{7,5},{8,10},{9,11},{10,... | collective-permute-start | bytes 786440 | tf_op jit(solution)/shard_map/ppermute | solution.py:16
  17.0 8.2 %collective-permute-start.2 = (f32[512,128]{1,0:T(8,128)}, f32[512,128]{1,0:T(8,128)S(1)}, u32[]{:S(2)}, u32[]{:S(2)}) collective-permute-start(f32[512,128]{1,0:T(8,128)} %matrix_hbm.1), channel_id=1, source_target_pairs={{0,8},{8,0},{16,24},{24,16},{1,9},{9,1},{17,25},{25,17},{2,10},{10... | collective-permute-start | bytes 786440 | tf_op jit(solution)/shard_map/ppermute | solution.py:16
  18.5 7.3 %collective-permute-start.3 = (f32[64,1024]{1,0:T(8,128)}, f32[64,1024]{1,0:T(8,128)S(1)}, u32[]{:S(2)}, u32[]{:S(2)}) collective-permute-start(f32[64,1024]{1,0:T(8,128)} %refs_0_.1), channel_id=1, source_target_pairs={{0,1},{1,0},{2,3},{3,2},{4,5},{5,4},{6,7},{7,6},{8,9},{9,8},{10,11... | collective-permute-start | bytes 786440 | tf_op jit(solution)/shard_map/ppermute | solution.py:16
  18.5 7.3 %collective-permute-start.5 = (f32[64,1024]{1,0:T(8,128)S(1)}, f32[64,1024]{1,0:T(8,128)S(1)}, u32[]{:S(2)}, u32[]{:S(2)}) collective-permute-start(f32[64,1024]{1,0:T(8,128)S(1)} %collective-permute-done.4.refs_2_), channel_id=1, source_target_pairs={{0,1},{1,0},{2,3},{3,2},{4,5},{5,4},{6,7},{7,6},{8,9},{9,8},{10,11... | collective-permute-start | bytes 786440 | tf_op jit(solution)/shard_map/ppermute | solution.py:16
  19.0 6.8 %collective-permute-start.7 = (f32[64,1024]{1,0:T(8,128)S(1)}, f32[64,1024]{1,0:T(8,128)S(1)}, u32[]{:S(2)}, u32[]{:S(2)}) collective-permute-start(f32[64,1024]{1,0:T(8,128)S(1)} %collective-permute-done.6.refs_4_), channel_id=1, source_target_pairs={{0,1},{1,0},{2,3},{3,2},{4,5},{5,4},{6,7},{7,6},{8,9},{9,8},{10,11... | collective-permute-start | bytes 786440 | tf_op jit(solution)/shard_map/ppermute | solution.py:16
  23.7 6.3 %collective-permute-start.9 = (f32[64,1024]{1,0:T(8,128)S(1)}, f32[64,1024]{1,0:T(8,128)S(1)}, u32[]{:S(2)}, u32[]{:S(2)}) collective-permute-start(f32[64,1024]{1,0:T(8,128)S(1)} %collective-permute-done.8.refs_0_), channel_id=1, source_target_pairs={{0,1},{1,0},{2,3},{3,2},{4,5},{5,4},{6,7},{7,6},{8,9},{9,8},{10,11... | collective-permute-start | bytes 786440 | tf_op jit(solution)/shard_map/ppermute | solution.py:16
  25.2 1.0 %copy-start = (f32[64,1024]{1,0:T(8,128)S(1)}, f32[64,1024]{1,0:T(8,128)}, u32[]{:S(2)}) copy-start(f32[64,1024]{1,0:T(8,128)} %refs_0_.1) | copy-start | bytes 786436
  27.0 13.3 %collective-permute-start.10 = (f32[384,128]{1,0:T(8,128)S(1)}, f32[384,128]{1,0:T(8,128)S(1)}, u32[]{:S(2)}, u32[]{:S(2)}) collective-permute-start(f32[384,128]{1,0:T(8,128)S(1)} %shard_map.42.refs_0_), channel_id=1, source_target_pairs={{0,16},{8,24},{16,0},{24,8},{1,17},{9,25},{17,1},{25,9},{2,18},{10... | collective-permute-start | bytes 589832 | tf_op jit(solution)/shard_map/ppermute | solution.py:16
  28.0 12.3 %collective-permute-start.11 = (f32[384,128]{1,0:T(8,128)S(1)}, f32[384,128]{1,0:T(8,128)S(1)}, u32[]{:S(2)}, u32[]{:S(2)}) collective-permute-start(f32[384,128]{1,0:T(8,128)S(1)} %shard_map.42.refs_0_), channel_id=1, source_target_pairs={{0,24},{8,16},{16,8},{24,0},{1,25},{9,17},{17,9},{25,1},{2,26},{10... | collective-permute-start | bytes 589832 | tf_op jit(solution)/shard_map/ppermute | solution.py:16
  30.4 10.6 %collective-permute-start.12 = (f32[128,128]{1,0:T(8,128)S(1)}, f32[128,128]{1,0:T(8,128)S(1)}, u32[]{:S(2)}, u32[]{:S(2)}) collective-permute-start(f32[128,128]{1,0:T(8,128)S(1)} %get-tuple-element.28.solved_ref), channel_id=1, source_target_pairs={{0,16},{8,24},{16,0},{24,8},{1,17},{9,25},{17,1},{25,9},{2,18},{10... | collective-permute-start | bytes 196616 | tf_op jit(solution)/shard_map/ppermute | solution.py:16
  31.1 9.9 %collective-permute-start.13 = (f32[128,128]{1,0:T(8,128)S(1)}, f32[128,128]{1,0:T(8,128)S(1)}, u32[]{:S(2)}, u32[]{:S(2)}) collective-permute-start(f32[128,128]{1,0:T(8,128)S(1)} %get-tuple-element.28.solved_ref), channel_id=1, source_target_pairs={{0,24},{8,16},{16,8},{24,0},{1,25},{9,17},{17,9},{25,1},{2,26},{10... | collective-permute-start | bytes 196616 | tf_op jit(solution)/shard_map/ppermute | solution.py:16

commit v7 on v6

--- a/solution.py
+++ b/solution.py
@@ -300,12 +300,12 @@
         return [piece, swap(piece, "pcol", 1)]
 
     near = both(panel) + both(swap(panel, "pcol", 2))
-    first_at = [(mask, 0, depth) for mask in range(4)]
-    far, relayed, relayed_at = [], [], []
+    near_at = [(mask, 0, depth) for mask in range(4)]
+    far, far_at, relayed, relayed_at = [], [], [], []
     for mask in range(4, n_cols, 4):
         piece = swap(panel, "pcol", mask)
         far += both(piece)
-        first_at += [(mask, 0, depth), (mask + 1, 0, depth)]
+        far_at += [(mask, 0, depth), (mask + 1, 0, depth)]
         relayed += both(swap(piece, "pcol", 2))
         relayed_at += [(mask + 2, 0, depth), (mask + 3, 0, depth)]
 
@@ -351,35 +351,35 @@
     def result(group):
         return pltpu.VMEM((sum(count for _, _, count in group), cols), f32)
 
-    groups = (first_at, relayed_at)
-    split0 = call(early, terms(first_at), [], *near, *far)
-    first = call(functools.partial(solve, 1, sources), result(first_at), [], top, *split0)
-    second, *split1 = call(
-        functools.partial(solve, 0, sources), [result(relayed_at)] + terms(relayed_at), [],
-        top, *relayed,
-    )
-    solved = [first, second]
+    groups = (near_at, far_at, relayed_at)
+    split0 = call(early, terms(near_at), [], *near)
+    first = call(functools.partial(solve, 1, sources), result(near_at), [], top, *split0)
+    second, *split1 = call(functools.partial(solve, 0, sources), [result(far_at)] + terms(far_at), [], top, *far)
+    third, *split2 = call(
+        functools.partial(solve, 0, sources), [result(relayed_at)] + terms(relayed_at), [], top, *relayed
+    )
+    solved = [first, second, third]
     got = [swap(piece, "prow", mask) for piece in solved for mask in masks]
 
     scratch = [pltpu.VMEM((block, cols), f32)]
     if 2 * depth % lanes:
         return call(
-            functools.partial(update, sources, masks, groups, 0, 2),
+            functools.partial(update, sources, masks, groups, 0, 3),
             jax.ShapeDtypeStruct((rows, cols), f32),
             scratch,
-            own, *solved, *split0, *split1, *got,
+            own, *solved, *split0, *split1, *split2, *got,
         )
     so_far = call(
-        functools.partial(update, sources, masks, groups, 1, 2),
+        functools.partial(update, sources, masks, groups, 1, 3),
         pltpu.VMEM((rows, cols), f32),
         scratch,
-        own, *solved[:-1], *split0, *split1, *got[: -len(masks)],
+        own, *solved[:-1], *split0, *split1, *split2, *got[: -len(masks)],
     )
     return call(
-        functools.partial(finish, sources, masks, groups, 2),
+        functools.partial(finish, sources, masks, groups, 3),
         jax.ShapeDtypeStruct((rows, cols), f32),
         [pltpu.VMEM((sources * solved[-1].shape[0], cols), f32)],
-        so_far, solved[-1], *split0, *split1, *got[-len(masks) :],
+        so_far, solved[-1], *split0, *split1, *split2, *got[-len(masks) :],
     )
 
 

time: 41.9 us -> 49.6 us (1.18)
  waiting for transfers between devices: 19.5 us -> 24.9 us
  starting transfers between devices: 16.5 us -> 18.6 us
    ppermute x14 -> x16, waiting for transfers between devices: 19.5 us -> 24.9 us  [swap(): lax.ppermute(block, axis, [(i, i ^ mask) for i in range(lax.axis_size(axi...]
    ppermute x14 -> x16, starting transfers between devices: 16.5 us -> 18.6 us  [swap(): lax.ppermute(block, axis, [(i, i ^ mask) for i in range(lax.axis_size(axi...]
    pallas_call x9 -> x10, Pallas kernels: 5.35 us -> 5.52 us  [call(): pl.pallas_call(kernel, out_shape=out_shape, in_specs=[VMEM if inside else...]
  transfers between devices with their start and end apart: 14 -> 16, of which waited for: 5 -> 6; matrix products, arithmetic and copies ran while one was open for 0% -> 0% of each run, Pallas kernels for 11% -> 10%
where the time goes in v7:
time: 49.6 us; the launch traced here: 49.4 us
  waiting for transfers between devices  24.9 us (50%)
  starting transfers between devices  18.6 us (38%)
  Pallas kernels  5.52 us (11%)
    ppermute x16, waiting for transfers between devices, swap(): lax.ppermute(block, axis, [(i, i ^ mask) for i in range(lax.axis_size(axi...  24.9 us
    ppermute x16, starting transfers between devices, swap(): lax.ppermute(block, axis, [(i, i ^ mask) for i in range(lax.axis_size(axi...  18.6 us
    pallas_call x10, Pallas kernels, call(): pl.pallas_call(kernel, out_shape=out_shape, in_specs=[VMEM if inside else...  5.52 us
  transfers between devices with their start and end apart: 16, of which 6 were waited for; matrix products, arithmetic and copies ran while one was open for 0% of the time, Pallas kernels for 10%

profile of v7, /device:TPU:0, one launch (start us, length us, event | category | flops | bytes accessed | tf_op | source)
XLA Modules:
  0.0 49.4 jit_solution(18370112644164683643)
XLA Ops:
  0.0 4.1 %collective-permute-start.6 = (f32[64,1024]{1,0:T(8,128)}, f32[64,1024]{1,0:T(8,128)S(1)}, u32[]{:S(2)}, u32[]{:S(2)}) collective-permute-start(f32[64,1024]{1,0:T(8,128)} %refs_0_.1), channel_id=1, source_target_pairs={{0,4},{1,5},{2,6},{3,7},{4,0},{5,1},{6,2},{7,3},{8,12},{9,13},{10,... | collective-permute-start | bytes 786440 | tf_op jit(solution)/shard_map/ppermute | solution.py:16
  4.1 1.6 %collective-permute-start.4 = (f32[64,1024]{1,0:T(8,128)}, f32[64,1024]{1,0:T(8,128)S(1)}, u32[]{:S(2)}, u32[]{:S(2)}) collective-permute-start(f32[64,1024]{1,0:T(8,128)} %refs_0_.1), channel_id=1, source_target_pairs={{0,2},{1,3},{2,0},{3,1},{4,6},{5,7},{6,4},{7,5},{8,10},{9,11},{10,... | collective-permute-start | bytes 786440 | tf_op jit(solution)/shard_map/ppermute | solution.py:16
  5.6 10.7 %collective-permute-done.6.refs_0_ = f32[64,1024]{1,0:T(8,128)S(1)} collective-permute-done((f32[64,1024]{1,0:T(8,128)}, f32[64,1024]{1,0:T(8,128)S(1)}, u32[]{:S(2)}, u32[]{:S(2)}) %collective-permute-start.6) | collective-permute-done | bytes 262176 | tf_op jit(solution)/shard_map/ppermute | solution.py:16
  16.3 0.7 %collective-permute-start.8 = (f32[64,1024]{1,0:T(8,128)S(1)}, f32[64,1024]{1,0:T(8,128)S(1)}, u32[]{:S(2)}, u32[]{:S(2)}) collective-permute-start(f32[64,1024]{1,0:T(8,128)S(1)} %collective-permute-done.6.refs_0_), channel_id=1, source_target_pairs={{0,2},{1,3},{2,0},{3,1},{4,6},{5,7},{6,4},{7,5},{8,10},{9,11},{10,... | collective-permute-start | bytes 786440 | tf_op jit(solution)/shard_map/ppermute | solution.py:16
  17.0 1.7 %shard_map.37 = (f32[264,128]{1,0:T(8,128)S(1)}, f32[264,128]{1,0:T(8,128)S(1)}, s32[512,128]{1,0:T(8,128)S(1)}, s32[1,1024]{1,0:T(1,128)S(1)}, f32[512,128]{1,0:T(8,128)S(1)}) custom-call(s32[1,1024]{1,0:T(1,128)} %bitcast.1, f32[512,128]{1,0:T(8,128)} %matrix_hbm.1), custom_call_target="tpu_custom_call" | custom-call | tf_op jit(solution)/shard_map/pallas_call | solution.py:20
  18.7 1.9 %collective-permute-start = (f32[264,128]{1,0:T(8,128)S(1)}, f32[264,128]{1,0:T(8,128)S(1)}, u32[]{:S(2)}, u32[]{:S(2)}) collective-permute-start(f32[264,128]{1,0:T(8,128)S(1)} %get-tuple-element.22), channel_id=1, source_target_pairs={{0,16},{8,24},{16,0},{24,8},{1,17},{9,25},{17,1},{25,9},{2,18},{10... | collective-permute-start | bytes 405512 | tf_op jit(solution)/shard_map/ppermute | solution.py:16
  20.7 1.1 %collective-permute-start.1 = (f32[264,128]{1,0:T(8,128)S(1)}, f32[264,128]{1,0:T(8,128)S(1)}, u32[]{:S(2)}, u32[]{:S(2)}) collective-permute-start(f32[264,128]{1,0:T(8,128)S(1)} %get-tuple-element.23), channel_id=1, source_target_pairs={{0,24},{8,16},{16,8},{24,0},{1,25},{9,17},{17,9},{25,1},{2,26},{10... | collective-permute-start | bytes 405512 | tf_op jit(solution)/shard_map/ppermute | solution.py:16
  21.7 0.5 %collective-permute-start.2 = (f32[512,128]{1,0:T(8,128)}, f32[512,128]{1,0:T(8,128)S(1)}, u32[]{:S(2)}, u32[]{:S(2)}) collective-permute-start(f32[512,128]{1,0:T(8,128)} %matrix_hbm.1), channel_id=1, source_target_pairs={{0,8},{8,0},{16,24},{24,16},{1,9},{9,1},{17,25},{25,17},{2,10},{10... | collective-permute-start | bytes 786440 | tf_op jit(solution)/shard_map/ppermute | solution.py:16
  22.3 4.0 %collective-permute-done.refs_0_.refs_2_ = f32[264,128]{1,0:T(8,128)S(1)} collective-permute-done((f32[264,128]{1,0:T(8,128)S(1)}, f32[264,128]{1,0:T(8,128)S(1)}, u32[]{:S(2)}, u32[]{:S(2)}) %collective-permute-start) | collective-permute-done | bytes 135200 | tf_op jit(solution)/shard_map/ppermute | solution.py:16
  26.3 0.0 collective-permute-start.3
  26.3 0.0 collective-permute-done.4.refs_2_
  26.3 0.5 %collective-permute-start.5 = (f32[64,1024]{1,0:T(8,128)S(1)}, f32[64,1024]{1,0:T(8,128)S(1)}, u32[]{:S(2)}, u32[]{:S(2)}) collective-permute-start(f32[64,1024]{1,0:T(8,128)S(1)} %collective-permute-done.4.refs_2_), channel_id=1, source_target_pairs={{0,1},{1,0},{2,3},{3,2},{4,5},{5,4},{6,7},{7,6},{8,9},{9,8},{10,11... | collective-permute-start | bytes 786440 | tf_op jit(solution)/shard_map/ppermute | solution.py:16
  26.8 1.2 %collective-permute-done.1.refs_1_.refs_3_ = f32[264,128]{1,0:T(8,128)S(1)} collective-permute-done((f32[264,128]{1,0:T(8,128)S(1)}, f32[264,128]{1,0:T(8,128)S(1)}, u32[]{:S(2)}, u32[]{:S(2)}) %collective-permute-start.1) | collective-permute-done | bytes 135200 | tf_op jit(solution)/shard_map/ppermute | solution.py:16
  28.0 0.0 collective-permute-start.7
  28.0 0.0 collective-permute-done.8.refs_0_
  28.0 0.5 %collective-permute-start.9 = (f32[64,1024]{1,0:T(8,128)S(1)}, f32[64,1024]{1,0:T(8,128)S(1)}, u32[]{:S(2)}, u32[]{:S(2)}) collective-permute-start(f32[64,1024]{1,0:T(8,128)S(1)} %collective-permute-done.8.refs_0_), channel_id=1, source_target_pairs={{0,1},{1,0},{2,3},{3,2},{4,5},{5,4},{6,7},{7,6},{8,9},{9,8},{10,11... | collective-permute-start | bytes 786440 | tf_op jit(solution)/shard_map/ppermute | solution.py:16
  28.5 1.1 %shard_map.39 = (bf16[1024,768]{1,0:T(8,128)(2,1)S(1)}, f32[1024,128]{1,0:T(8,128)S(1)}) custom-call(s32[1,1024]{1,0:T(1,128)S(1)} %get-tuple-element.24.piv_row), custom_call_target="tpu_custom_call" | custom-call | tf_op jit(solution)/shard_map/pallas_call | solution.py:20
  29.6 1.5 %collective-permute-done.2.refs_1_ = f32[512,128]{1,0:T(8,128)S(1)} collective-permute-done((f32[512,128]{1,0:T(8,128)}, f32[512,128]{1,0:T(8,128)S(1)}, u32[]{:S(2)}, u32[]{:S(2)}) %collective-permute-start.2) | collective-permute-done | bytes 262176 | tf_op jit(solution)/shard_map/ppermute | solution.py:16
  31.1 0.0 copy-start
  31.1 0.6 %shard_map.40.top_ref = bf16[1024,256]{1,0:T(8,128)(2,1)S(1)} custom-call(bf16[1024,768]{1,0:T(8,128)(2,1)S(1)} %get-tuple-element.25.chosen_ref, f32[1024,128]{1,0:T(8,128)S(1)} %get-tuple-element.26.keep_ref, f32[512,128]{1,0:T(8,128)S(1)} %get-tuple-element.21.matrix_ref.refs_0_, f32[512,128]{1,0:T(8,128)S(1)} %collective-permute-done.2.refs_1_, ...), custom_call_target="tpu_custom_call" | custom-call | tf_op jit(solution)/shard_map/pallas_call | solution.py:20
  31.7 0.0 collective-permute-done.3.refs_1_
  31.7 0.0 collective-permute-done.5.refs_3_
  31.7 0.3 copy-done
  32.0 0.2 shard_map.41
  32.2 0.4 shard_map.42.refs_0_
  32.7 1.3 %collective-permute-start.10 = (f32[256,128]{1,0:T(8,128)S(1)}, f32[256,128]{1,0:T(8,128)S(1)}, u32[]{:S(2)}, u32[]{:S(2)}) collective-permute-start(f32[256,128]{1,0:T(8,128)S(1)} %shard_map.42.refs_0_), channel_id=1, source_target_pairs={{0,16},{8,24},{16,0},{24,8},{1,17},{9,25},{17,1},{25,9},{2,18},{10... | collective-permute-start | bytes 393224 | tf_op jit(solution)/shard_map/ppermute | solution.py:16
  34.0 1.7 %collective-permute-start.11 = (f32[256,128]{1,0:T(8,128)S(1)}, f32[256,128]{1,0:T(8,128)S(1)}, u32[]{:S(2)}, u32[]{:S(2)}) collective-permute-start(f32[256,128]{1,0:T(8,128)S(1)} %shard_map.42.refs_0_), channel_id=1, source_target_pairs={{0,24},{8,16},{16,8},{24,0},{1,25},{9,17},{17,9},{25,1},{2,26},{10... | collective-permute-start | bytes 393224 | tf_op jit(solution)/shard_map/ppermute | solution.py:16
  35.7 0.0 collective-permute-done.7.refs_1_
  35.7 0.4 shard_map.43
  36.1 1.0 %collective-permute-start.12 = (f32[128,128]{1,0:T(8,128)S(1)}, f32[128,128]{1,0:T(8,128)S(1)}, u32[]{:S(2)}, u32[]{:S(2)}) collective-permute-start(f32[128,128]{1,0:T(8,128)S(1)} %get-tuple-element.29.refs_1_), channel_id=1, source_target_pairs={{0,16},{8,24},{16,0},{24,8},{1,17},{9,25},{17,1},{25,9},{2,18},{10... | collective-permute-start | bytes 196616 | tf_op jit(solution)/shard_map/ppermute | solution.py:16
  37.1 1.0 %collective-permute-start.13 = (f32[128,128]{1,0:T(8,128)S(1)}, f32[128,128]{1,0:T(8,128)S(1)}, u32[]{:S(2)}, u32[]{:S(2)}) collective-permute-start(f32[128,128]{1,0:T(8,128)S(1)} %get-tuple-element.29.refs_1_), channel_id=1, source_target_pairs={{0,24},{8,16},{16,8},{24,0},{1,25},{9,17},{17,9},{25,1},{2,26},{10... | collective-permute-start | bytes 196616 | tf_op jit(solution)/shard_map/ppermute | solution.py:16
  38.1 0.0 collective-permute-done.9.refs_1_
  38.1 0.4 shard_map.44
  38.5 0.7 %collective-permute-start.14 = (f32[128,128]{1,0:T(8,128)S(1)}, f32[128,128]{1,0:T(8,128)S(1)}, u32[]{:S(2)}, u32[]{:S(2)}) collective-permute-start(f32[128,128]{1,0:T(8,128)S(1)} %get-tuple-element.34.solved_ref), channel_id=1, source_target_pairs={{0,16},{8,24},{16,0},{24,8},{1,17},{9,25},{17,1},{25,9},{2,18},{10... | collective-permute-start | bytes 196616 | tf_op jit(solution)/shard_map/ppermute | solution.py:16
  39.2 4.3 %collective-permute-done.12.refs_10_ = f32[128,128]{1,0:T(8,128)S(1)} collective-permute-done((f32[128,128]{1,0:T(8,128)S(1)}, f32[128,128]{1,0:T(8,128)S(1)}, u32[]{:S(2)}, u32[]{:S(2)}) %collective-permute-start.12) | collective-permute-done | bytes 65568 | tf_op jit(solution)/shard_map/ppermute | solution.py:16
  43.5 1.9 %collective-permute-start.15 = (f32[128,128]{1,0:T(8,128)S(1)}, f32[128,128]{1,0:T(8,128)S(1)}, u32[]{:S(2)}, u32[]{:S(2)}) collective-permute-start(f32[128,128]{1,0:T(8,128)S(1)} %get-tuple-element.34.solved_ref), channel_id=1, source_target_pairs={{0,24},{8,16},{16,8},{24,0},{1,25},{9,17},{17,9},{25,1},{2,26},{10... | collective-permute-start | bytes 196616 | tf_op jit(solution)/shard_map/ppermute | solution.py:16
  45.5 0.0 collective-permute-done.13.refs_11_
  45.5 0.0 collective-permute-done.10.refs_8_
  45.5 0.0 collective-permute-done.11.refs_9_
  45.5 0.0 collective-permute-done.14.refs_6_
  45.5 3.2 %collective-permute-done.15.refs_7_ = f32[128,128]{1,0:T(8,128)S(1)} collective-permute-done((f32[128,128]{1,0:T(8,128)S(1)}, f32[128,128]{1,0:T(8,128)S(1)}, u32[]{:S(2)}, u32[]{:S(2)}) %collective-permute-start.15) | collective-permute-done | bytes 65568 | tf_op jit(solution)/shard_map/ppermute | solution.py:16
  48.7 0.7 %shard_map.46 = f32[512,128]{1,0:T(8,128)} custom-call(f32[512,128]{1,0:T(8,128)S(1)} %shard_map.45.so_far_ref, f32[128,128]{1,0:T(8,128)S(1)} %get-tuple-element.34.solved_ref, bf16[256,1024]{1,0:T(8,128)(2,1)S(1)} %get-tuple-element.27.refs_0_.refs_2_, bf16[256,1024]{1,0:T(8,128)(2,1)S(1)} %get-tuple-element.28.refs_1_.refs_3_, ...), custom_call_target="tpu_custom_call" | custom-call | tf_op jit(solution)/shard_map/pallas_call | solution.py:20
  (2 shorter events, 0.0 us)
Async XLA Ops:
  0.0 16.3 %collective-permute-start.6 = (f32[64,1024]{1,0:T(8,128)}, f32[64,1024]{1,0:T(8,128)S(1)}, u32[]{:S(2)}, u32[]{:S(2)}) collective-permute-start(f32[64,1024]{1,0:T(8,128)} %refs_0_.1), channel_id=1, source_target_pairs={{0,4},{1,5},{2,6},{3,7},{4,0},{5,1},{6,2},{7,3},{8,12},{9,13},{10,... | collective-permute-start | bytes 786440 | tf_op jit(solution)/shard_map/ppermute | solution.py:16
  4.1 22.3 %collective-permute-start.4 = (f32[64,1024]{1,0:T(8,128)}, f32[64,1024]{1,0:T(8,128)S(1)}, u32[]{:S(2)}, u32[]{:S(2)}) collective-permute-start(f32[64,1024]{1,0:T(8,128)} %refs_0_.1), channel_id=1, source_target_pairs={{0,2},{1,3},{2,0},{3,1},{4,6},{5,7},{6,4},{7,5},{8,10},{9,11},{10,... | collective-permute-start | bytes 786440 | tf_op jit(solution)/shard_map/ppermute | solution.py:16
  16.3 11.7 %collective-permute-start.8 = (f32[64,1024]{1,0:T(8,128)S(1)}, f32[64,1024]{1,0:T(8,128)S(1)}, u32[]{:S(2)}, u32[]{:S(2)}) collective-permute-start(f32[64,1024]{1,0:T(8,128)S(1)} %collective-permute-done.6.refs_0_), channel_id=1, source_target_pairs={{0,2},{1,3},{2,0},{3,1},{4,6},{5,7},{6,4},{7,5},{8,10},{9,11},{10,... | collective-permute-start | bytes 786440 | tf_op jit(solution)/shard_map/ppermute | solution.py:16
  18.7 7.6 %collective-permute-start = (f32[264,128]{1,0:T(8,128)S(1)}, f32[264,128]{1,0:T(8,128)S(1)}, u32[]{:S(2)}, u32[]{:S(2)}) collective-permute-start(f32[264,128]{1,0:T(8,128)S(1)} %get-tuple-element.22), channel_id=1, source_target_pairs={{0,16},{8,24},{16,0},{24,8},{1,17},{9,25},{17,1},{25,9},{2,18},{10... | collective-permute-start | bytes 405512 | tf_op jit(solution)/shard_map/ppermute | solution.py:16
  20.7 7.4 %collective-permute-start.1 = (f32[264,128]{1,0:T(8,128)S(1)}, f32[264,128]{1,0:T(8,128)S(1)}, u32[]{:S(2)}, u32[]{:S(2)}) collective-permute-start(f32[264,128]{1,0:T(8,128)S(1)} %get-tuple-element.23), channel_id=1, source_target_pairs={{0,24},{8,16},{16,8},{24,0},{1,25},{9,17},{17,9},{25,1},{2,26},{10... | collective-permute-start | bytes 405512 | tf_op jit(solution)/shard_map/ppermute | solution.py:16
  21.7 9.3 %collective-permute-start.2 = (f32[512,128]{1,0:T(8,128)}, f32[512,128]{1,0:T(8,128)S(1)}, u32[]{:S(2)}, u32[]{:S(2)}) collective-permute-start(f32[512,128]{1,0:T(8,128)} %matrix_hbm.1), channel_id=1, source_target_pairs={{0,8},{8,0},{16,24},{24,16},{1,9},{9,1},{17,25},{25,17},{2,10},{10... | collective-permute-start | bytes 786440 | tf_op jit(solution)/shard_map/ppermute | solution.py:16
  26.3 5.4 %collective-permute-start.3 = (f32[64,1024]{1,0:T(8,128)}, f32[64,1024]{1,0:T(8,128)S(1)}, u32[]{:S(2)}, u32[]{:S(2)}) collective-permute-start(f32[64,1024]{1,0:T(8,128)} %refs_0_.1), channel_id=1, source_target_pairs={{0,1},{1,0},{2,3},{3,2},{4,5},{5,4},{6,7},{7,6},{8,9},{9,8},{10,11... | collective-permute-start | bytes 786440 | tf_op jit(solution)/shard_map/ppermute | solution.py:16
  26.3 5.4 %collective-permute-start.5 = (f32[64,1024]{1,0:T(8,128)S(1)}, f32[64,1024]{1,0:T(8,128)S(1)}, u32[]{:S(2)}, u32[]{:S(2)}) collective-permute-start(f32[64,1024]{1,0:T(8,128)S(1)} %collective-permute-done.4.refs_2_), channel_id=1, source_target_pairs={{0,1},{1,0},{2,3},{3,2},{4,5},{5,4},{6,7},{7,6},{8,9},{9,8},{10,11... | collective-permute-start | bytes 786440 | tf_op jit(solution)/shard_map/ppermute | solution.py:16
  28.0 7.6 %collective-permute-start.7 = (f32[64,1024]{1,0:T(8,128)S(1)}, f32[64,1024]{1,0:T(8,128)S(1)}, u32[]{:S(2)}, u32[]{:S(2)}) collective-permute-start(f32[64,1024]{1,0:T(8,128)S(1)} %collective-permute-done.6.refs_0_), channel_id=1, source_target_pairs={{0,1},{1,0},{2,3},{3,2},{4,5},{5,4},{6,7},{7,6},{8,9},{9,8},{10,11... | collective-permute-start | bytes 786440 | tf_op jit(solution)/shard_map/ppermute | solution.py:16
  28.0 10.1 %collective-permute-start.9 = (f32[64,1024]{1,0:T(8,128)S(1)}, f32[64,1024]{1,0:T(8,128)S(1)}, u32[]{:S(2)}, u32[]{:S(2)}) collective-permute-start(f32[64,1024]{1,0:T(8,128)S(1)} %collective-permute-done.8.refs_0_), channel_id=1, source_target_pairs={{0,1},{1,0},{2,3},{3,2},{4,5},{5,4},{6,7},{7,6},{8,9},{9,8},{10,11... | collective-permute-start | bytes 786440 | tf_op jit(solution)/shard_map/ppermute | solution.py:16
  31.1 1.0 %copy-start = (f32[64,1024]{1,0:T(8,128)S(1)}, f32[64,1024]{1,0:T(8,128)}, u32[]{:S(2)}) copy-start(f32[64,1024]{1,0:T(8,128)} %refs_0_.1) | copy-start | bytes 786436
  32.7 12.8 %collective-permute-start.10 = (f32[256,128]{1,0:T(8,128)S(1)}, f32[256,128]{1,0:T(8,128)S(1)}, u32[]{:S(2)}, u32[]{:S(2)}) collective-permute-start(f32[256,128]{1,0:T(8,128)S(1)} %shard_map.42.refs_0_), channel_id=1, source_target_pairs={{0,16},{8,24},{16,0},{24,8},{1,17},{9,25},{17,1},{25,9},{2,18},{10... | collective-permute-start | bytes 393224 | tf_op jit(solution)/shard_map/ppermute | solution.py:16
  34.0 11.5 %collective-permute-start.11 = (f32[256,128]{1,0:T(8,128)S(1)}, f32[256,128]{1,0:T(8,128)S(1)}, u32[]{:S(2)}, u32[]{:S(2)}) collective-permute-start(f32[256,128]{1,0:T(8,128)S(1)} %shard_map.42.refs_0_), channel_id=1, source_target_pairs={{0,24},{8,16},{16,8},{24,0},{1,25},{9,17},{17,9},{25,1},{2,26},{10... | collective-permute-start | bytes 393224 | tf_op jit(solution)/shard_map/ppermute | solution.py:16
  36.1 7.5 %collective-permute-start.12 = (f32[128,128]{1,0:T(8,128)S(1)}, f32[128,128]{1,0:T(8,128)S(1)}, u32[]{:S(2)}, u32[]{:S(2)}) collective-permute-start(f32[128,128]{1,0:T(8,128)S(1)} %get-tuple-element.29.refs_1_), channel_id=1, source_target_pairs={{0,16},{8,24},{16,0},{24,8},{1,17},{9,25},{17,1},{25,9},{2,18},{10... | collective-permute-start | bytes 196616 | tf_op jit(solution)/shard_map/ppermute | solution.py:16
  37.1 8.4 %collective-permute-start.13 = (f32[128,128]{1,0:T(8,128)S(1)}, f32[128,128]{1,0:T(8,128)S(1)}, u32[]{:S(2)}, u32[]{:S(2)}) collective-permute-start(f32[128,128]{1,0:T(8,128)S(1)} %get-tuple-element.29.refs_1_), channel_id=1, source_target_pairs={{0,24},{8,16},{16,8},{24,0},{1,25},{9,17},{17,9},{25,1},{2,26},{10... | collective-permute-start | bytes 196616 | tf_op jit(solution)/shard_map/ppermute | solution.py:16
  38.5 7.0 %collective-permute-start.14 = (f32[128,128]{1,0:T(8,128)S(1)}, f32[128,128]{1,0:T(8,128)S(1)}, u32[]{:S(2)}, u32[]{:S(2)}) collective-permute-start(f32[128,128]{1,0:T(8,128)S(1)} %get-tuple-element.34.solved_ref), channel_id=1, source_target_pairs={{0,16},{8,24},{16,0},{24,8},{1,17},{9,25},{17,1},{25,9},{2,18},{10... | collective-permute-start | bytes 196616 | tf_op jit(solution)/shard_map/ppermute | solution.py:16
  43.5 5.2 %collective-permute-start.15 = (f32[128,128]{1,0:T(8,128)S(1)}, f32[128,128]{1,0:T(8,128)S(1)}, u32[]{:S(2)}, u32[]{:S(2)}) collective-permute-start(f32[128,128]{1,0:T(8,128)S(1)} %get-tuple-element.34.solved_ref), channel_id=1, source_target_pairs={{0,24},{8,16},{16,8},{24,0},{1,25},{9,17},{17,9},{25,1},{2,26},{10... | collective-permute-start | bytes 196616 | tf_op jit(solution)/shard_map/ppermute | solution.py:16

commit v8 on v7

--- a/solution.py
+++ b/solution.py
@@ -300,8 +300,10 @@
         return [piece, swap(piece, "pcol", 1)]
 
     near = both(panel) + both(swap(panel, "pcol", 2))
-    near_at = [(mask, 0, depth) for mask in range(4)]
-    far, far_at, relayed, relayed_at = [], [], [], []
+    near, far = near[:2], near[2:]
+    near_at = [(mask, 0, depth) for mask in range(2)]
+    far_at = [(mask, 0, depth) for mask in range(2, 4)]
+    relayed, relayed_at = [], []
     for mask in range(4, n_cols, 4):
         piece = swap(panel, "pcol", mask)
         far += both(piece)

time: 49.6 us -> 49.1 us (0.990)
  starting transfers between devices: 18.6 us -> 17.3 us
  waiting for transfers between devices: 24.9 us -> 25.9 us
    ppermute x16, starting transfers between devices: 18.6 us -> 17.3 us  [swap(): lax.ppermute(block, axis, [(i, i ^ mask) for i in range(lax.axis_size(axi...]
    ppermute x16, waiting for transfers between devices: 24.9 us -> 25.9 us  [swap(): lax.ppermute(block, axis, [(i, i ^ mask) for i in range(lax.axis_size(axi...]
where the time goes in v8:
time: 49.1 us; the launch traced here: 48.9 us
  waiting for transfers between devices  25.9 us (53%)
  starting transfers between devices  17.3 us (35%)
  Pallas kernels  5.53 us (11%)
    ppermute x16, waiting for transfers between devices, swap(): lax.ppermute(block, axis, [(i, i ^ mask) for i in range(lax.axis_size(axi...  25.9 us
    ppermute x16, starting transfers between devices, swap(): lax.ppermute(block, axis, [(i, i ^ mask) for i in range(lax.axis_size(axi...  17.3 us
    pallas_call x10, Pallas kernels, call(): pl.pallas_call(kernel, out_shape=out_shape, in_specs=[VMEM if inside else...  5.53 us
  transfers between devices with their start and end apart: 16, of which 6 were waited for; matrix products, arithmetic and copies ran while one was open for 0% of the time, Pallas kernels for 10%

profile of v8, /device:TPU:0, one launch (start us, length us, event | category | flops | bytes accessed | tf_op | source)
XLA Modules:
  0.0 48.9 jit_solution(14899569676910047912)
XLA Ops:
  0.0 4.1 %collective-permute-start.6 = (f32[64,1024]{1,0:T(8,128)}, f32[64,1024]{1,0:T(8,128)S(1)}, u32[]{:S(2)}, u32[]{:S(2)}) collective-permute-start(f32[64,1024]{1,0:T(8,128)} %refs_0_.1), channel_id=1, source_target_pairs={{0,4},{1,5},{2,6},{3,7},{4,0},{5,1},{6,2},{7,3},{8,12},{9,13},{10,... | collective-permute-start | bytes 786440 | tf_op jit(solution)/shard_map/ppermute | solution.py:16
  4.1 1.6 %collective-permute-start.4 = (f32[64,1024]{1,0:T(8,128)}, f32[64,1024]{1,0:T(8,128)S(1)}, u32[]{:S(2)}, u32[]{:S(2)}) collective-permute-start(f32[64,1024]{1,0:T(8,128)} %refs_0_.1), channel_id=1, source_target_pairs={{0,2},{1,3},{2,0},{3,1},{4,6},{5,7},{6,4},{7,5},{8,10},{9,11},{10,... | collective-permute-start | bytes 786440 | tf_op jit(solution)/shard_map/ppermute | solution.py:16
  5.6 10.7 %collective-permute-done.6.refs_2_ = f32[64,1024]{1,0:T(8,128)S(1)} collective-permute-done((f32[64,1024]{1,0:T(8,128)}, f32[64,1024]{1,0:T(8,128)S(1)}, u32[]{:S(2)}, u32[]{:S(2)}) %collective-permute-start.6) | collective-permute-done | bytes 262176 | tf_op jit(solution)/shard_map/ppermute | solution.py:16
  16.3 0.7 %collective-permute-start.8 = (f32[64,1024]{1,0:T(8,128)S(1)}, f32[64,1024]{1,0:T(8,128)S(1)}, u32[]{:S(2)}, u32[]{:S(2)}) collective-permute-start(f32[64,1024]{1,0:T(8,128)S(1)} %collective-permute-done.6.refs_2_), channel_id=1, source_target_pairs={{0,2},{1,3},{2,0},{3,1},{4,6},{5,7},{6,4},{7,5},{8,10},{9,11},{10,... | collective-permute-start | bytes 786440 | tf_op jit(solution)/shard_map/ppermute | solution.py:16
  17.0 1.7 %shard_map.37 = (f32[264,128]{1,0:T(8,128)S(1)}, f32[264,128]{1,0:T(8,128)S(1)}, s32[512,128]{1,0:T(8,128)S(1)}, s32[1,1024]{1,0:T(1,128)S(1)}, f32[512,128]{1,0:T(8,128)S(1)}) custom-call(s32[1,1024]{1,0:T(1,128)} %bitcast.1, f32[512,128]{1,0:T(8,128)} %matrix_hbm.1), custom_call_target="tpu_custom_call" | custom-call | tf_op jit(solution)/shard_map/pallas_call | solution.py:20
  18.7 1.9 %collective-permute-start = (f32[264,128]{1,0:T(8,128)S(1)}, f32[264,128]{1,0:T(8,128)S(1)}, u32[]{:S(2)}, u32[]{:S(2)}) collective-permute-start(f32[264,128]{1,0:T(8,128)S(1)} %get-tuple-element.22), channel_id=1, source_target_pairs={{0,16},{8,24},{16,0},{24,8},{1,17},{9,25},{17,1},{25,9},{2,18},{10... | collective-permute-start | bytes 405512 | tf_op jit(solution)/shard_map/ppermute | solution.py:16
  20.7 1.1 %collective-permute-start.1 = (f32[264,128]{1,0:T(8,128)S(1)}, f32[264,128]{1,0:T(8,128)S(1)}, u32[]{:S(2)}, u32[]{:S(2)}) collective-permute-start(f32[264,128]{1,0:T(8,128)S(1)} %get-tuple-element.23), channel_id=1, source_target_pairs={{0,24},{8,16},{16,8},{24,0},{1,25},{9,17},{17,9},{25,1},{2,26},{10... | collective-permute-start | bytes 405512 | tf_op jit(solution)/shard_map/ppermute | solution.py:16
  21.7 0.5 %collective-permute-start.2 = (f32[512,128]{1,0:T(8,128)}, f32[512,128]{1,0:T(8,128)S(1)}, u32[]{:S(2)}, u32[]{:S(2)}) collective-permute-start(f32[512,128]{1,0:T(8,128)} %matrix_hbm.1), channel_id=1, source_target_pairs={{0,8},{8,0},{16,24},{24,16},{1,9},{9,1},{17,25},{25,17},{2,10},{10... | collective-permute-start | bytes 786440 | tf_op jit(solution)/shard_map/ppermute | solution.py:16
  22.3 0.0 collective-permute-done.4.refs_0_
  22.3 0.0 collective-permute-start.5
  22.3 4.0 %collective-permute-done.refs_0_.refs_2_ = f32[264,128]{1,0:T(8,128)S(1)} collective-permute-done((f32[264,128]{1,0:T(8,128)S(1)}, f32[264,128]{1,0:T(8,128)S(1)}, u32[]{:S(2)}, u32[]{:S(2)}) %collective-permute-start) | collective-permute-done | bytes 135200 | tf_op jit(solution)/shard_map/ppermute | solution.py:16
  26.3 0.0 collective-permute-start.7
  26.3 1.7 %collective-permute-done.1.refs_1_.refs_3_ = f32[264,128]{1,0:T(8,128)S(1)} collective-permute-done((f32[264,128]{1,0:T(8,128)S(1)}, f32[264,128]{1,0:T(8,128)S(1)}, u32[]{:S(2)}, u32[]{:S(2)}) %collective-permute-start.1) | collective-permute-done | bytes 135200 | tf_op jit(solution)/shard_map/ppermute | solution.py:16
  28.0 0.0 collective-permute-start.3
  28.0 0.0 collective-permute-done.8.refs_0_
  28.0 0.5 %collective-permute-start.9 = (f32[64,1024]{1,0:T(8,128)S(1)}, f32[64,1024]{1,0:T(8,128)S(1)}, u32[]{:S(2)}, u32[]{:S(2)}) collective-permute-start(f32[64,1024]{1,0:T(8,128)S(1)} %collective-permute-done.8.refs_0_), channel_id=1, source_target_pairs={{0,1},{1,0},{2,3},{3,2},{4,5},{5,4},{6,7},{7,6},{8,9},{9,8},{10,11... | collective-permute-start | bytes 786440 | tf_op jit(solution)/shard_map/ppermute | solution.py:16
  28.6 1.1 %shard_map.39 = (bf16[1024,768]{1,0:T(8,128)(2,1)S(1)}, f32[1024,128]{1,0:T(8,128)S(1)}) custom-call(s32[1,1024]{1,0:T(1,128)S(1)} %get-tuple-element.24.piv_row), custom_call_target="tpu_custom_call" | custom-call | tf_op jit(solution)/shard_map/pallas_call | solution.py:20
  29.6 1.5 %collective-permute-done.2.refs_1_ = f32[512,128]{1,0:T(8,128)S(1)} collective-permute-done((f32[512,128]{1,0:T(8,128)}, f32[512,128]{1,0:T(8,128)S(1)}, u32[]{:S(2)}, u32[]{:S(2)}) %collective-permute-start.2) | collective-permute-done | bytes 262176 | tf_op jit(solution)/shard_map/ppermute | solution.py:16
  31.1 0.6 %shard_map.40.top_ref = bf16[1024,256]{1,0:T(8,128)(2,1)S(1)} custom-call(bf16[1024,768]{1,0:T(8,128)(2,1)S(1)} %get-tuple-element.25.chosen_ref, f32[1024,128]{1,0:T(8,128)S(1)} %get-tuple-element.26.keep_ref, f32[512,128]{1,0:T(8,128)S(1)} %get-tuple-element.21.matrix_ref.refs_0_, f32[512,128]{1,0:T(8,128)S(1)} %collective-permute-done.2.refs_1_, ...), custom_call_target="tpu_custom_call" | custom-call | tf_op jit(solution)/shard_map/pallas_call | solution.py:20
  31.7 0.0 copy-start
  31.7 0.0 collective-permute-done.5.refs_1_
  31.7 0.0 collective-permute-done.7.refs_3_
  31.8 0.6 %shard_map.43 = (f32[256,128]{1,0:T(8,128)S(1)}, bf16[256,1024]{1,0:T(8,128)(2,1)S(1)}, bf16[256,1024]{1,0:T(8,128)(2,1)S(1)}) custom-call(bf16[1024,256]{1,0:T(8,128)(2,1)S(1)} %shard_map.40.top_ref, f32[64,1024]{1,0:T(8,128)S(1)} %collective-permute-done.4.refs_0_, f32[64,1024]{1,0:T(8,128)S(1)} %collective-permute-done.5.refs_1_, ...), custom_call_target="tpu_custom_call" | custom-call | tf_op jit(solution)/shard_map/pallas_call | solution.py:20
  32.4 0.6 %collective-permute-start.12 = (f32[256,128]{1,0:T(8,128)S(1)}, f32[256,128]{1,0:T(8,128)S(1)}, u32[]{:S(2)}, u32[]{:S(2)}) collective-permute-start(f32[256,128]{1,0:T(8,128)S(1)} %get-tuple-element.29.refs_1_), channel_id=1, source_target_pairs={{0,16},{8,24},{16,0},{24,8},{1,17},{9,25},{17,1},{25,9},{2,18},{10... | collective-permute-start | bytes 393224 | tf_op jit(solution)/shard_map/ppermute | solution.py:16
  33.0 2.4 %collective-permute-start.13 = (f32[256,128]{1,0:T(8,128)S(1)}, f32[256,128]{1,0:T(8,128)S(1)}, u32[]{:S(2)}, u32[]{:S(2)}) collective-permute-start(f32[256,128]{1,0:T(8,128)S(1)} %get-tuple-element.29.refs_1_), channel_id=1, source_target_pairs={{0,24},{8,16},{16,8},{24,0},{1,25},{9,17},{17,9},{25,1},{2,26},{10... | collective-permute-start | bytes 393224 | tf_op jit(solution)/shard_map/ppermute | solution.py:16
  35.4 0.0 collective-permute-done.3.refs_1_
  35.4 0.0 copy-done
  35.4 0.1 shard_map.41
  35.5 0.3 shard_map.42.refs_0_
  35.8 0.4 collective-permute-start.10
  36.1 1.7 %collective-permute-start.11 = (f32[128,128]{1,0:T(8,128)S(1)}, f32[128,128]{1,0:T(8,128)S(1)}, u32[]{:S(2)}, u32[]{:S(2)}) collective-permute-start(f32[128,128]{1,0:T(8,128)S(1)} %shard_map.42.refs_0_), channel_id=1, source_target_pairs={{0,24},{8,16},{16,8},{24,0},{1,25},{9,17},{17,9},{25,1},{2,26},{10... | collective-permute-start | bytes 196616 | tf_op jit(solution)/shard_map/ppermute | solution.py:16
  37.8 0.0 collective-permute-done.9.refs_1_
  37.9 0.4 shard_map.44
  38.2 0.1 collective-permute-start.14
  38.3 4.7 %collective-permute-done.10.refs_8_ = f32[128,128]{1,0:T(8,128)S(1)} collective-permute-done((f32[128,128]{1,0:T(8,128)S(1)}, f32[128,128]{1,0:T(8,128)S(1)}, u32[]{:S(2)}, u32[]{:S(2)}) %collective-permute-start.10) | collective-permute-done | bytes 65568 | tf_op jit(solution)/shard_map/ppermute | solution.py:16
  43.0 1.7 %collective-permute-start.15 = (f32[128,128]{1,0:T(8,128)S(1)}, f32[128,128]{1,0:T(8,128)S(1)}, u32[]{:S(2)}, u32[]{:S(2)}) collective-permute-start(f32[128,128]{1,0:T(8,128)S(1)} %get-tuple-element.34.solved_ref), channel_id=1, source_target_pairs={{0,24},{8,16},{16,8},{24,0},{1,25},{9,17},{17,9},{25,1},{2,26},{10... | collective-permute-start | bytes 196616 | tf_op jit(solution)/shard_map/ppermute | solution.py:16
  44.7 0.0 collective-permute-done.11.refs_9_
  44.7 0.0 collective-permute-done.12.refs_10_
  44.7 0.0 collective-permute-done.13.refs_11_
  44.8 0.0 collective-permute-done.14.refs_6_
  44.8 3.4 %collective-permute-done.15.refs_7_ = f32[128,128]{1,0:T(8,128)S(1)} collective-permute-done((f32[128,128]{1,0:T(8,128)S(1)}, f32[128,128]{1,0:T(8,128)S(1)}, u32[]{:S(2)}, u32[]{:S(2)}) %collective-permute-start.15) | collective-permute-done | bytes 65568 | tf_op jit(solution)/shard_map/ppermute | solution.py:16
  48.2 0.7 %shard_map.46 = f32[512,128]{1,0:T(8,128)} custom-call(f32[512,128]{1,0:T(8,128)S(1)} %shard_map.45.so_far_ref, f32[128,128]{1,0:T(8,128)S(1)} %get-tuple-element.34.solved_ref, bf16[128,1024]{1,0:T(8,128)(2,1)S(1)} %get-tuple-element.27.refs_0_.refs_2_, bf16[128,1024]{1,0:T(8,128)(2,1)S(1)} %get-tuple-element.28.refs_1_.refs_3_, ...), custom_call_target="tpu_custom_call" | custom-call | tf_op jit(solution)/shard_map/pallas_call | solution.py:20
  (2 shorter events, 0.0 us)
Async XLA Ops:
  0.0 16.3 %collective-permute-start.6 = (f32[64,1024]{1,0:T(8,128)}, f32[64,1024]{1,0:T(8,128)S(1)}, u32[]{:S(2)}, u32[]{:S(2)}) collective-permute-start(f32[64,1024]{1,0:T(8,128)} %refs_0_.1), channel_id=1, source_target_pairs={{0,4},{1,5},{2,6},{3,7},{4,0},{5,1},{6,2},{7,3},{8,12},{9,13},{10,... | collective-permute-start | bytes 786440 | tf_op jit(solution)/shard_map/ppermute | solution.py:16
  4.1 18.2 %collective-permute-start.4 = (f32[64,1024]{1,0:T(8,128)}, f32[64,1024]{1,0:T(8,128)S(1)}, u32[]{:S(2)}, u32[]{:S(2)}) collective-permute-start(f32[64,1024]{1,0:T(8,128)} %refs_0_.1), channel_id=1, source_target_pairs={{0,2},{1,3},{2,0},{3,1},{4,6},{5,7},{6,4},{7,5},{8,10},{9,11},{10,... | collective-permute-start | bytes 786440 | tf_op jit(solution)/shard_map/ppermute | solution.py:16
  16.3 11.7 %collective-permute-start.8 = (f32[64,1024]{1,0:T(8,128)S(1)}, f32[64,1024]{1,0:T(8,128)S(1)}, u32[]{:S(2)}, u32[]{:S(2)}) collective-permute-start(f32[64,1024]{1,0:T(8,128)S(1)} %collective-permute-done.6.refs_2_), channel_id=1, source_target_pairs={{0,2},{1,3},{2,0},{3,1},{4,6},{5,7},{6,4},{7,5},{8,10},{9,11},{10,... | collective-permute-start | bytes 786440 | tf_op jit(solution)/shard_map/ppermute | solution.py:16
  18.7 7.6 %collective-permute-start = (f32[264,128]{1,0:T(8,128)S(1)}, f32[264,128]{1,0:T(8,128)S(1)}, u32[]{:S(2)}, u32[]{:S(2)}) collective-permute-start(f32[264,128]{1,0:T(8,128)S(1)} %get-tuple-element.22), channel_id=1, source_target_pairs={{0,16},{8,24},{16,0},{24,8},{1,17},{9,25},{17,1},{25,9},{2,18},{10... | collective-permute-start | bytes 405512 | tf_op jit(solution)/shard_map/ppermute | solution.py:16
  20.7 7.4 %collective-permute-start.1 = (f32[264,128]{1,0:T(8,128)S(1)}, f32[264,128]{1,0:T(8,128)S(1)}, u32[]{:S(2)}, u32[]{:S(2)}) collective-permute-start(f32[264,128]{1,0:T(8,128)S(1)} %get-tuple-element.23), channel_id=1, source_target_pairs={{0,24},{8,16},{16,8},{24,0},{1,25},{9,17},{17,9},{25,1},{2,26},{10... | collective-permute-start | bytes 405512 | tf_op jit(solution)/shard_map/ppermute | solution.py:16
  21.7 9.3 %collective-permute-start.2 = (f32[512,128]{1,0:T(8,128)}, f32[512,128]{1,0:T(8,128)S(1)}, u32[]{:S(2)}, u32[]{:S(2)}) collective-permute-start(f32[512,128]{1,0:T(8,128)} %matrix_hbm.1), channel_id=1, source_target_pairs={{0,8},{8,0},{16,24},{24,16},{1,9},{9,1},{17,25},{25,17},{2,10},{10... | collective-permute-start | bytes 786440 | tf_op jit(solution)/shard_map/ppermute | solution.py:16
  22.3 9.5 %collective-permute-start.5 = (f32[64,1024]{1,0:T(8,128)S(1)}, f32[64,1024]{1,0:T(8,128)S(1)}, u32[]{:S(2)}, u32[]{:S(2)}) collective-permute-start(f32[64,1024]{1,0:T(8,128)S(1)} %collective-permute-done.4.refs_0_), channel_id=1, source_target_pairs={{0,1},{1,0},{2,3},{3,2},{4,5},{5,4},{6,7},{7,6},{8,9},{9,8},{10,11... | collective-permute-start | bytes 786440 | tf_op jit(solution)/shard_map/ppermute | solution.py:16
  26.3 5.4 %collective-permute-start.7 = (f32[64,1024]{1,0:T(8,128)S(1)}, f32[64,1024]{1,0:T(8,128)S(1)}, u32[]{:S(2)}, u32[]{:S(2)}) collective-permute-start(f32[64,1024]{1,0:T(8,128)S(1)} %collective-permute-done.6.refs_2_), channel_id=1, source_target_pairs={{0,1},{1,0},{2,3},{3,2},{4,5},{5,4},{6,7},{7,6},{8,9},{9,8},{10,11... | collective-permute-start | bytes 786440 | tf_op jit(solution)/shard_map/ppermute | solution.py:16
  28.0 7.3 %collective-permute-start.3 = (f32[64,1024]{1,0:T(8,128)}, f32[64,1024]{1,0:T(8,128)S(1)}, u32[]{:S(2)}, u32[]{:S(2)}) collective-permute-start(f32[64,1024]{1,0:T(8,128)} %refs_0_.1), channel_id=1, source_target_pairs={{0,1},{1,0},{2,3},{3,2},{4,5},{5,4},{6,7},{7,6},{8,9},{9,8},{10,11... | collective-permute-start | bytes 786440 | tf_op jit(solution)/shard_map/ppermute | solution.py:16
  28.0 9.8 %collective-permute-start.9 = (f32[64,1024]{1,0:T(8,128)S(1)}, f32[64,1024]{1,0:T(8,128)S(1)}, u32[]{:S(2)}, u32[]{:S(2)}) collective-permute-start(f32[64,1024]{1,0:T(8,128)S(1)} %collective-permute-done.8.refs_0_), channel_id=1, source_target_pairs={{0,1},{1,0},{2,3},{3,2},{4,5},{5,4},{6,7},{7,6},{8,9},{9,8},{10,11... | collective-permute-start | bytes 786440 | tf_op jit(solution)/shard_map/ppermute | solution.py:16
  31.7 3.7 %copy-start = (f32[64,1024]{1,0:T(8,128)S(1)}, f32[64,1024]{1,0:T(8,128)}, u32[]{:S(2)}) copy-start(f32[64,1024]{1,0:T(8,128)} %refs_0_.1) | copy-start | bytes 786436
  32.4 12.4 %collective-permute-start.12 = (f32[256,128]{1,0:T(8,128)S(1)}, f32[256,128]{1,0:T(8,128)S(1)}, u32[]{:S(2)}, u32[]{:S(2)}) collective-permute-start(f32[256,128]{1,0:T(8,128)S(1)} %get-tuple-element.29.refs_1_), channel_id=1, source_target_pairs={{0,16},{8,24},{16,0},{24,8},{1,17},{9,25},{17,1},{25,9},{2,18},{10... | collective-permute-start | bytes 393224 | tf_op jit(solution)/shard_map/ppermute | solution.py:16
  33.0 11.7 %collective-permute-start.13 = (f32[256,128]{1,0:T(8,128)S(1)}, f32[256,128]{1,0:T(8,128)S(1)}, u32[]{:S(2)}, u32[]{:S(2)}) collective-permute-start(f32[256,128]{1,0:T(8,128)S(1)} %get-tuple-element.29.refs_1_), channel_id=1, source_target_pairs={{0,24},{8,16},{16,8},{24,0},{1,25},{9,17},{17,9},{25,1},{2,26},{10... | collective-permute-start | bytes 393224 | tf_op jit(solution)/shard_map/ppermute | solution.py:16
  35.8 7.2 %collective-permute-start.10 = (f32[128,128]{1,0:T(8,128)S(1)}, f32[128,128]{1,0:T(8,128)S(1)}, u32[]{:S(2)}, u32[]{:S(2)}) collective-permute-start(f32[128,128]{1,0:T(8,128)S(1)} %shard_map.42.refs_0_), channel_id=1, source_target_pairs={{0,16},{8,24},{16,0},{24,8},{1,17},{9,25},{17,1},{25,9},{2,18},{10... | collective-permute-start | bytes 196616 | tf_op jit(solution)/shard_map/ppermute | solution.py:16
  36.1 8.6 %collective-permute-start.11 = (f32[128,128]{1,0:T(8,128)S(1)}, f32[128,128]{1,0:T(8,128)S(1)}, u32[]{:S(2)}, u32[]{:S(2)}) collective-permute-start(f32[128,128]{1,0:T(8,128)S(1)} %shard_map.42.refs_0_), channel_id=1, source_target_pairs={{0,24},{8,16},{16,8},{24,0},{1,25},{9,17},{17,9},{25,1},{2,26},{10... | collective-permute-start | bytes 196616 | tf_op jit(solution)/shard_map/ppermute | solution.py:16
  38.2 6.5 %collective-permute-start.14 = (f32[128,128]{1,0:T(8,128)S(1)}, f32[128,128]{1,0:T(8,128)S(1)}, u32[]{:S(2)}, u32[]{:S(2)}) collective-permute-start(f32[128,128]{1,0:T(8,128)S(1)} %get-tuple-element.34.solved_ref), channel_id=1, source_target_pairs={{0,16},{8,24},{16,0},{24,8},{1,17},{9,25},{17,1},{25,9},{2,18},{10... | collective-permute-start | bytes 196616 | tf_op jit(solution)/shard_map/ppermute | solution.py:16
  43.0 5.2 %collective-permute-start.15 = (f32[128,128]{1,0:T(8,128)S(1)}, f32[128,128]{1,0:T(8,128)S(1)}, u32[]{:S(2)}, u32[]{:S(2)}) collective-permute-start(f32[128,128]{1,0:T(8,128)S(1)} %get-tuple-element.34.solved_ref), channel_id=1, source_target_pairs={{0,24},{8,16},{16,8},{24,0},{1,25},{9,17},{17,9},{25,1},{2,26},{10... | collective-permute-start | bytes 196616 | tf_op jit(solution)/shard_map/ppermute | solution.py:16

commit v9 on v8

--- a/solution.py
+++ b/solution.py
@@ -361,7 +361,13 @@
         functools.partial(solve, 0, sources), [result(relayed_at)] + terms(relayed_at), [], top, *relayed
     )
     solved = [first, second, third]
-    got = [swap(piece, "prow", mask) for piece in solved for mask in masks]
+    got = []
+    for i, piece in enumerate(solved):
+        for mask in masks:
+            if i == 0 and mask % 2 and mask - 1 in masks:
+                got.append(swap(got[-1], "prow", 1))
+            else:
+                got.append(swap(piece, "prow", mask))
 
     scratch = [pltpu.VMEM((block, cols), f32)]
     if 2 * depth % lanes:

time: 49.1 us -> 47.5 us (0.967)
  waiting for transfers between devices: 25.9 us -> 20.5 us
  starting transfers between devices: 17.3 us -> 20.3 us
  local copies, waits for them, and re-layouts: 0.01 us -> 0.95 us
    ppermute x16, waiting for transfers between devices: 25.9 us -> 20.5 us  [swap(): lax.ppermute(block, axis, [(i, i ^ mask) for i in range(lax.axis_size(axi...]
    ppermute x16, starting transfers between devices: 17.3 us -> 20.3 us  [swap(): lax.ppermute(block, axis, [(i, i ^ mask) for i in range(lax.axis_size(axi...]
    unnamed x2, local copies, waits for them, and re-layouts: 0.01 us -> 0.95 us
  transfers between devices with their start and end apart: 16 -> 16, of which waited for: 6 -> 7; matrix products, arithmetic and copies ran while one was open for 0% -> 0% of each run, Pallas kernels for 10% -> 10%
where the time goes in v9:
time: 47.5 us; the launch traced here: 47.3 us
  waiting for transfers between devices  20.5 us (43%)
  starting transfers between devices  20.3 us (43%)
  Pallas kernels  5.5 us (12%)
  local copies, waits for them, and re-layouts  0.95 us (2%)
    ppermute x16, waiting for transfers between devices, swap(): lax.ppermute(block, axis, [(i, i ^ mask) for i in range(lax.axis_size(axi...  20.5 us
    ppermute x16, starting transfers between devices, swap(): lax.ppermute(block, axis, [(i, i ^ mask) for i in range(lax.axis_size(axi...  20.3 us
    pallas_call x10, Pallas kernels, call(): pl.pallas_call(kernel, out_shape=out_shape, in_specs=[VMEM if inside else...  5.5 us
  transfers between devices with their start and end apart: 16, of which 7 were waited for; matrix products, arithmetic and copies ran while one was open for 0% of the time, Pallas kernels for 10%

profile of v9, /device:TPU:0, one launch (start us, length us, event | category | flops | bytes accessed | tf_op | source)
XLA Modules:
  0.0 47.3 jit_solution(922898140072906041)
XLA Ops:
  0.0 4.1 %collective-permute-start.6 = (f32[64,1024]{1,0:T(8,128)}, f32[64,1024]{1,0:T(8,128)S(1)}, u32[]{:S(2)}, u32[]{:S(2)}) collective-permute-start(f32[64,1024]{1,0:T(8,128)} %refs_0_.1), channel_id=1, source_target_pairs={{0,4},{1,5},{2,6},{3,7},{4,0},{5,1},{6,2},{7,3},{8,12},{9,13},{10,... | collective-permute-start | bytes 786440 | tf_op jit(solution)/shard_map/ppermute | solution.py:16
  4.1 1.6 %collective-permute-start.4 = (f32[64,1024]{1,0:T(8,128)}, f32[64,1024]{1,0:T(8,128)S(1)}, u32[]{:S(2)}, u32[]{:S(2)}) collective-permute-start(f32[64,1024]{1,0:T(8,128)} %refs_0_.1), channel_id=1, source_target_pairs={{0,2},{1,3},{2,0},{3,1},{4,6},{5,7},{6,4},{7,5},{8,10},{9,11},{10,... | collective-permute-start | bytes 786440 | tf_op jit(solution)/shard_map/ppermute | solution.py:16
  5.6 10.7 %collective-permute-done.6.refs_2_ = f32[64,1024]{1,0:T(8,128)S(1)} collective-permute-done((f32[64,1024]{1,0:T(8,128)}, f32[64,1024]{1,0:T(8,128)S(1)}, u32[]{:S(2)}, u32[]{:S(2)}) %collective-permute-start.6) | collective-permute-done | bytes 262176 | tf_op jit(solution)/shard_map/ppermute | solution.py:16
  16.3 0.7 %collective-permute-start.8 = (f32[64,1024]{1,0:T(8,128)S(1)}, f32[64,1024]{1,0:T(8,128)S(1)}, u32[]{:S(2)}, u32[]{:S(2)}) collective-permute-start(f32[64,1024]{1,0:T(8,128)S(1)} %collective-permute-done.6.refs_2_), channel_id=1, source_target_pairs={{0,2},{1,3},{2,0},{3,1},{4,6},{5,7},{6,4},{7,5},{8,10},{9,11},{10,... | collective-permute-start | bytes 786440 | tf_op jit(solution)/shard_map/ppermute | solution.py:16
  17.0 0.0 collective-permute-start.3
  17.0 1.7 %shard_map.37 = (f32[264,128]{1,0:T(8,128)S(1)}, f32[264,128]{1,0:T(8,128)S(1)}, s32[512,128]{1,0:T(8,128)S(1)}, s32[1,1024]{1,0:T(1,128)S(1)}, f32[512,128]{1,0:T(8,128)S(1)}) custom-call(s32[1,1024]{1,0:T(1,128)} %bitcast.1, f32[512,128]{1,0:T(8,128)} %matrix_hbm.1), custom_call_target="tpu_custom_call" | custom-call | tf_op jit(solution)/shard_map/pallas_call | solution.py:20
  18.7 2.0 %collective-permute-start = (f32[264,128]{1,0:T(8,128)S(1)}, f32[264,128]{1,0:T(8,128)S(1)}, u32[]{:S(2)}, u32[]{:S(2)}) collective-permute-start(f32[264,128]{1,0:T(8,128)S(1)} %get-tuple-element.22), channel_id=1, source_target_pairs={{0,16},{8,24},{16,0},{24,8},{1,17},{9,25},{17,1},{25,9},{2,18},{10... | collective-permute-start | bytes 405512 | tf_op jit(solution)/shard_map/ppermute | solution.py:16
  20.7 1.5 %collective-permute-start.2 = (f32[512,128]{1,0:T(8,128)}, f32[512,128]{1,0:T(8,128)S(1)}, u32[]{:S(2)}, u32[]{:S(2)}) collective-permute-start(f32[512,128]{1,0:T(8,128)} %matrix_hbm.1), channel_id=1, source_target_pairs={{0,8},{8,0},{16,24},{24,16},{1,9},{9,1},{17,25},{25,17},{2,10},{10... | collective-permute-start | bytes 786440 | tf_op jit(solution)/shard_map/ppermute | solution.py:16
  22.2 0.0 collective-permute-done.4.refs_0_
  22.2 0.0 collective-permute-start.5
  22.2 2.8 %collective-permute-done.refs_0_.refs_2_ = f32[264,128]{1,0:T(8,128)S(1)} collective-permute-done((f32[264,128]{1,0:T(8,128)S(1)}, f32[264,128]{1,0:T(8,128)S(1)}, u32[]{:S(2)}, u32[]{:S(2)}) %collective-permute-start) | collective-permute-done | bytes 135200 | tf_op jit(solution)/shard_map/ppermute | solution.py:16
  24.9 0.0 collective-permute-start.7
  24.9 0.0 collective-permute-done.8.refs_0_
  24.9 0.5 %collective-permute-start.9 = (f32[64,1024]{1,0:T(8,128)S(1)}, f32[64,1024]{1,0:T(8,128)S(1)}, u32[]{:S(2)}, u32[]{:S(2)}) collective-permute-start(f32[64,1024]{1,0:T(8,128)S(1)} %collective-permute-done.8.refs_0_), channel_id=1, source_target_pairs={{0,1},{1,0},{2,3},{3,2},{4,5},{5,4},{6,7},{7,6},{8,9},{9,8},{10,11... | collective-permute-start | bytes 786440 | tf_op jit(solution)/shard_map/ppermute | solution.py:16
  25.5 0.0 collective-permute-done.3.refs_1_
  25.5 2.7 %collective-permute-start.1 = (f32[264,128]{1,0:T(8,128)S(1)}, f32[264,128]{1,0:T(8,128)S(1)}, u32[]{:S(2)}, u32[]{:S(2)}) collective-permute-start(f32[264,128]{1,0:T(8,128)S(1)} %get-tuple-element.23), channel_id=1, source_target_pairs={{0,24},{8,16},{16,8},{24,0},{1,25},{9,17},{17,9},{25,1},{2,26},{10... | collective-permute-start | bytes 405512 | tf_op jit(solution)/shard_map/ppermute | solution.py:16
  28.1 1.1 %shard_map.39 = (bf16[1024,768]{1,0:T(8,128)(2,1)S(1)}, f32[1024,128]{1,0:T(8,128)S(1)}) custom-call(s32[1,1024]{1,0:T(1,128)S(1)} %get-tuple-element.24.piv_row), custom_call_target="tpu_custom_call" | custom-call | tf_op jit(solution)/shard_map/pallas_call | solution.py:20
  29.2 0.0 copy-start
  29.2 0.9 %copy-done = f32[64,1024]{1,0:T(8,128)S(1)} copy-done((f32[64,1024]{1,0:T(8,128)S(1)}, f32[64,1024]{1,0:T(8,128)}, u32[]{:S(2)}) %copy-start) | copy-done | bytes 262168
  30.2 0.1 shard_map.41
  30.2 1.8 %collective-permute-done.1.refs_1_.refs_3_ = f32[264,128]{1,0:T(8,128)S(1)} collective-permute-done((f32[264,128]{1,0:T(8,128)S(1)}, f32[264,128]{1,0:T(8,128)S(1)}, u32[]{:S(2)}, u32[]{:S(2)}) %collective-permute-start.1) | collective-permute-done | bytes 135200 | tf_op jit(solution)/shard_map/ppermute | solution.py:16
  32.0 0.0 collective-permute-done.2.refs_1_
  32.0 0.6 %shard_map.40.top_ref = bf16[1024,256]{1,0:T(8,128)(2,1)S(1)} custom-call(bf16[1024,768]{1,0:T(8,128)(2,1)S(1)} %get-tuple-element.25.chosen_ref, f32[1024,128]{1,0:T(8,128)S(1)} %get-tuple-element.26.keep_ref, f32[512,128]{1,0:T(8,128)S(1)} %get-tuple-element.21.matrix_ref.refs_0_, f32[512,128]{1,0:T(8,128)S(1)} %collective-permute-done.2.refs_1_, ...), custom_call_target="tpu_custom_call" | custom-call | tf_op jit(solution)/shard_map/pallas_call | solution.py:20
  32.7 0.3 shard_map.42.refs_0_
  33.0 0.7 %collective-permute-start.10 = (f32[128,128]{1,0:T(8,128)S(1)}, f32[128,128]{1,0:T(8,128)S(1)}, u32[]{:S(2)}, u32[]{:S(2)}) collective-permute-start(f32[128,128]{1,0:T(8,128)S(1)} %shard_map.42.refs_0_), channel_id=1, source_target_pairs={{0,16},{8,24},{16,0},{24,8},{1,17},{9,25},{17,1},{25,9},{2,18},{10... | collective-permute-start | bytes 196616 | tf_op jit(solution)/shard_map/ppermute | solution.py:16
  33.7 0.0 collective-permute-done.5.refs_1_
  33.7 0.0 collective-permute-done.7.refs_3_
  33.7 0.6 %shard_map.43 = (f32[256,128]{1,0:T(8,128)S(1)}, bf16[256,1024]{1,0:T(8,128)(2,1)S(1)}, bf16[256,1024]{1,0:T(8,128)(2,1)S(1)}) custom-call(bf16[1024,256]{1,0:T(8,128)(2,1)S(1)} %shard_map.40.top_ref, f32[64,1024]{1,0:T(8,128)S(1)} %collective-permute-done.4.refs_0_, f32[64,1024]{1,0:T(8,128)S(1)} %collective-permute-done.5.refs_1_, ...), custom_call_target="tpu_custom_call" | custom-call | tf_op jit(solution)/shard_map/pallas_call | solution.py:20
  34.3 1.0 %collective-permute-start.12 = (f32[256,128]{1,0:T(8,128)S(1)}, f32[256,128]{1,0:T(8,128)S(1)}, u32[]{:S(2)}, u32[]{:S(2)}) collective-permute-start(f32[256,128]{1,0:T(8,128)S(1)} %get-tuple-element.29.refs_1_), channel_id=1, source_target_pairs={{0,16},{8,24},{16,0},{24,8},{1,17},{9,25},{17,1},{25,9},{2,18},{10... | collective-permute-start | bytes 393224 | tf_op jit(solution)/shard_map/ppermute | solution.py:16
  35.3 2.0 %collective-permute-start.13 = (f32[256,128]{1,0:T(8,128)S(1)}, f32[256,128]{1,0:T(8,128)S(1)}, u32[]{:S(2)}, u32[]{:S(2)}) collective-permute-start(f32[256,128]{1,0:T(8,128)S(1)} %get-tuple-element.29.refs_1_), channel_id=1, source_target_pairs={{0,24},{8,16},{16,8},{24,0},{1,25},{9,17},{17,9},{25,1},{2,26},{10... | collective-permute-start | bytes 393224 | tf_op jit(solution)/shard_map/ppermute | solution.py:16
  37.3 2.1 %collective-permute-done.10.refs_8_ = f32[128,128]{1,0:T(8,128)S(1)} collective-permute-done((f32[128,128]{1,0:T(8,128)S(1)}, f32[128,128]{1,0:T(8,128)S(1)}, u32[]{:S(2)}, u32[]{:S(2)}) %collective-permute-start.10) | collective-permute-done | bytes 65568 | tf_op jit(solution)/shard_map/ppermute | solution.py:16
  39.4 1.5 %collective-permute-start.11 = (f32[128,128]{1,0:T(8,128)S(1)}, f32[128,128]{1,0:T(8,128)S(1)}, u32[]{:S(2)}, u32[]{:S(2)}) collective-permute-start(f32[128,128]{1,0:T(8,128)S(1)} %collective-permute-done.10.refs_8_), channel_id=1, source_target_pairs={{0,8},{8,0},{16,24},{24,16},{1,9},{9,1},{17,25},{25,17},{2,10},{10... | collective-permute-start | bytes 196616 | tf_op jit(solution)/shard_map/ppermute | solution.py:16
  40.9 0.0 collective-permute-done.9.refs_1_
  40.9 0.4 shard_map.44
  41.3 0.1 collective-permute-start.14
  41.4 2.0 %collective-permute-start.15 = (f32[128,128]{1,0:T(8,128)S(1)}, f32[128,128]{1,0:T(8,128)S(1)}, u32[]{:S(2)}, u32[]{:S(2)}) collective-permute-start(f32[128,128]{1,0:T(8,128)S(1)} %get-tuple-element.34.solved_ref), channel_id=1, source_target_pairs={{0,24},{8,16},{16,8},{24,0},{1,25},{9,17},{17,9},{25,1},{2,26},{10... | collective-permute-start | bytes 196616 | tf_op jit(solution)/shard_map/ppermute | solution.py:16
  43.4 0.3 collective-permute-done.11.refs_9_
  43.7 0.0 collective-permute-done.12.refs_10_
  43.7 0.0 collective-permute-done.13.refs_11_
  43.7 1.9 %collective-permute-done.14.refs_6_ = f32[128,128]{1,0:T(8,128)S(1)} collective-permute-done((f32[128,128]{1,0:T(8,128)S(1)}, f32[128,128]{1,0:T(8,128)S(1)}, u32[]{:S(2)}, u32[]{:S(2)}) %collective-permute-start.14) | collective-permute-done | bytes 65568 | tf_op jit(solution)/shard_map/ppermute | solution.py:16
  45.6 1.0 %collective-permute-done.15.refs_7_ = f32[128,128]{1,0:T(8,128)S(1)} collective-permute-done((f32[128,128]{1,0:T(8,128)S(1)}, f32[128,128]{1,0:T(8,128)S(1)}, u32[]{:S(2)}, u32[]{:S(2)}) %collective-permute-start.15) | collective-permute-done | bytes 65568 | tf_op jit(solution)/shard_map/ppermute | solution.py:16
  46.6 0.7 %shard_map.46 = f32[512,128]{1,0:T(8,128)} custom-call(f32[512,128]{1,0:T(8,128)S(1)} %shard_map.45.so_far_ref, f32[128,128]{1,0:T(8,128)S(1)} %get-tuple-element.34.solved_ref, bf16[128,1024]{1,0:T(8,128)(2,1)S(1)} %get-tuple-element.27.refs_0_.refs_2_, bf16[128,1024]{1,0:T(8,128)(2,1)S(1)} %get-tuple-element.28.refs_1_.refs_3_, ...), custom_call_target="tpu_custom_call" | custom-call | tf_op jit(solution)/shard_map/pallas_call | solution.py:20
  (2 shorter events, 0.0 us)
Async XLA Ops:
  0.0 16.3 %collective-permute-start.6 = (f32[64,1024]{1,0:T(8,128)}, f32[64,1024]{1,0:T(8,128)S(1)}, u32[]{:S(2)}, u32[]{:S(2)}) collective-permute-start(f32[64,1024]{1,0:T(8,128)} %refs_0_.1), channel_id=1, source_target_pairs={{0,4},{1,5},{2,6},{3,7},{4,0},{5,1},{6,2},{7,3},{8,12},{9,13},{10,... | collective-permute-start | bytes 786440 | tf_op jit(solution)/shard_map/ppermute | solution.py:16
  4.1 18.1 %collective-permute-start.4 = (f32[64,1024]{1,0:T(8,128)}, f32[64,1024]{1,0:T(8,128)S(1)}, u32[]{:S(2)}, u32[]{:S(2)}) collective-permute-start(f32[64,1024]{1,0:T(8,128)} %refs_0_.1), channel_id=1, source_target_pairs={{0,2},{1,3},{2,0},{3,1},{4,6},{5,7},{6,4},{7,5},{8,10},{9,11},{10,... | collective-permute-start | bytes 786440 | tf_op jit(solution)/shard_map/ppermute | solution.py:16
  16.3 8.6 %collective-permute-start.8 = (f32[64,1024]{1,0:T(8,128)S(1)}, f32[64,1024]{1,0:T(8,128)S(1)}, u32[]{:S(2)}, u32[]{:S(2)}) collective-permute-start(f32[64,1024]{1,0:T(8,128)S(1)} %collective-permute-done.6.refs_2_), channel_id=1, source_target_pairs={{0,2},{1,3},{2,0},{3,1},{4,6},{5,7},{6,4},{7,5},{8,10},{9,11},{10,... | collective-permute-start | bytes 786440 | tf_op jit(solution)/shard_map/ppermute | solution.py:16
  17.0 8.4 %collective-permute-start.3 = (f32[64,1024]{1,0:T(8,128)}, f32[64,1024]{1,0:T(8,128)S(1)}, u32[]{:S(2)}, u32[]{:S(2)}) collective-permute-start(f32[64,1024]{1,0:T(8,128)} %refs_0_.1), channel_id=1, source_target_pairs={{0,1},{1,0},{2,3},{3,2},{4,5},{5,4},{6,7},{7,6},{8,9},{9,8},{10,11... | collective-permute-start | bytes 786440 | tf_op jit(solution)/shard_map/ppermute | solution.py:16
  18.7 6.2 %collective-permute-start = (f32[264,128]{1,0:T(8,128)S(1)}, f32[264,128]{1,0:T(8,128)S(1)}, u32[]{:S(2)}, u32[]{:S(2)}) collective-permute-start(f32[264,128]{1,0:T(8,128)S(1)} %get-tuple-element.22), channel_id=1, source_target_pairs={{0,16},{8,24},{16,0},{24,8},{1,17},{9,25},{17,1},{25,9},{2,18},{10... | collective-permute-start | bytes 405512 | tf_op jit(solution)/shard_map/ppermute | solution.py:16
  20.7 11.3 %collective-permute-start.2 = (f32[512,128]{1,0:T(8,128)}, f32[512,128]{1,0:T(8,128)S(1)}, u32[]{:S(2)}, u32[]{:S(2)}) collective-permute-start(f32[512,128]{1,0:T(8,128)} %matrix_hbm.1), channel_id=1, source_target_pairs={{0,8},{8,0},{16,24},{24,16},{1,9},{9,1},{17,25},{25,17},{2,10},{10... | collective-permute-start | bytes 786440 | tf_op jit(solution)/shard_map/ppermute | solution.py:16
  22.2 11.5 %collective-permute-start.5 = (f32[64,1024]{1,0:T(8,128)S(1)}, f32[64,1024]{1,0:T(8,128)S(1)}, u32[]{:S(2)}, u32[]{:S(2)}) collective-permute-start(f32[64,1024]{1,0:T(8,128)S(1)} %collective-permute-done.4.refs_0_), channel_id=1, source_target_pairs={{0,1},{1,0},{2,3},{3,2},{4,5},{5,4},{6,7},{7,6},{8,9},{9,8},{10,11... | collective-permute-start | bytes 786440 | tf_op jit(solution)/shard_map/ppermute | solution.py:16
  24.9 8.8 %collective-permute-start.7 = (f32[64,1024]{1,0:T(8,128)S(1)}, f32[64,1024]{1,0:T(8,128)S(1)}, u32[]{:S(2)}, u32[]{:S(2)}) collective-permute-start(f32[64,1024]{1,0:T(8,128)S(1)} %collective-permute-done.6.refs_2_), channel_id=1, source_target_pairs={{0,1},{1,0},{2,3},{3,2},{4,5},{5,4},{6,7},{7,6},{8,9},{9,8},{10,11... | collective-permute-start | bytes 786440 | tf_op jit(solution)/shard_map/ppermute | solution.py:16
  24.9 16.0 %collective-permute-start.9 = (f32[64,1024]{1,0:T(8,128)S(1)}, f32[64,1024]{1,0:T(8,128)S(1)}, u32[]{:S(2)}, u32[]{:S(2)}) collective-permute-start(f32[64,1024]{1,0:T(8,128)S(1)} %collective-permute-done.8.refs_0_), channel_id=1, source_target_pairs={{0,1},{1,0},{2,3},{3,2},{4,5},{5,4},{6,7},{7,6},{8,9},{9,8},{10,11... | collective-permute-start | bytes 786440 | tf_op jit(solution)/shard_map/ppermute | solution.py:16
  25.5 6.6 %collective-permute-start.1 = (f32[264,128]{1,0:T(8,128)S(1)}, f32[264,128]{1,0:T(8,128)S(1)}, u32[]{:S(2)}, u32[]{:S(2)}) collective-permute-start(f32[264,128]{1,0:T(8,128)S(1)} %get-tuple-element.23), channel_id=1, source_target_pairs={{0,24},{8,16},{16,8},{24,0},{1,25},{9,17},{17,9},{25,1},{2,26},{10... | collective-permute-start | bytes 405512 | tf_op jit(solution)/shard_map/ppermute | solution.py:16
  29.2 1.0 %copy-start = (f32[64,1024]{1,0:T(8,128)S(1)}, f32[64,1024]{1,0:T(8,128)}, u32[]{:S(2)}) copy-start(f32[64,1024]{1,0:T(8,128)} %refs_0_.1) | copy-start | bytes 786436
  33.0 6.4 %collective-permute-start.10 = (f32[128,128]{1,0:T(8,128)S(1)}, f32[128,128]{1,0:T(8,128)S(1)}, u32[]{:S(2)}, u32[]{:S(2)}) collective-permute-start(f32[128,128]{1,0:T(8,128)S(1)} %shard_map.42.refs_0_), channel_id=1, source_target_pairs={{0,16},{8,24},{16,0},{24,8},{1,17},{9,25},{17,1},{25,9},{2,18},{10... | collective-permute-start | bytes 196616 | tf_op jit(solution)/shard_map/ppermute | solution.py:16
  34.3 9.4 %collective-permute-start.12 = (f32[256,128]{1,0:T(8,128)S(1)}, f32[256,128]{1,0:T(8,128)S(1)}, u32[]{:S(2)}, u32[]{:S(2)}) collective-permute-start(f32[256,128]{1,0:T(8,128)S(1)} %get-tuple-element.29.refs_1_), channel_id=1, source_target_pairs={{0,16},{8,24},{16,0},{24,8},{1,17},{9,25},{17,1},{25,9},{2,18},{10... | collective-permute-start | bytes 393224 | tf_op jit(solution)/shard_map/ppermute | solution.py:16
  35.3 8.4 %collective-permute-start.13 = (f32[256,128]{1,0:T(8,128)S(1)}, f32[256,128]{1,0:T(8,128)S(1)}, u32[]{:S(2)}, u32[]{:S(2)}) collective-permute-start(f32[256,128]{1,0:T(8,128)S(1)} %get-tuple-element.29.refs_1_), channel_id=1, source_target_pairs={{0,24},{8,16},{16,8},{24,0},{1,25},{9,17},{17,9},{25,1},{2,26},{10... | collective-permute-start | bytes 393224 | tf_op jit(solution)/shard_map/ppermute | solution.py:16
  39.4 4.3 %collective-permute-start.11 = (f32[128,128]{1,0:T(8,128)S(1)}, f32[128,128]{1,0:T(8,128)S(1)}, u32[]{:S(2)}, u32[]{:S(2)}) collective-permute-start(f32[128,128]{1,0:T(8,128)S(1)} %collective-permute-done.10.refs_8_), channel_id=1, source_target_pairs={{0,8},{8,0},{16,24},{24,16},{1,9},{9,1},{17,25},{25,17},{2,10},{10... | collective-permute-start | bytes 196616 | tf_op jit(solution)/shard_map/ppermute | solution.py:16
  41.3 4.3 %collective-permute-start.14 = (f32[128,128]{1,0:T(8,128)S(1)}, f32[128,128]{1,0:T(8,128)S(1)}, u32[]{:S(2)}, u32[]{:S(2)}) collective-permute-start(f32[128,128]{1,0:T(8,128)S(1)} %get-tuple-element.34.solved_ref), channel_id=1, source_target_pairs={{0,16},{8,24},{16,0},{24,8},{1,17},{9,25},{17,1},{25,9},{2,18},{10... | collective-permute-start | bytes 196616 | tf_op jit(solution)/shard_map/ppermute | solution.py:16
  41.4 5.2 %collective-permute-start.15 = (f32[128,128]{1,0:T(8,128)S(1)}, f32[128,128]{1,0:T(8,128)S(1)}, u32[]{:S(2)}, u32[]{:S(2)}) collective-permute-start(f32[128,128]{1,0:T(8,128)S(1)} %get-tuple-element.34.solved_ref), channel_id=1, source_target_pairs={{0,24},{8,16},{16,8},{24,0},{1,25},{9,17},{17,9},{25,1},{2,26},{10... | collective-permute-start | bytes 196616 | tf_op jit(solution)/shard_map/ppermute | solution.py:16

commit v10 on v9

--- a/solution.py
+++ b/solution.py
@@ -123,26 +123,31 @@
                 chosen_ref[:, pl.ds(m * span + i, lanes)] = hot(column - i == lane)
 
 
-def prepare(sources, masks, chosen_ref, keep_ref, *refs):
-    *refs, top_ref, whole, table = refs
-    blocks, packs = refs[:sources], refs[sources:]
-    rows, cols = blocks[0].shape
-    cap = packs[0].shape[0]
-    span = table.shape[0] // len(masks)
+def keep(sources, keep_ref, *refs):
+    *blocks, old_ref, whole = refs
+    rows = blocks[0].shape[0]
     me = lax.axis_index("prow")
 
     @pl.when(me < sources)
     def _():
         for mask, ref in enumerate(blocks):
             whole[pl.ds(pl.multiple_of((me ^ mask) * rows, rows), rows), :] = ref[...]
+        old_ref[...] = jnp.concatenate(halves(jnp.where(keep_ref[:, :1] > 0.0, whole[...], 0.0)), axis=1)
+
+
+def prepare(sources, masks, chosen_ref, old_ref, *refs):
+    *packs, top_ref, table = refs
+    cap, cols = packs[0].shape
+    span = table.shape[0] // len(masks)
+
+    @pl.when(lax.axis_index("prow") < sources)
+    def _():
         for m, ref in enumerate(packs):
             table[pl.ds(m * span, cap), :] = ref[...]
             if span > cap:
                 table[pl.ds(m * span + cap, span - cap), :] = jnp.zeros((span - cap, cols), jnp.float32)
-        high, low = halves(jnp.where(keep_ref[:, :1] > 0.0, whole[...], 0.0))
-        old = jnp.concatenate([high.astype(jnp.float32), low.astype(jnp.float32)], axis=1)
         new = dot(chosen_ref[...], jnp.concatenate(halves(table[...]), axis=1))
-        top_ref[...] = (old + new).astype(jnp.bfloat16)
+        top_ref[...] = (old_ref[...].astype(jnp.float32) + new).astype(jnp.bfloat16)
 
 
 def lower(sources, masks, col_ref, matrix_ref, *refs):
@@ -328,17 +333,23 @@
     packs = [swap(piece, "prow", mask) for mask, piece in zip(masks, packs)]
 
     span = -(-cap // lanes) * lanes
-    chosen, keep = call(
+    chosen, kept = call(
         functools.partial(hots, sources, masks),
         [pltpu.VMEM((block, below * span), bf16), pltpu.VMEM((block, lanes), f32)],
         [slot],
         pivot_row,
     )
+    old = call(
+        functools.partial(keep, sources),
+        pltpu.VMEM((block, 2 * cols), bf16),
+        [pltpu.VMEM((block, cols), f32)],
+        kept, *blocks,
+    )
     top = call(
         functools.partial(prepare, sources, masks),
         pltpu.VMEM((block, 2 * cols), bf16),
-        [pltpu.VMEM((block, cols), f32), pltpu.VMEM((below * span, cols), f32)],
-        chosen, keep, *blocks, *packs,
+        [pltpu.VMEM((below * span, cols), f32)],
+        chosen, old, *packs,
     )
     own = call(
         functools.partial(lower, sources, masks),

time: 47.5 us -> 48.8 us (1.027)
  waiting for transfers between devices: 20.5 us -> 23.4 us
  starting transfers between devices: 20.3 us -> 18.5 us
    ppermute x16, waiting for transfers between devices: 20.5 us -> 23.4 us  [swap(): lax.ppermute(block, axis, [(i, i ^ mask) for i in range(lax.axis_size(axi...]
    ppermute x16, starting transfers between devices: 20.3 us -> 18.5 us  [swap(): lax.ppermute(block, axis, [(i, i ^ mask) for i in range(lax.axis_size(axi...]
    pallas_call x10 -> x11, Pallas kernels: 5.5 us -> 5.68 us  [call(): pl.pallas_call(kernel, out_shape=out_shape, in_specs=[VMEM if inside else...]
  transfers between devices with their start and end apart: 16 -> 16, of which waited for: 7 -> 8; matrix products, arithmetic and copies ran while one was open for 0% -> 0% of each run, Pallas kernels for 10% -> 10%
where the time goes in v10:
time: 48.8 us; the launch traced here: 48.7 us
  waiting for transfers between devices  23.4 us (48%)
  starting transfers between devices  18.5 us (38%)
  Pallas kernels  5.68 us (12%)
  local copies, waits for them, and re-layouts  0.95 us (2%)
    ppermute x16, waiting for transfers between devices, swap(): lax.ppermute(block, axis, [(i, i ^ mask) for i in range(lax.axis_size(axi...  23.4 us
    ppermute x16, starting transfers between devices, swap(): lax.ppermute(block, axis, [(i, i ^ mask) for i in range(lax.axis_size(axi...  18.5 us
    pallas_call x11, Pallas kernels, call(): pl.pallas_call(kernel, out_shape=out_shape, in_specs=[VMEM if inside else...  5.68 us
  transfers between devices with their start and end apart: 16, of which 8 were waited for; matrix products, arithmetic and copies ran while one was open for 0% of the time, Pallas kernels for 10%

profile of v10, /device:TPU:0, one launch (start us, length us, event | category | flops | bytes accessed | tf_op | source)
XLA Modules:
  0.0 48.7 jit_solution(11683828641222706048)
XLA Ops:
  0.0 4.1 %collective-permute-start.6 = (f32[64,1024]{1,0:T(8,128)}, f32[64,1024]{1,0:T(8,128)S(1)}, u32[]{:S(2)}, u32[]{:S(2)}) collective-permute-start(f32[64,1024]{1,0:T(8,128)} %refs_0_.1), channel_id=1, source_target_pairs={{0,4},{1,5},{2,6},{3,7},{4,0},{5,1},{6,2},{7,3},{8,12},{9,13},{10,... | collective-permute-start | bytes 786440 | tf_op jit(solution)/shard_map/ppermute | solution.py:16
  4.1 1.6 %collective-permute-start.4 = (f32[64,1024]{1,0:T(8,128)}, f32[64,1024]{1,0:T(8,128)S(1)}, u32[]{:S(2)}, u32[]{:S(2)}) collective-permute-start(f32[64,1024]{1,0:T(8,128)} %refs_0_.1), channel_id=1, source_target_pairs={{0,2},{1,3},{2,0},{3,1},{4,6},{5,7},{6,4},{7,5},{8,10},{9,11},{10,... | collective-permute-start | bytes 786440 | tf_op jit(solution)/shard_map/ppermute | solution.py:16
  5.6 10.7 %collective-permute-done.6.refs_2_ = f32[64,1024]{1,0:T(8,128)S(1)} collective-permute-done((f32[64,1024]{1,0:T(8,128)}, f32[64,1024]{1,0:T(8,128)S(1)}, u32[]{:S(2)}, u32[]{:S(2)}) %collective-permute-start.6) | collective-permute-done | bytes 262176 | tf_op jit(solution)/shard_map/ppermute | solution.py:16
  16.3 0.7 %collective-permute-start.8 = (f32[64,1024]{1,0:T(8,128)S(1)}, f32[64,1024]{1,0:T(8,128)S(1)}, u32[]{:S(2)}, u32[]{:S(2)}) collective-permute-start(f32[64,1024]{1,0:T(8,128)S(1)} %collective-permute-done.6.refs_2_), channel_id=1, source_target_pairs={{0,2},{1,3},{2,0},{3,1},{4,6},{5,7},{6,4},{7,5},{8,10},{9,11},{10,... | collective-permute-start | bytes 786440 | tf_op jit(solution)/shard_map/ppermute | solution.py:16
  17.0 1.5 %collective-permute-start.2 = (f32[512,128]{1,0:T(8,128)}, f32[512,128]{1,0:T(8,128)S(1)}, u32[]{:S(2)}, u32[]{:S(2)}) collective-permute-start(f32[512,128]{1,0:T(8,128)} %matrix_hbm.1), channel_id=1, source_target_pairs={{0,8},{8,0},{16,24},{24,16},{1,9},{9,1},{17,25},{25,17},{2,10},{10... | collective-permute-start | bytes 786440 | tf_op jit(solution)/shard_map/ppermute | solution.py:16
  18.5 0.0 collective-permute-start.3
  18.5 0.0 collective-permute-done.4.refs_0_
  18.5 0.5 %collective-permute-start.5 = (f32[64,1024]{1,0:T(8,128)S(1)}, f32[64,1024]{1,0:T(8,128)S(1)}, u32[]{:S(2)}, u32[]{:S(2)}) collective-permute-start(f32[64,1024]{1,0:T(8,128)S(1)} %collective-permute-done.4.refs_0_), channel_id=1, source_target_pairs={{0,1},{1,0},{2,3},{3,2},{4,5},{5,4},{6,7},{7,6},{8,9},{9,8},{10,11... | collective-permute-start | bytes 786440 | tf_op jit(solution)/shard_map/ppermute | solution.py:16
  19.0 0.0 collective-permute-start.7
  19.0 4.7 %collective-permute-done.8.refs_0_ = f32[64,1024]{1,0:T(8,128)S(1)} collective-permute-done((f32[64,1024]{1,0:T(8,128)S(1)}, f32[64,1024]{1,0:T(8,128)S(1)}, u32[]{:S(2)}, u32[]{:S(2)}) %collective-permute-start.8) | collective-permute-done | bytes 262176 | tf_op jit(solution)/shard_map/ppermute | solution.py:16
  23.7 0.0 collective-permute-start.9
  23.7 1.7 %shard_map.37 = (f32[264,128]{1,0:T(8,128)S(1)}, f32[264,128]{1,0:T(8,128)S(1)}, s32[512,128]{1,0:T(8,128)S(1)}, s32[1,1024]{1,0:T(1,128)S(1)}, f32[512,128]{1,0:T(8,128)S(1)}) custom-call(s32[1,1024]{1,0:T(1,128)} %bitcast.1, f32[512,128]{1,0:T(8,128)} %matrix_hbm.1), custom_call_target="tpu_custom_call" | custom-call | tf_op jit(solution)/shard_map/pallas_call | solution.py:20
  25.4 0.0 collective-permute-done.2.refs_1_
  25.4 1.7 %collective-permute-start = (f32[264,128]{1,0:T(8,128)S(1)}, f32[264,128]{1,0:T(8,128)S(1)}, u32[]{:S(2)}, u32[]{:S(2)}) collective-permute-start(f32[264,128]{1,0:T(8,128)S(1)} %get-tuple-element.22), channel_id=1, source_target_pairs={{0,16},{8,24},{16,0},{24,8},{1,17},{9,25},{17,1},{25,9},{2,18},{10... | collective-permute-start | bytes 405512 | tf_op jit(solution)/shard_map/ppermute | solution.py:16
  27.2 0.0 collective-permute-done.3.refs_1_
  27.2 1.1 %collective-permute-start.1 = (f32[264,128]{1,0:T(8,128)S(1)}, f32[264,128]{1,0:T(8,128)S(1)}, u32[]{:S(2)}, u32[]{:S(2)}) collective-permute-start(f32[264,128]{1,0:T(8,128)S(1)} %get-tuple-element.23), channel_id=1, source_target_pairs={{0,24},{8,16},{16,8},{24,0},{1,25},{9,17},{17,9},{25,1},{2,26},{10... | collective-permute-start | bytes 405512 | tf_op jit(solution)/shard_map/ppermute | solution.py:16
  28.3 1.1 %shard_map.39 = (bf16[1024,768]{1,0:T(8,128)(2,1)S(1)}, f32[1024,128]{1,0:T(8,128)S(1)}) custom-call(s32[1,1024]{1,0:T(1,128)S(1)} %get-tuple-element.24.piv_row), custom_call_target="tpu_custom_call" | custom-call | tf_op jit(solution)/shard_map/pallas_call | solution.py:20
  29.3 0.0 copy-start
  29.3 0.9 %copy-done = f32[64,1024]{1,0:T(8,128)S(1)} copy-done((f32[64,1024]{1,0:T(8,128)S(1)}, f32[64,1024]{1,0:T(8,128)}, u32[]{:S(2)}) %copy-start) | copy-done | bytes 262168
  30.3 0.1 shard_map.42
  30.4 0.2 shard_map.40.old_ref
  30.6 3.8 %collective-permute-done.refs_0_ = f32[264,128]{1,0:T(8,128)S(1)} collective-permute-done((f32[264,128]{1,0:T(8,128)S(1)}, f32[264,128]{1,0:T(8,128)S(1)}, u32[]{:S(2)}, u32[]{:S(2)}) %collective-permute-start) | collective-permute-done | bytes 135200 | tf_op jit(solution)/shard_map/ppermute | solution.py:16
  34.4 0.0 collective-permute-done.1.refs_1_
  34.4 0.6 %shard_map.41.top_ref = bf16[1024,256]{1,0:T(8,128)(2,1)S(1)} custom-call(bf16[1024,768]{1,0:T(8,128)(2,1)S(1)} %get-tuple-element.25.chosen_ref, bf16[1024,256]{1,0:T(8,128)(2,1)S(1)} %shard_map.40.old_ref, f32[264,128]{1,0:T(8,128)S(1)} %collective-permute-done.refs_0_, f32[264,128]{1,0:T(8,128)S(1)} %collective-permute-done.1.refs_1_), custom_call_target="tpu_custom_call" | custom-call | tf_op jit(solution)/shard_map/pallas_call | solution.py:20
  35.0 0.3 shard_map.43.refs_0_
  35.3 0.8 %collective-permute-start.10 = (f32[128,128]{1,0:T(8,128)S(1)}, f32[128,128]{1,0:T(8,128)S(1)}, u32[]{:S(2)}, u32[]{:S(2)}) collective-permute-start(f32[128,128]{1,0:T(8,128)S(1)} %shard_map.43.refs_0_), channel_id=1, source_target_pairs={{0,16},{8,24},{16,0},{24,8},{1,17},{9,25},{17,1},{25,9},{2,18},{10... | collective-permute-start | bytes 196616 | tf_op jit(solution)/shard_map/ppermute | solution.py:16
  36.1 0.0 collective-permute-done.5.refs_1_
  36.1 0.0 collective-permute-done.7.refs_3_
  36.1 0.6 %shard_map.44 = (f32[256,128]{1,0:T(8,128)S(1)}, bf16[256,1024]{1,0:T(8,128)(2,1)S(1)}, bf16[256,1024]{1,0:T(8,128)(2,1)S(1)}) custom-call(bf16[1024,256]{1,0:T(8,128)(2,1)S(1)} %shard_map.41.top_ref, f32[64,1024]{1,0:T(8,128)S(1)} %collective-permute-done.4.refs_0_, f32[64,1024]{1,0:T(8,128)S(1)} %collective-permute-done.5.refs_1_, ...), custom_call_target="tpu_custom_call" | custom-call | tf_op jit(solution)/shard_map/pallas_call | solution.py:20
  36.7 1.0 %collective-permute-start.12 = (f32[256,128]{1,0:T(8,128)S(1)}, f32[256,128]{1,0:T(8,128)S(1)}, u32[]{:S(2)}, u32[]{:S(2)}) collective-permute-start(f32[256,128]{1,0:T(8,128)S(1)} %get-tuple-element.29.refs_1_), channel_id=1, source_target_pairs={{0,16},{8,24},{16,0},{24,8},{1,17},{9,25},{17,1},{25,9},{2,18},{10... | collective-permute-start | bytes 393224 | tf_op jit(solution)/shard_map/ppermute | solution.py:16
  37.7 2.0 %collective-permute-start.13 = (f32[256,128]{1,0:T(8,128)S(1)}, f32[256,128]{1,0:T(8,128)S(1)}, u32[]{:S(2)}, u32[]{:S(2)}) collective-permute-start(f32[256,128]{1,0:T(8,128)S(1)} %get-tuple-element.29.refs_1_), channel_id=1, source_target_pairs={{0,24},{8,16},{16,8},{24,0},{1,25},{9,17},{17,9},{25,1},{2,26},{10... | collective-permute-start | bytes 393224 | tf_op jit(solution)/shard_map/ppermute | solution.py:16
  39.7 2.1 %collective-permute-done.10.refs_8_ = f32[128,128]{1,0:T(8,128)S(1)} collective-permute-done((f32[128,128]{1,0:T(8,128)S(1)}, f32[128,128]{1,0:T(8,128)S(1)}, u32[]{:S(2)}, u32[]{:S(2)}) %collective-permute-start.10) | collective-permute-done | bytes 65568 | tf_op jit(solution)/shard_map/ppermute | solution.py:16
  41.8 0.0 collective-permute-start.11
  41.8 0.0 collective-permute-done.9.refs_1_
  41.8 0.4 shard_map.45
  42.2 0.5 collective-permute-start.14
  42.6 3.1 %collective-permute-start.15 = (f32[128,128]{1,0:T(8,128)S(1)}, f32[128,128]{1,0:T(8,128)S(1)}, u32[]{:S(2)}, u32[]{:S(2)}) collective-permute-start(f32[128,128]{1,0:T(8,128)S(1)} %get-tuple-element.34.solved_ref), channel_id=1, source_target_pairs={{0,24},{8,16},{16,8},{24,0},{1,25},{9,17},{17,9},{25,1},{2,26},{10... | collective-permute-start | bytes 196616 | tf_op jit(solution)/shard_map/ppermute | solution.py:16
  45.7 0.3 collective-permute-done.11.refs_9_
  46.0 0.4 collective-permute-done.12.refs_10_
  46.4 0.0 collective-permute-done.13.refs_11_
  46.5 0.7 %collective-permute-done.14.refs_6_ = f32[128,128]{1,0:T(8,128)S(1)} collective-permute-done((f32[128,128]{1,0:T(8,128)S(1)}, f32[128,128]{1,0:T(8,128)S(1)}, u32[]{:S(2)}, u32[]{:S(2)}) %collective-permute-start.14) | collective-permute-done | bytes 65568 | tf_op jit(solution)/shard_map/ppermute | solution.py:16
  47.1 0.8 %collective-permute-done.15.refs_7_ = f32[128,128]{1,0:T(8,128)S(1)} collective-permute-done((f32[128,128]{1,0:T(8,128)S(1)}, f32[128,128]{1,0:T(8,128)S(1)}, u32[]{:S(2)}, u32[]{:S(2)}) %collective-permute-start.15) | collective-permute-done | bytes 65568 | tf_op jit(solution)/shard_map/ppermute | solution.py:16
  47.9 0.7 %shard_map.47 = f32[512,128]{1,0:T(8,128)} custom-call(f32[512,128]{1,0:T(8,128)S(1)} %shard_map.46.so_far_ref, f32[128,128]{1,0:T(8,128)S(1)} %get-tuple-element.34.solved_ref, bf16[128,1024]{1,0:T(8,128)(2,1)S(1)} %get-tuple-element.27.refs_0_.refs_2_, bf16[128,1024]{1,0:T(8,128)(2,1)S(1)} %get-tuple-element.28.refs_1_.refs_3_, ...), custom_call_target="tpu_custom_call" | custom-call | tf_op jit(solution)/shard_map/pallas_call | solution.py:20
  (2 shorter events, 0.0 us)
Async XLA Ops:
  0.0 16.3 %collective-permute-start.6 = (f32[64,1024]{1,0:T(8,128)}, f32[64,1024]{1,0:T(8,128)S(1)}, u32[]{:S(2)}, u32[]{:S(2)}) collective-permute-start(f32[64,1024]{1,0:T(8,128)} %refs_0_.1), channel_id=1, source_target_pairs={{0,4},{1,5},{2,6},{3,7},{4,0},{5,1},{6,2},{7,3},{8,12},{9,13},{10,... | collective-permute-start | bytes 786440 | tf_op jit(solution)/shard_map/ppermute | solution.py:16
  4.1 14.5 %collective-permute-start.4 = (f32[64,1024]{1,0:T(8,128)}, f32[64,1024]{1,0:T(8,128)S(1)}, u32[]{:S(2)}, u32[]{:S(2)}) collective-permute-start(f32[64,1024]{1,0:T(8,128)} %refs_0_.1), channel_id=1, source_target_pairs={{0,2},{1,3},{2,0},{3,1},{4,6},{5,7},{6,4},{7,5},{8,10},{9,11},{10,... | collective-permute-start | bytes 786440 | tf_op jit(solution)/shard_map/ppermute | solution.py:16
  16.3 7.4 %collective-permute-start.8 = (f32[64,1024]{1,0:T(8,128)S(1)}, f32[64,1024]{1,0:T(8,128)S(1)}, u32[]{:S(2)}, u32[]{:S(2)}) collective-permute-start(f32[64,1024]{1,0:T(8,128)S(1)} %collective-permute-done.6.refs_2_), channel_id=1, source_target_pairs={{0,2},{1,3},{2,0},{3,1},{4,6},{5,7},{6,4},{7,5},{8,10},{9,11},{10,... | collective-permute-start | bytes 786440 | tf_op jit(solution)/shard_map/ppermute | solution.py:16
  17.0 8.4 %collective-permute-start.2 = (f32[512,128]{1,0:T(8,128)}, f32[512,128]{1,0:T(8,128)S(1)}, u32[]{:S(2)}, u32[]{:S(2)}) collective-permute-start(f32[512,128]{1,0:T(8,128)} %matrix_hbm.1), channel_id=1, source_target_pairs={{0,8},{8,0},{16,24},{24,16},{1,9},{9,1},{17,25},{25,17},{2,10},{10... | collective-permute-start | bytes 786440 | tf_op jit(solution)/shard_map/ppermute | solution.py:16
  18.5 8.7 %collective-permute-start.3 = (f32[64,1024]{1,0:T(8,128)}, f32[64,1024]{1,0:T(8,128)S(1)}, u32[]{:S(2)}, u32[]{:S(2)}) collective-permute-start(f32[64,1024]{1,0:T(8,128)} %refs_0_.1), channel_id=1, source_target_pairs={{0,1},{1,0},{2,3},{3,2},{4,5},{5,4},{6,7},{7,6},{8,9},{9,8},{10,11... | collective-permute-start | bytes 786440 | tf_op jit(solution)/shard_map/ppermute | solution.py:16
  18.5 17.6 %collective-permute-start.5 = (f32[64,1024]{1,0:T(8,128)S(1)}, f32[64,1024]{1,0:T(8,128)S(1)}, u32[]{:S(2)}, u32[]{:S(2)}) collective-permute-start(f32[64,1024]{1,0:T(8,128)S(1)} %collective-permute-done.4.refs_0_), channel_id=1, source_target_pairs={{0,1},{1,0},{2,3},{3,2},{4,5},{5,4},{6,7},{7,6},{8,9},{9,8},{10,11... | collective-permute-start | bytes 786440 | tf_op jit(solution)/shard_map/ppermute | solution.py:16
  19.0 17.0 %collective-permute-start.7 = (f32[64,1024]{1,0:T(8,128)S(1)}, f32[64,1024]{1,0:T(8,128)S(1)}, u32[]{:S(2)}, u32[]{:S(2)}) collective-permute-start(f32[64,1024]{1,0:T(8,128)S(1)} %collective-permute-done.6.refs_2_), channel_id=1, source_target_pairs={{0,1},{1,0},{2,3},{3,2},{4,5},{5,4},{6,7},{7,6},{8,9},{9,8},{10,11... | collective-permute-start | bytes 786440 | tf_op jit(solution)/shard_map/ppermute | solution.py:16
  23.7 18.1 %collective-permute-start.9 = (f32[64,1024]{1,0:T(8,128)S(1)}, f32[64,1024]{1,0:T(8,128)S(1)}, u32[]{:S(2)}, u32[]{:S(2)}) collective-permute-start(f32[64,1024]{1,0:T(8,128)S(1)} %collective-permute-done.8.refs_0_), channel_id=1, source_target_pairs={{0,1},{1,0},{2,3},{3,2},{4,5},{5,4},{6,7},{7,6},{8,9},{9,8},{10,11... | collective-permute-start | bytes 786440 | tf_op jit(solution)/shard_map/ppermute | solution.py:16
  25.4 9.0 %collective-permute-start = (f32[264,128]{1,0:T(8,128)S(1)}, f32[264,128]{1,0:T(8,128)S(1)}, u32[]{:S(2)}, u32[]{:S(2)}) collective-permute-start(f32[264,128]{1,0:T(8,128)S(1)} %get-tuple-element.22), channel_id=1, source_target_pairs={{0,16},{8,24},{16,0},{24,8},{1,17},{9,25},{17,1},{25,9},{2,18},{10... | collective-permute-start | bytes 405512 | tf_op jit(solution)/shard_map/ppermute | solution.py:16
  27.2 7.2 %collective-permute-start.1 = (f32[264,128]{1,0:T(8,128)S(1)}, f32[264,128]{1,0:T(8,128)S(1)}, u32[]{:S(2)}, u32[]{:S(2)}) collective-permute-start(f32[264,128]{1,0:T(8,128)S(1)} %get-tuple-element.23), channel_id=1, source_target_pairs={{0,24},{8,16},{16,8},{24,0},{1,25},{9,17},{17,9},{25,1},{2,26},{10... | collective-permute-start | bytes 405512 | tf_op jit(solution)/shard_map/ppermute | solution.py:16
  29.3 1.0 %copy-start = (f32[64,1024]{1,0:T(8,128)S(1)}, f32[64,1024]{1,0:T(8,128)}, u32[]{:S(2)}) copy-start(f32[64,1024]{1,0:T(8,128)} %refs_0_.1) | copy-start | bytes 786436
  35.3 6.4 %collective-permute-start.10 = (f32[128,128]{1,0:T(8,128)S(1)}, f32[128,128]{1,0:T(8,128)S(1)}, u32[]{:S(2)}, u32[]{:S(2)}) collective-permute-start(f32[128,128]{1,0:T(8,128)S(1)} %shard_map.43.refs_0_), channel_id=1, source_target_pairs={{0,16},{8,24},{16,0},{24,8},{1,17},{9,25},{17,1},{25,9},{2,18},{10... | collective-permute-start | bytes 196616 | tf_op jit(solution)/shard_map/ppermute | solution.py:16
  36.7 9.8 %collective-permute-start.12 = (f32[256,128]{1,0:T(8,128)S(1)}, f32[256,128]{1,0:T(8,128)S(1)}, u32[]{:S(2)}, u32[]{:S(2)}) collective-permute-start(f32[256,128]{1,0:T(8,128)S(1)} %get-tuple-element.29.refs_1_), channel_id=1, source_target_pairs={{0,16},{8,24},{16,0},{24,8},{1,17},{9,25},{17,1},{25,9},{2,18},{10... | collective-permute-start | bytes 393224 | tf_op jit(solution)/shard_map/ppermute | solution.py:16
  37.7 8.8 %collective-permute-start.13 = (f32[256,128]{1,0:T(8,128)S(1)}, f32[256,128]{1,0:T(8,128)S(1)}, u32[]{:S(2)}, u32[]{:S(2)}) collective-permute-start(f32[256,128]{1,0:T(8,128)S(1)} %get-tuple-element.29.refs_1_), channel_id=1, source_target_pairs={{0,24},{8,16},{16,8},{24,0},{1,25},{9,17},{17,9},{25,1},{2,26},{10... | collective-permute-start | bytes 393224 | tf_op jit(solution)/shard_map/ppermute | solution.py:16
  41.8 4.3 %collective-permute-start.11 = (f32[128,128]{1,0:T(8,128)S(1)}, f32[128,128]{1,0:T(8,128)S(1)}, u32[]{:S(2)}, u32[]{:S(2)}) collective-permute-start(f32[128,128]{1,0:T(8,128)S(1)} %collective-permute-done.10.refs_8_), channel_id=1, source_target_pairs={{0,8},{8,0},{16,24},{24,16},{1,9},{9,1},{17,25},{25,17},{2,10},{10... | collective-permute-start | bytes 196616 | tf_op jit(solution)/shard_map/ppermute | solution.py:16
  42.2 5.0 %collective-permute-start.14 = (f32[128,128]{1,0:T(8,128)S(1)}, f32[128,128]{1,0:T(8,128)S(1)}, u32[]{:S(2)}, u32[]{:S(2)}) collective-permute-start(f32[128,128]{1,0:T(8,128)S(1)} %get-tuple-element.34.solved_ref), channel_id=1, source_target_pairs={{0,16},{8,24},{16,0},{24,8},{1,17},{9,25},{17,1},{25,9},{2,18},{10... | collective-permute-start | bytes 196616 | tf_op jit(solution)/shard_map/ppermute | solution.py:16
  42.6 5.3 %collective-permute-start.15 = (f32[128,128]{1,0:T(8,128)S(1)}, f32[128,128]{1,0:T(8,128)S(1)}, u32[]{:S(2)}, u32[]{:S(2)}) collective-permute-start(f32[128,128]{1,0:T(8,128)S(1)} %get-tuple-element.34.solved_ref), channel_id=1, source_target_pairs={{0,24},{8,16},{16,8},{24,0},{1,25},{9,17},{17,9},{25,1},{2,26},{10... | collective-permute-start | bytes 196616 | tf_op jit(solution)/shard_map/ppermute | solution.py:16
